TPU v7x, 32 devices: a whole 2x2x4 slice. The times are simulated.
32 devices in a mesh: tile: 16 (over z, y, x), mode: 2 (over core).
Axes of the slice: x: 2, y: 2, z: 4, core: 2. Of those that a mesh axis runs over, the one named last changes fastest.
Arguments:
- object_tiles: float32 [2, 2048, 2048], P(None, 'tile'), may hold values from -6 to 6
- probe_modes: float32 [4, 2, 256, 256], P('mode'), may hold values from -5 to 5
- amplitudes: float32 [16, 256, 256], P('tile'), may hold values from 0.25 to 4
- scan_offsets: int32 [8192, 2], replicated, may hold values from 0 to 1792, as said below
- slot_scan: int32 [16], P('tile'), may hold values from 0 to 8191, as said below
- slot_count: int32 [16], P('tile'), may hold values from 0 to 1, as said below
Outputs:
- updated_object: float32 [2, 2048, 2048], P(None, 'tile')
- object_gradient: float32 [2, 2048, 2048], P(None, 'tile')
Inputs may be any that keep to these rules, and one draw needn't show every extreme that they name: `scan_offsets`: every patch of 256 x 256 pixels at an offset lies inside the object. `slot_scan`: on every index d of tile but the last, the row offset of each slot's scan position lies in [d * 128, (d + 1) * 128). The positions of one device's slots are distinct. `slot_count`: the live slots of a device are its first ones. The last index of tile holds none, every other holds at least one; some index holds 1.
All inputs are finite; a program needn't handle non-finite values.
Results may differ from a plain program's by a relative error of at most 0.0001.
Values sent between devices are 32-bit elements; how exact they have to be, the bound alone decides.
No kernel may reach another device: no remote copies, remote signals or barrier semaphores. Data moves between devices by JAX's collectives and lax.ppermute only.
A program may use at most 64 MiB of HBM per device.

v0:
```python
import math

import jax
import jax.numpy as jnp
from jax import lax
from jax.sharding import PartitionSpec as P

FLOOR = 0.25
ALPHA = 0.5


def from_behind(value, axis, steps):
    count = lax.axis_size(axis)
    initial, last = (max(0, -steps), min(count, count - steps))
    return lax.ppermute(value, axis, [(source, source + steps) for source in range(initial, last)])


def tables(frame):
    index = jnp.arange(frame, dtype=jnp.int32)
    phase = (index[:, None] * index[None, :] % frame).astype(jnp.float32) * (2.0 * math.pi / frame)
    scale = 1.0 / math.sqrt(frame)
    return (jnp.cos(phase) * scale, -jnp.sin(phase) * scale)


def product(first, second):
    return jnp.matmul(first, second, precision=lax.Precision.HIGHEST)


def transform(real_part, imag_part, cos_table, sin_table):
    inner_re = product(cos_table, real_part) - product(sin_table, imag_part)
    inner_im = product(cos_table, imag_part) + product(sin_table, real_part)
    outer_re = product(inner_re, cos_table) - product(inner_im, sin_table)
    outer_im = product(inner_im, cos_table) + product(inner_re, sin_table)
    return (outer_re, outer_im)


def shards(object_tiles, probe_modes, amplitudes, scan_offsets, slot_scan, slot_count):
    height = object_tiles.shape[1]
    breadth = object_tiles.shape[2]
    frame = probe_modes.shape[2]
    slot_total = slot_scan.shape[0]
    device = lax.axis_index("tile")
    anchor = jnp.zeros((), jnp.int32)
    cos_table, sin_table = tables(frame)
    probe_re = probe_modes[:, 0]
    probe_im = probe_modes[:, 1]
    illumination = lax.psum(jnp.sum(probe_re * probe_re + probe_im * probe_im, axis=0), "mode")
    offsets = jnp.take(scan_offsets, slot_scan, axis=0)
    row_start = offsets[:, 0] - device * height
    col_start = offsets[:, 1]
    active = (jnp.arange(slot_total, dtype=jnp.int32) < slot_count[0]).astype(jnp.float32)

    def cut_columns(col_at):
        return lax.dynamic_slice(object_tiles, (anchor, anchor, col_at), (2, height, frame))

    their_starts = []
    pieces = [jax.vmap(cut_columns)(col_start)]
    for distance in (1, 2):
        remote = from_behind(col_start, "tile", distance)
        their_starts.append(remote)
        windows = jax.vmap(cut_columns)(remote)
        pieces.append(from_behind(windows, "tile", -distance))
    canvas = jnp.concatenate(pieces, axis=2)

    def cut_rows(column_block, row_at):
        return lax.dynamic_slice(column_block, (anchor, row_at, anchor), (2, frame, frame))

    patches = jax.vmap(cut_rows)(canvas, row_start)
    patch_re = patches[:, 0][:, None]
    patch_im = patches[:, 1][:, None]
    wave_re = probe_re[None] * patch_re - probe_im[None] * patch_im
    wave_im = probe_re[None] * patch_im + probe_im[None] * patch_re
    far_re, far_im = transform(wave_re, wave_im, cos_table, sin_table)
    intensity = lax.psum(jnp.sum(far_re * far_re + far_im * far_im, axis=1), "mode")
    factor = (amplitudes / jnp.sqrt(jnp.maximum(intensity, FLOOR)))[:, None]
    back_re, back_im = transform(far_re * factor, far_im * factor, cos_table, -sin_table)
    delta_re = back_re - wave_re
    delta_im = back_im - wave_im
    weights = active[:, None, None]
    grad_re = jnp.sum(probe_re[None] * delta_re + probe_im[None] * delta_im, axis=1) * weights
    grad_im = jnp.sum(probe_re[None] * delta_im - probe_im[None] * delta_re, axis=1) * weights
    coverage = illumination[None] * weights
    contribution = jnp.stack([grad_re, grad_im, coverage], axis=1)
    channels = contribution.shape[1]

    def place(piece, row_at):
        empty = jnp.zeros((channels, 3 * height, frame), jnp.float32)
        return lax.dynamic_update_slice(empty, piece, (anchor, row_at, anchor))

    padded = jax.vmap(place)(contribution, row_start)
    blocks = [(padded[:, :, :height], col_start)]
    for distance in (1, 2):
        arrived = from_behind(
            padded[:, :, distance * height : (distance + 1) * height], "tile", distance
        )
        blocks.append((arrived, their_starts[distance - 1]))
    totals = jnp.zeros((channels, height, breadth), jnp.float32)
    for block, starts in blocks:

        def add_block(index, accum, block=block, starts=starts):
            current = lax.dynamic_slice(
                accum, (anchor, anchor, starts[index]), (channels, height, frame)
            )
            return lax.dynamic_update_slice(
                accum, current + block[index], (anchor, anchor, starts[index])
            )

        totals = lax.fori_loop(0, slot_total, add_block, totals)
    cover = totals[2]
    gradient = totals[:2]
    gradient = lax.psum(gradient, "mode")
    updated = object_tiles + gradient / (cover + ALPHA)
    return (updated, gradient)


def solution(mesh):
    return jax.shard_map(
        shards,
        mesh=mesh,
        in_specs=(
            P(None, "tile", None),
            P("mode", None, None, None),
            P("tile", None, None),
            P(),
            P("tile"),
            P("tile"),
        ),
        out_specs=(P(None, "tile", None), P(None, "tile", None)),
        check_vma=False,
    )
```

profile of v0, /device:TPU:9, one launch (start us, length us, event | category | flops | bytes accessed | tf_op | source)
XLA Modules:
  0.0 182.8 jit_solution(3276640202237334104)
XLA Ops:
  9.2 3.1 %collective-permute-start.2 = (s32[1]{0:T(128)}, s32[1]{0:T(128)}, u32[]{:S(2)}, u32[]{:S(2)}) collective-permute-start(s32[1]{0:T(128)} %bitcast.10), channel_id=1, source_target_pairs={{0,4},{2,6},{4,8},{6,10},{8,12},{10,14},{12,16},{14,18},{16,20},{1... | collective-permute-start | bytes 20 | tf_op jit(solution)/shard_map/ppermute | solution.py:15
  12.4 3.1 %collective-permute-start = (s32[1]{0:T(128)}, s32[1]{0:T(128)}, u32[]{:S(2)}, u32[]{:S(2)}) collective-permute-start(s32[1]{0:T(128)} %bitcast.10), channel_id=1, source_target_pairs={{0,2},{2,4},{4,6},{6,8},{8,10},{10,12},{12,14},{14,16},{16,18},{18... | collective-permute-start | bytes 20 | tf_op jit(solution)/shard_map/ppermute | solution.py:15
  22.7 2.9 %collective-permute-start.3 = (f32[1,2,128,256]{3,2,1,0:T(8,128)S(1)}, f32[1,2,128,256]{3,2,1,0:T(8,128)S(1)}, u32[]{:S(2)}, u32[]{:S(2)}) collective-permute-start(f32[1,2,128,256]{3,2,1,0:T(8,128)S(1)} %get-tuple-element.117), channel_id=1, source_target_pairs={{4,0},{6,2},{8,4},{10,6},{12,8},{14,10},{16,12},{18,14},{20,16},{2... | collective-permute-start | bytes 786440 | tf_op jit(solution)/shard_map/ppermute | solution.py:15
  25.6 3.1 %collective-permute-start.1 = (f32[1,2,128,256]{3,2,1,0:T(8,128)S(1)}, f32[1,2,128,256]{3,2,1,0:T(8,128)S(1)}, u32[]{:S(2)}, u32[]{:S(2)}) collective-permute-start(f32[1,2,128,256]{3,2,1,0:T(8,128)S(1)} %get-tuple-element.118), channel_id=1, source_target_pairs={{2,0},{4,2},{6,4},{8,6},{10,8},{12,10},{14,12},{16,14},{18,16},{20... | collective-permute-start | bytes 786440 | tf_op jit(solution)/shard_map/ppermute | solution.py:15
  30.3 5.2 %collective-permute-done.1 = f32[1,2,128,256]{3,2,1,0:T(8,128)S(1)} collective-permute-done((f32[1,2,128,256]{3,2,1,0:T(8,128)S(1)}, f32[1,2,128,256]{3,2,1,0:T(8,128)S(1)}, u32[]{:S(2)}, u32[]{:S(2)}) %collective-permute-start.1) | collective-permute-done | bytes 262176 | tf_op jit(solution)/shard_map/ppermute | solution.py:15
  36.0 1.6 fusion.46
  37.6 1.6 fusion.42
  39.2 1.6 fusion.5
  42.5 1.6 fusion.4
  44.1 1.6 fusion.40
  45.7 1.6 convolution_subtract_fusion.2
  47.3 2.5 %add_reduce_fusion = (f32[256,256]{1,0:T(8,128)}, f32[2,256,256]{2,1,0:T(8,128)S(1)}) fusion(f32[2,256,256]{2,1,0:T(8,128)S(1)} %convolution_subtract_fusion.2, f32[2,256,256]{2,1,0:T(8,128)S(1)} %fusion.40, f32[2,256,256]{2,1,0:T(8,128)S(1)} %fusion.5), kind=kOutput, calls=%fused_computation.41 | convolution fusion | flops 404291584 | bytes 2359296 | tf_op jit(solution)/shard_map/dot_general | solution.py:26
  50.5 21.9 %all-reduce.7.cloned.1.call-done = f32[1,256,256]{2,1,0:T(8,128)} async-done(((f32[1,256,256]{2,1,0:T(8,128)}), f32[1,256,256]{2,1,0:T(8,128)}) %all-reduce.7.cloned.1.call-update) | async-done | bytes 262160 | tf_op jit(solution)/shard_map/psum | solution.py:74
  73.5 1.6 fusion.21
  75.1 1.6 fusion.17
  76.8 1.7 fusion.2
  78.4 1.7 fusion.3
  80.1 1.6 fusion.37
  81.7 1.6 fusion.34
  83.2 1.6 fusion.1
  84.8 2.6 %fusion.12 = (f32[256,256]{1,0:T(8,128)S(1)}, f32[256,256]{1,0:T(8,128)S(1)}, f32[256,256]{1,0:T(8,128)}) fusion(f32[2,256,256]{2,1,0:T(8,128)S(1)} %fusion.1, f32[2,2,256,256]{3,2,1,0:T(8,128)S(1)} %copy-done.1, f32[2,256,256]{2,1,0:T(8,128)S(1)} %get-tuple-element.121, f32[2,256,256]{2,1,0:T(8,128)S(1)} %fusion.34, f32[2,256,256]{2,1,0:T(8,128)S(1)} %fusion.3), kind=kOutput, calls=%fused_computation.31 | convolution fusion | flops 405405696 | bytes 3932160 | tf_op jit(solution)/shard_map/dot_general | solution.py:26
  87.5 2.7 %and_reduce_fusion = pred[]{:T(512)} fusion(s32[4]{0:T(128)S(1)} %copy-done.3, s32[1]{0:T(128)} %bitcast.7, s32[1]{0:T(128)} %bitcast.6, s32[1]{0:T(128)} %bitcast.5, s32[1]{0:T(128)} %constant.96.clone.1), kind=kLoop, calls=%fused_computation.118 | loop fusion | flops 27 | bytes 33 | tf_op jit(solution)/shard_map/reduce.1
  90.9 16.2 %all-reduce.9.cloned.1.call-done = f32[256,256]{1,0:T(8,128)} async-done(((f32[256,256]{1,0:T(8,128)}), f32[256,256]{1,0:T(8,128)}) %all-reduce.9.cloned.1.call-update) | async-done | bytes 262160 | tf_op jit(solution)/shard_map/psum | solution.py:47
  108.9 5.1 %scatter.4 = f32[1,3,384,256]{3,2,1,0:T(8,128)S(1)} dynamic-update-slice(f32[1,3,384,256]{3,2,1,0:T(8,128)S(1)} %broadcast_in_dim.32, f32[1,3,256,256]{3,2,1,0:T(8,128)S(1)} %maximum_select_fusion, s32[]{:T(128)} %constant.95.clone.1, s32[]{:T(128)} %constant.95.clone.1, s32[]{:T(128)} %bitcast.49, s32[]{:T(128)} %constant.95.clone.1) | dynamic-update-slice | bytes 1572868 | tf_op jit(solution)/shard_map/vmap(vmap())/scatter | solution.py:88
  114.9 2.4 %collective-permute-start.4 = (f32[1,3,128,256]{3,2,1,0:T(8,128)}, f32[1,3,128,256]{3,2,1,0:T(8,128)}, u32[]{:S(2)}, u32[]{:S(2)}) collective-permute-start(f32[1,3,128,256]{3,2,1,0:T(8,128)} %get-tuple-element.123), channel_id=1, source_target_pairs={{0,2},{2,4},{4,6},{6,8},{8,10},{10,12},{12,14},{14,16},{16,18},{18... | collective-permute-start | bytes 1179656 | tf_op jit(solution)/shard_map/ppermute | solution.py:15
  117.3 2.7 %collective-permute-start.5 = (f32[1,3,128,256]{3,2,1,0:T(8,128)}, f32[1,3,128,256]{3,2,1,0:T(8,128)}, u32[]{:S(2)}, u32[]{:S(2)}) collective-permute-start(f32[1,3,128,256]{3,2,1,0:T(8,128)} %get-tuple-element.122), channel_id=1, source_target_pairs={{0,4},{2,6},{4,8},{6,10},{8,12},{10,14},{12,16},{14,18},{16,20},{1... | collective-permute-start | bytes 1179656 | tf_op jit(solution)/shard_map/ppermute | solution.py:15
  125.9 5.5 %dynamic_update_slice.12 = f32[3,128,2048]{2,1,0:T(8,128)S(1)} dynamic-update-slice(f32[3,128,2048]{2,1,0:T(8,128)S(1)} %broadcast_in_dim.31, f32[3,128,256]{2,1,0:T(8,128)S(1)} %get-tuple-element.124, s32[]{:T(128)} %constant.95.clone.1, s32[]{:T(128)} %constant.95.clone.1, s32[]{:T(128)S(6)} %select_n.101) | dynamic-update-slice | bytes 786436 | tf_op jit(solution)/shard_map/while/body/eval_jaxpr/dynamic_update_slice | solution.py:104
  131.4 2.8 %collective-permute-done.4 = f32[1,3,128,256]{3,2,1,0:T(8,128)} collective-permute-done((f32[1,3,128,256]{3,2,1,0:T(8,128)}, f32[1,3,128,256]{3,2,1,0:T(8,128)}, u32[]{:S(2)}, u32[]{:S(2)}) %collective-permute-start.4) | collective-permute-done | bytes 393248 | tf_op jit(solution)/shard_map/ppermute | solution.py:15
  135.4 5.5 %dynamic_update_slice.13 = f32[3,128,2048]{2,1,0:T(8,128)S(1)} dynamic-update-slice(f32[3,128,2048]{2,1,0:T(8,128)S(1)} %dynamic_update_slice.12, f32[3,128,256]{2,1,0:T(8,128)S(1)} %bitcast_add_fusion.1, s32[]{:T(128)} %constant.95.clone.1, s32[]{:T(128)} %constant.95.clone.1, s32[]{:T(128)S(6)} %select_n.102) | dynamic-update-slice | bytes 786436 | tf_op jit(solution)/shard_map/while/body/eval_jaxpr/dynamic_update_slice | solution.py:104
  142.0 5.5 %dynamic_update_slice.14 = f32[3,128,2048]{2,1,0:T(8,128)S(1)} dynamic-update-slice(f32[3,128,2048]{2,1,0:T(8,128)S(1)} %dynamic_update_slice.13, f32[3,128,256]{2,1,0:T(8,128)S(1)} %bitcast_add_fusion, s32[]{:T(128)} %constant.95.clone.1, s32[]{:T(128)} %constant.95.clone.1, s32[]{:T(128)S(6)} %select_n.103) | dynamic-update-slice | bytes 786436 | tf_op jit(solution)/shard_map/while/body/eval_jaxpr/dynamic_update_slice | solution.py:104
  150.1 20.3 %all-reduce.11.cloned.1.call-done = f32[2,128,2048]{2,1,0:T(8,128)} async-done(((f32[2,128,2048]{2,1,0:T(8,128)}), f32[2,128,2048]{2,1,0:T(8,128)}) %all-reduce.11.cloned.1.call-update) | async-done | bytes 2097168 | tf_op jit(solution)/shard_map/psum | solution.py:111
  170.4 4.5 %divide_add_fusion = f32[2,128,2048]{2,1,0:T(8,128)} fusion(f32[2,128,2048]{2,1,0:T(8,128)} %param.8, f32[2,128,2048]{2,1,0:T(8,128)} %all-reduce.11.cloned.1.call-done, f32[128,2048]{1,0:T(8,128)} %fusion.6), kind=kLoop, calls=%fused_computation | loop fusion | flops 1048576 | bytes 7340032 | tf_op jit(solution)/shard_map/add | solution.py:112
  (41 shorter events, 17.0 us)
Async XLA Ops:
  7.2 28.7 %copy-start.1 = (f32[2,2,256,256]{3,2,1,0:T(8,128)S(1)}, f32[2,2,256,256]{3,2,1,0:T(8,128)}, u32[]{:S(2)}) copy-start(f32[2,2,256,256]{3,2,1,0:T(8,128)} %param.9) | copy-start | bytes 3145732
  7.2 65.3 %all-reduce.7.cloned.1.call-start = ((), (), s32[]{:S(2)}) async-start(), calls=%async_computation | async-start | bytes 524288 | tf_op jit(solution)/shard_map/psum | solution.py:74
  9.2 8.0 %collective-permute-start.2 = (s32[1]{0:T(128)}, s32[1]{0:T(128)}, u32[]{:S(2)}, u32[]{:S(2)}) collective-permute-start(s32[1]{0:T(128)} %bitcast.10), channel_id=1, source_target_pairs={{0,4},{2,6},{4,8},{6,10},{8,12},{10,14},{12,16},{14,18},{16,20},{1... | collective-permute-start | bytes 20 | tf_op jit(solution)/shard_map/ppermute | solution.py:15
  12.4 6.3 %collective-permute-start = (s32[1]{0:T(128)}, s32[1]{0:T(128)}, u32[]{:S(2)}, u32[]{:S(2)}) collective-permute-start(s32[1]{0:T(128)} %bitcast.10), channel_id=1, source_target_pairs={{0,2},{2,4},{4,6},{6,8},{8,10},{10,12},{12,14},{14,16},{16,18},{18... | collective-permute-start | bytes 20 | tf_op jit(solution)/shard_map/ppermute | solution.py:15
  22.7 7.7 %collective-permute-start.3 = (f32[1,2,128,256]{3,2,1,0:T(8,128)S(1)}, f32[1,2,128,256]{3,2,1,0:T(8,128)S(1)}, u32[]{:S(2)}, u32[]{:S(2)}) collective-permute-start(f32[1,2,128,256]{3,2,1,0:T(8,128)S(1)} %get-tuple-element.117), channel_id=1, source_target_pairs={{4,0},{6,2},{8,4},{10,6},{12,8},{14,10},{16,12},{18,14},{20,16},{2... | collective-permute-start | bytes 786440 | tf_op jit(solution)/shard_map/ppermute | solution.py:15
  25.6 10.0 %collective-permute-start.1 = (f32[1,2,128,256]{3,2,1,0:T(8,128)S(1)}, f32[1,2,128,256]{3,2,1,0:T(8,128)S(1)}, u32[]{:S(2)}, u32[]{:S(2)}) collective-permute-start(f32[1,2,128,256]{3,2,1,0:T(8,128)S(1)} %get-tuple-element.118), channel_id=1, source_target_pairs={{2,0},{4,2},{6,4},{8,6},{10,8},{12,10},{14,12},{16,14},{18,16},{20... | collective-permute-start | bytes 786440 | tf_op jit(solution)/shard_map/ppermute | solution.py:15
  45.7 4.1 %copy-start.4 = (s32[1,3]{1,0:T(1,128)S(1)}, s32[1,3]{1,0:T(1,128)}, u32[]{:S(2)}) copy-start(s32[1,3]{1,0:T(1,128)} %constant.105.clone.1) | copy-start | bytes 40
  45.7 26.8 %copy-start.2 = (f32[1,256,256]{2,1,0:T(8,128)S(1)}, f32[1,256,256]{2,1,0:T(8,128)}, u32[]{:S(2)}) copy-start(f32[1,256,256]{2,1,0:T(8,128)} %param.10) | copy-start | bytes 786436
  49.8 57.3 %all-reduce.9.cloned.1.call-start = ((), (), s32[]{:S(2)}) async-start(), calls=%async_computation.1 | async-start | bytes 524288 | tf_op jit(solution)/shard_map/psum | solution.py:47
  84.8 2.7 %copy-start.3 = (s32[4]{0:T(128)S(1)}, s32[4]{0:T(128)}, u32[]{:S(2)}) copy-start(s32[4]{0:T(128)} %constant.106.clone.1) | copy-start | bytes 52
  87.5 82.9 %all-reduce.11.cloned.1.call-start = ((), (), s32[]{:S(2)}) async-start(), calls=%async_computation.2 | async-start | bytes 4194304 | tf_op jit(solution)/shard_map/psum | solution.py:111
  114.9 19.3 %collective-permute-start.4 = (f32[1,3,128,256]{3,2,1,0:T(8,128)}, f32[1,3,128,256]{3,2,1,0:T(8,128)}, u32[]{:S(2)}, u32[]{:S(2)}) collective-permute-start(f32[1,3,128,256]{3,2,1,0:T(8,128)} %get-tuple-element.123), channel_id=1, source_target_pairs={{0,2},{2,4},{4,6},{6,8},{8,10},{10,12},{12,14},{14,16},{16,18},{18... | collective-permute-start | bytes 1179656 | tf_op jit(solution)/shard_map/ppermute | solution.py:15
  117.3 23.5 %collective-permute-start.5 = (f32[1,3,128,256]{3,2,1,0:T(8,128)}, f32[1,3,128,256]{3,2,1,0:T(8,128)}, u32[]{:S(2)}, u32[]{:S(2)}) collective-permute-start(f32[1,3,128,256]{3,2,1,0:T(8,128)} %get-tuple-element.122), channel_id=1, source_target_pairs={{0,4},{2,6},{4,8},{6,10},{8,12},{10,14},{12,16},{14,18},{16,20},{1... | collective-permute-start | bytes 1179656 | tf_op jit(solution)/shard_map/ppermute | solution.py:15
  170.4 4.5 %copy-start = (f32[2,128,2048]{2,1,0:T(8,128)S(1)}, f32[2,128,2048]{2,1,0:T(8,128)}, u32[]{:S(2)}) copy-start(f32[2,128,2048]{2,1,0:T(8,128)} %all-reduce.11.cloned.1.call-done) | copy-start | bytes 6291460
Sparse Core Ops, SparseCore 0:
  49.9 22.5 all-reduce.6
  87.6 19.4 all-reduce.8
  149.1 21.2 all-reduce.10
where the time goes:
time: 184 us; the launch traced here: 183 us
  waiting for transfers between devices  67.6 us (37%)
  local copies, waits for them, and re-layouts  28.4 us (15%)
  matrix products  27.6 us (15%)
  between operations  27.2 us (15%)
  starting transfers between devices  17.5 us (10%)
  other arithmetic  14.4 us (8%)
    dot_general x16, matrix products, product(): return jnp.matmul(first, second, precision=lax.Precision.HIGHEST)  27.6 us
    psum x1, waiting for transfers between devices, shards(): lax.psum(jnp.sum(far_re * far_re + far_im * far_im, axis=1), 'mode')  21.9 us
    psum x1, waiting for transfers between devices, shards(): gradient = lax.psum(gradient, 'mode')  20.3 us
    ppermute x6, starting transfers between devices, from_behind(): lax.ppermute(value, axis, [(source, source + steps) for source in range(i...  17.4 us
    dynamic_update_slice x3, local copies, waits for them, and re-layouts, add_block(): lax.dynamic_update_slice(accum, current + block[index], (anchor, anchor,...  16.4 us
    psum x1, waiting for transfers between devices, shards(): lax.psum(jnp.sum(probe_re * probe_re + probe_im * probe_im, axis=0), 'mode')  16.2 us
    ppermute x6, waiting for transfers between devices, from_behind(): lax.ppermute(value, axis, [(source, source + steps) for source in range(i...  9.1 us
    scatter x1, local copies, waits for them, and re-layouts, place(): return lax.dynamic_update_slice(empty, piece, (anchor, row_at, anchor))  5.08 us
  transfers between devices with their start and end apart: 9, of which 7 were waited for; matrix products, arithmetic and copies ran while one was open for 9% of the time, Pallas kernels for 0%

commit v1 on v0

v1 whole, which is shorter than its diff:
```python
import math

import jax
import jax.numpy as jnp
import numpy as np
from jax import lax
from jax.experimental import pallas as pl
from jax.experimental.pallas import tpu as pltpu
from jax.sharding import PartitionSpec as P

FLOOR = 0.25
ALPHA = 0.5
LANES = 128
AXES = ("tile", "mode")
VMEM = pltpu.VMEM
SMEM = pltpu.SMEM


def split(value):
    high = value.astype(jnp.bfloat16)
    low = (value - high.astype(jnp.float32)).astype(jnp.bfloat16)
    return high, low


def matrices(frame):
    half = frame // 2
    pixel = np.arange(half)[:, None]
    wave = np.arange(half)[None, :]
    blocks = []
    for parity in (0, 1):
        phase = 2.0 * math.pi * (pixel * (2 * wave + parity) % frame) / frame
        cos, sin = np.cos(phase) / math.sqrt(frame), np.sin(phase) / math.sqrt(frame)
        forward = np.block([[cos, -sin], [sin, cos]])
        for table in (forward, forward.T):
            high = table.astype(jnp.bfloat16)
            blocks.append(high)
            blocks.append((table - high.astype(np.float64)).astype(jnp.bfloat16))
    return np.stack(blocks)


def lookup(table_ref, scan):
    base = pl.multiple_of((scan // LANES) * LANES, LANES)
    chunk = table_ref[:, pl.ds(base, LANES)].astype(jnp.float32)
    lane = lax.broadcasted_iota(jnp.int32, chunk.shape, 1)
    picked = jnp.where(lane == scan - base, chunk, 0.0)
    row = jnp.sum(picked[0:1]).astype(jnp.int32)
    col = jnp.sum(picked[1:2]).astype(jnp.int32)
    return row, col


def strip_window(object_ref, col):
    blocks = object_ref.shape[2] // LANES
    block, shift = col // LANES, col % LANES
    first = object_ref[:, :, pl.ds(pl.multiple_of(block * LANES, LANES), LANES)]
    second = object_ref[:, :, pl.ds(pl.multiple_of((block + 1) * LANES, LANES), LANES)]
    last = jnp.minimum(block + 2, blocks - 1)
    third = object_ref[:, :, pl.ds(pl.multiple_of(last * LANES, LANES), LANES)]
    lane = lax.broadcasted_iota(jnp.int32, first.shape, 2)
    return jnp.where(lane < shift, third, first), second


def select_kernel(scan_ref, table_ref, object_ref, out_ref):
    _, col = lookup(table_ref, scan_ref[0])
    low, high = strip_window(object_ref, col)
    out_ref[:, :, :LANES] = low
    out_ref[:, :, LANES:] = high


def rolled(value, row, col):
    return pltpu.roll(pltpu.roll(value, col, 1), row, 0)


def prepare_kernel(
    own_scan_ref, received_ref, swapped_ref, table_ref, object_ref, own_probe_ref, other_probe_ref,
    amplitude_ref, probe_ref, factor_ref, window_ref, light_ref, nearer_ref, farther_ref, place_ref, rows_ref,
):
    modes = own_probe_ref.shape[0]
    height = object_ref.shape[1]
    frame = own_probe_ref.shape[2]
    tile = lax.axis_index("tile")
    core = lax.axis_index("mode")
    row, col = lookup(table_ref, own_scan_ref[0])
    row = row - tile * height
    shift = col % LANES
    total = jnp.zeros((frame, frame), jnp.float32)
    for index in range(2 * modes):
        source = own_probe_ref if index < modes else other_probe_ref
        for part in range(2):
            value = source[index % modes, part]
            total = total + value * value
            probe_ref[index, part] = rolled(value, row, shift)
    light_ref[...] = rolled(total, row, shift)
    low, high = strip_window(object_ref, col)
    window_ref[:, :, :LANES] = low
    window_ref[:, :, LANES:] = high
    nearer_scan = jnp.where(core == 0, received_ref[0], swapped_ref[0])
    farther_scan = jnp.where(core == 0, swapped_ref[0], received_ref[0])
    row1, col1 = lookup(table_ref, nearer_scan)
    row2, col2 = lookup(table_ref, farther_scan)
    row1 = row1 - (tile - 1) * height
    row2 = row2 - (tile - 2) * height
    row1 = jnp.where(tile < 1, 0, row1)
    row2 = jnp.where(tile < 2, 0, row2)
    nearer_ref[...] = rolled(total, row1, col1 % LANES)[height:]
    farther_ref[...] = rolled(total, row2, col2 % LANES)[:height]
    place_ref[0] = row
    place_ref[1] = col
    place_ref[2] = row1
    place_ref[3] = col1
    place_ref[4] = row2
    place_ref[5] = col2
    place_ref[6] = 0
    place_ref[7] = 0
    source = lax.broadcasted_iota(jnp.int32, (frame, frame), 0)
    target = lax.broadcasted_iota(jnp.int32, (frame, frame), 1)
    half = frame // 2
    order = jnp.where(target < half, 2 * target, 2 * target - frame + 1)
    pick = jnp.where(source == order, 1.0, 0.0).astype(jnp.bfloat16)
    value = amplitude_ref[0]
    high = value.astype(jnp.bfloat16)
    rest = value - high.astype(jnp.float32)
    middle = rest.astype(jnp.bfloat16)
    low = (rest - middle.astype(jnp.float32)).astype(jnp.bfloat16)
    columns = jnp.dot(high, pick, preferred_element_type=jnp.float32)
    columns = columns + jnp.dot(middle, pick, preferred_element_type=jnp.float32)
    columns = columns + jnp.dot(low, pick, preferred_element_type=jnp.float32)
    for index in range(frame // LANES):
        at = slice(index * LANES, (index + 1) * LANES)
        rows_ref[index] = columns[:, at]
        factor_ref[:half, at] = rows_ref[index, pl.ds(0, half, stride=2), :]
        factor_ref[half:, at] = rows_ref[index, pl.ds(1, half, stride=2), :]


def right(value, high, low):
    first, second = split(value)
    return jnp.dot(
        jnp.concatenate([first, second, first], axis=1),
        jnp.concatenate([high, high, low], axis=0),
        preferred_element_type=jnp.float32,
    )


def left(high, low, value):
    first, second = split(value)
    return jnp.dot(
        jnp.concatenate([high, high, low], axis=1),
        jnp.concatenate([first, second, first], axis=0),
        preferred_element_type=jnp.float32,
    )


def wave_kernel(
    count_ref, place_ref, window_ref, received_ref, swapped_ref, probe_ref, amplitude_ref, light_ref,
    matrix_ref, send_ref, keep_ref, patch_ref, far_ref,
):
    modes, _, frame, _ = probe_ref.shape
    height = window_ref.shape[1]
    half = frame // 2
    core = lax.axis_index("mode")
    row = place_ref[0]
    level = lax.broadcasted_iota(jnp.int32, (height, frame), 0)
    for part in range(2):
        got, given = received_ref[part], swapped_ref[part]
        nearer = jnp.where(core == 0, got, given)
        farther = jnp.where(core == 0, given, got)
        patch_ref[part, :height] = jnp.where(level < row, farther, window_ref[part])
        patch_ref[part, height:] = nearer
    intensity = jnp.zeros((frame, frame), jnp.float32)
    for mode in range(modes):
        probe_re, probe_im = probe_ref[mode, 0], probe_ref[mode, 1]
        patch_re, patch_im = patch_ref[0], patch_ref[1]
        wave_re = probe_re * patch_re - probe_im * patch_im
        wave_im = probe_re * patch_im + probe_im * patch_re
        added = jnp.concatenate([wave_re[:, :half] + wave_re[:, half:], wave_im[:, :half] + wave_im[:, half:]], axis=1)
        taken = jnp.concatenate([wave_re[:, :half] - wave_re[:, half:], wave_im[:, :half] - wave_im[:, half:]], axis=1)
        even = right(added, matrix_ref[0], matrix_ref[1])
        odd = right(taken, matrix_ref[4], matrix_ref[5])
        mid_re = jnp.concatenate([even[:, :half], odd[:, :half]], axis=1)
        mid_im = jnp.concatenate([even[:, half:], odd[:, half:]], axis=1)
        added = jnp.concatenate([mid_re[:half] + mid_re[half:], mid_im[:half] + mid_im[half:]], axis=0)
        taken = jnp.concatenate([mid_re[:half] - mid_re[half:], mid_im[:half] - mid_im[half:]], axis=0)
        even = left(matrix_ref[2], matrix_ref[3], added)
        odd = left(matrix_ref[6], matrix_ref[7], taken)
        far_ref[mode, 0] = even
        far_ref[mode, 1] = odd
        squares = jnp.concatenate(
            [even[:half] * even[:half] + even[half:] * even[half:], odd[:half] * odd[:half] + odd[half:] * odd[half:]],
            axis=0,
        )
        intensity = intensity + squares
    factor = amplitude_ref[...] * lax.rsqrt(jnp.maximum(intensity, FLOOR))
    grad_re = jnp.zeros((frame, frame), jnp.float32)
    grad_im = jnp.zeros((frame, frame), jnp.float32)
    even_factor = jnp.concatenate([factor[:half], factor[:half]], axis=0)
    odd_factor = jnp.concatenate([factor[half:], factor[half:]], axis=0)
    for mode in range(modes):
        even = left(matrix_ref[0], matrix_ref[1], far_ref[mode, 0] * even_factor)
        odd = left(matrix_ref[4], matrix_ref[5], far_ref[mode, 1] * odd_factor)
        top, bottom = even + odd, even - odd
        mid_re = jnp.concatenate([top[:half], bottom[:half]], axis=0)
        mid_im = jnp.concatenate([top[half:], bottom[half:]], axis=0)
        even = right(jnp.concatenate([mid_re[:, :half], mid_im[:, :half]], axis=1), matrix_ref[2], matrix_ref[3])
        odd = right(jnp.concatenate([mid_re[:, half:], mid_im[:, half:]], axis=1), matrix_ref[6], matrix_ref[7])
        fore, aft = even + odd, even - odd
        back_re = jnp.concatenate([fore[:, :half], aft[:, :half]], axis=1)
        back_im = jnp.concatenate([fore[:, half:], aft[:, half:]], axis=1)
        probe_re, probe_im = probe_ref[mode, 0], probe_ref[mode, 1]
        grad_re = grad_re + (probe_re * back_re + probe_im * back_im)
        grad_im = grad_im + (probe_re * back_im - probe_im * back_re)
    live = (count_ref[0] > 0).astype(jnp.float32)
    grad_re = (grad_re - light_ref[...] * patch_ref[0]) * live
    grad_im = (grad_im - light_ref[...] * patch_ref[1]) * live
    send_ref[:height] = jnp.where(core == 0, grad_re[height:], grad_re[:height])
    send_ref[height : 2 * height] = jnp.where(core == 0, grad_im[height:], grad_im[:height])
    send_ref[2 * height :] = jnp.full((8, frame), live, jnp.float32)
    keep_ref[0] = grad_re[:height]
    keep_ref[1] = grad_im[:height]


def covers(col, block, low, high, lane):
    start, shift = col // LANES, col % LANES
    distance = block - start
    value = jnp.where(distance == 1, high, low)
    first = jnp.where(distance == 0, shift, jnp.where(distance == 1, 0, LANES))
    last = jnp.where(distance == 2, shift, 0)
    keep = (lane >= first) | (lane < last)
    return jnp.where(keep, value, 0.0)


def base_kernel(
    count_ref, place_ref, object_ref, keep_ref, light_ref, updated_ref, gradient_ref, total_ref, weight_ref,
    new_ref, sems,
):
    height, breadth = object_ref.shape[1:]
    row, col = place_ref[0], place_ref[1]
    live = (count_ref[0] > 0).astype(jnp.float32)
    total_ref[...] = jnp.zeros_like(total_ref)
    weight_ref[...] = jnp.zeros_like(weight_ref)
    new_ref[...] = object_ref[...]
    lane = lax.broadcasted_iota(jnp.int32, (height, LANES), 1)
    level = lax.broadcasted_iota(jnp.int32, (height, LANES), 0)
    kept = level >= row
    for offset in range(3):
        block = jnp.minimum(col // LANES + offset, breadth // LANES - 1)
        at = pl.ds(pl.multiple_of(block * LANES, LANES), LANES)
        light = covers(col, block, light_ref[:height, :LANES], light_ref[:height, LANES:], lane)
        weight = jnp.where(kept, light * live, 0.0)
        weight_ref[:, at] = weight
        for part in range(2):
            change = covers(col, block, keep_ref[part, :, :LANES], keep_ref[part, :, LANES:], lane)
            change = jnp.where(kept, change, 0.0)
            total_ref[part, :, at] = change
            new_ref[part, :, at] = object_ref[part, :, at] + change / (weight + ALPHA)
    first = pltpu.make_async_copy(total_ref, gradient_ref, sems.at[0])
    second = pltpu.make_async_copy(new_ref, updated_ref, sems.at[1])
    first.start()
    second.start()
    first.wait()
    second.wait()


def final_kernel(
    place_ref, object_ref, total_ref, weight_ref, nearer_ref, farther_ref, received_ref, swapped_ref,
    old_updated_ref, old_gradient_ref, updated_ref, gradient_ref, new_ref, sum_ref, sems,
):
    del old_updated_ref, old_gradient_ref
    height, breadth = object_ref.shape[1:]
    blocks = breadth // LANES
    core = lax.axis_index("mode")
    col1, row2, col2 = place_ref[3], place_ref[4], place_ref[5]
    lane = lax.broadcasted_iota(jnp.int32, (height, LANES), 1)
    level = lax.broadcasted_iota(jnp.int32, (height, LANES), 0)
    start1, start2 = col1 // LANES, col2 // LANES
    copies = []
    for slot in range(6):
        start, offset = (start1, slot) if slot < 3 else (start2, slot - 3)
        block = jnp.minimum(start + offset, blocks - 1)
        fresh = start + offset < blocks
        if slot >= 3:
            fresh = fresh & ((block < start1) | (block > start1 + 2))
        at = pl.ds(pl.multiple_of(block * LANES, LANES), LANES)

        def halves(ref, base):
            return ref[base : base + height, :LANES], ref[base : base + height, LANES:]

        def pick(base):
            got, given = halves(received_ref, base), halves(swapped_ref, base)
            near = tuple(jnp.where(core == 0, a, b) for a, b in zip(got, given))
            far = tuple(jnp.where(core == 0, b, a) for a, b in zip(got, given))
            return near, far

        got, given = received_ref[2 * height : 2 * height + 1, :1], swapped_ref[2 * height : 2 * height + 1, :1]
        near_live = jnp.where(core == 0, got, given)
        far_live = jnp.where(core == 0, given, got)
        light = covers(col1, block, *halves(nearer_ref, 0), lane) * near_live
        light = light + jnp.where(level < row2, covers(col2, block, *halves(farther_ref, 0), lane), 0.0) * far_live
        scale = 1.0 / (weight_ref[:, at] + light + ALPHA)
        for part in range(2):
            near, far = pick(part * height)
            change = total_ref[part, :, at] + covers(col1, block, *near, lane)
            change = change + jnp.where(level < row2, covers(col2, block, *far, lane), 0.0)
            sum_ref[slot, part] = change
            new_ref[slot, part] = object_ref[part, :, at] + change * scale
        one = pltpu.make_async_copy(sum_ref.at[slot], gradient_ref.at[:, :, at], sems.at[2 * slot])
        two = pltpu.make_async_copy(new_ref.at[slot], updated_ref.at[:, :, at], sems.at[2 * slot + 1])
        copies.append((fresh, one, two))

        @pl.when(fresh)
        def _(one=one, two=two):
            one.start()
            two.start()

    for fresh, one, two in copies:

        @pl.when(fresh)
        def _(one=one, two=two):
            one.wait()
            two.wait()


def call(kernel, out_shape, in_specs, out_specs, scratch=(), cost=1, aliases=None):
    return pl.pallas_call(
        kernel,
        out_shape=out_shape,
        in_specs=in_specs,
        out_specs=out_specs,
        scratch_shapes=list(scratch),
        input_output_aliases=aliases or {},
        cost_estimate=pl.CostEstimate(flops=cost * 1000000, bytes_accessed=cost * 1000000, transcendentals=0),
        name=kernel.__name__,
    )


def space(where):
    return pl.BlockSpec(memory_space=where)


def shape(*dims, dtype=jnp.float32):
    return jax.ShapeDtypeStruct(dims, dtype)


def solution(mesh):
    tiles, cores = mesh.shape["tile"], mesh.shape["mode"]
    up = [(2 * t, 2 * (t + 1)) for t in range(tiles - 1)] + [(2 * t + 1, 2 * (t + 2) + 1) for t in range(tiles - 2)]
    down = [(target, source) for source, target in up]
    swap = [(2 * t + core, 2 * t + 1 - core) for t in range(tiles) for core in range(2)]
    assert cores == 2

    def move(value, pairs):
        return lax.ppermute(value, AXES, pairs)

    def shards(object_tiles, probe_modes, amplitudes, scan_offsets, slot_scan, slot_count):
        height, breadth = object_tiles.shape[1:]
        modes, _, frame, _ = probe_modes.shape
        assert slot_scan.shape[0] == 1 and frame == 2 * height and height == LANES
        table = scan_offsets.T
        matrix = jnp.asarray(matrices(frame))
        received_scan = move(slot_scan, up)
        other_probe = move(probe_modes, swap)
        window = call(
            select_kernel, shape(2, height, frame), [space(SMEM), space(VMEM), space(VMEM)], space(VMEM)
        )(received_scan, table, object_tiles)
        received = move(window, down)
        swapped_scan = move(received_scan, swap)
        probe, amplitude, own_window, light, nearer, farther, place = call(
            prepare_kernel,
            (
                shape(2 * modes, 2, frame, frame),
                shape(frame, frame),
                shape(2, height, frame),
                shape(frame, frame),
                shape(height, frame),
                shape(height, frame),
                shape(8, dtype=jnp.int32),
            ),
            [space(SMEM)] * 3 + [space(VMEM)] * 5,
            [space(VMEM)] * 6 + [space(SMEM)],
            [pltpu.VMEM((frame // LANES, frame, LANES), jnp.float32)],
            cost=5,
        )(slot_scan, received_scan, swapped_scan, table, object_tiles, probe_modes, other_probe, amplitudes)
        swapped = move(received, swap)
        send, keep = call(
            wave_kernel,
            (shape(2 * height + 8, frame), shape(2, height, frame)),
            [space(SMEM)] * 2 + [space(VMEM)] * 7,
            [space(VMEM)] * 2,
            [
                pltpu.VMEM((2, frame, frame), jnp.float32),
                pltpu.VMEM((2 * modes, 2, frame, frame), jnp.float32),
            ],
            cost=5,
        )(slot_count, place, own_window, received, swapped, probe, amplitude, light, matrix)
        received_change = move(send, up)
        updated, gradient, total, weight = call(
            base_kernel,
            (
                shape(2, height, breadth),
                shape(2, height, breadth),
                shape(2, height, breadth),
                shape(height, breadth),
            ),
            [space(SMEM)] * 2 + [space(VMEM)] * 3,
            [space(pl.ANY)] * 2 + [space(VMEM)] * 2,
            [pltpu.VMEM((2, height, breadth), jnp.float32), pltpu.SemaphoreType.DMA((2,))],
            cost=5,
        )(slot_count, place, object_tiles, keep, light)
        swapped_change = move(received_change, swap)
        updated, gradient = call(
            final_kernel,
            (shape(2, height, breadth), shape(2, height, breadth)),
            [space(SMEM)] + [space(VMEM)] * 7 + [space(pl.ANY)] * 2,
            [space(pl.ANY)] * 2,
            [
                pltpu.VMEM((6, 2, height, LANES), jnp.float32),
                pltpu.VMEM((6, 2, height, LANES), jnp.float32),
                pltpu.SemaphoreType.DMA((12,)),
            ],
            aliases={8: 0, 9: 1},
        )(place, object_tiles, total, weight, nearer, farther, received_change, swapped_change, updated, gradient)
        return (updated, gradient)

    return jax.shard_map(
        shards,
        mesh=mesh,
        in_specs=(
            P(None, "tile", None),
            P("mode", None, None, None),
            P("tile", None, None),
            P(),
            P("tile"),
            P("tile"),
        ),
        out_specs=(P(None, "tile", None), P(None, "tile", None)),
        check_vma=False,
    )
```

time: 184 us -> 63.2 us (0.34)
  waiting for transfers between devices: 67.6 us -> 15.7 us
  Pallas kernels: 0 us -> 28 us
  matrix products: 27.6 us -> 0 us
  local copies, waits for them, and re-layouts: 28.4 us -> 2.36 us
  between operations: 27.2 us -> 2.03 us
  other arithmetic: 14.4 us -> 0 us
  starting transfers between devices: 17.5 us -> 14.8 us
    psum x3 -> x0, waiting for transfers between devices: 58.5 us -> none  [the longest x1 21.9 us: shards(): lax.psum(jnp.sum(far_re * far_re + far_im * far_im, axis=1), 'mode')]
    pallas_call x0 -> x5, Pallas kernels: none -> 28 us  [the longest x1 8.07 us: shards(): call(wave_kernel, (shape(2 * height + 8, frame), shape(2, height, frame))...]
    dot_general x16 -> x0, matrix products: 27.6 us -> none  [product(): return jnp.matmul(first, second, precision=lax.Precision.HIGHEST)]
    dynamic_update_slice x3 -> x0, local copies, waits for them, and re-layouts: 16.4 us -> none  [add_block(): lax.dynamic_update_slice(accum, current + block[index], (anchor, anchor,...]
    add x3 -> x0, other arithmetic: 6.85 us -> none  [the longest x1 4.51 us: shards(): updated = object_tiles + gradient / (cover + ALPHA)]
    ppermute x6 -> x7, waiting for transfers between devices: 9.1 us -> 15.7 us  [move(): return lax.ppermute(value, AXES, pairs)]
    scatter x1 -> x0, local copies, waits for them, and re-layouts: 5.08 us -> none  [place(): return lax.dynamic_update_slice(empty, piece, (anchor, row_at, anchor))]
    another operation x4 -> x0, other arithmetic: 4.36 us -> none
  transfers between devices with their start and end apart: 9 -> 7, of which waited for: 7 -> 4; matrix products, arithmetic and copies ran while one was open for 9% -> 0% of each run, Pallas kernels for 0% -> 25%
where the time goes in v1:
time: 63.2 us; the launch traced here: 63 us
  Pallas kernels  28 us (44%)
  waiting for transfers between devices  15.7 us (25%)
  starting transfers between devices  14.8 us (23%)
  local copies, waits for them, and re-layouts  2.36 us (4%)
  between operations  2.03 us (3%)
    ppermute x7, waiting for transfers between devices, move(): return lax.ppermute(value, AXES, pairs)  15.7 us
    ppermute x7, starting transfers between devices, move(): return lax.ppermute(value, AXES, pairs)  14.8 us
    pallas_call x1, Pallas kernels, shards(): call(wave_kernel, (shape(2 * height + 8, frame), shape(2, height, frame))...  8.07 us
    pallas_call x1, Pallas kernels, shards(): call(prepare_kernel, (shape(2 * modes, 2, frame, frame), shape(frame, fra...  6.61 us
    pallas_call x1, Pallas kernels, shards(): call(base_kernel, (shape(2, height, breadth), shape(2, height, breadth),...  5.86 us
    pallas_call x1, Pallas kernels, shards(): call(final_kernel, (shape(2, height, breadth), shape(2, height, breadth))...  4.32 us
    pallas_call x1, Pallas kernels, shards(): call(select_kernel, shape(2, height, frame), [space(SMEM), space(VMEM), s...  3.15 us
    unnamed x10, local copies, waits for them, and re-layouts  2.36 us
  transfers between devices with their start and end apart: 7, of which 4 were waited for; matrix products, arithmetic and copies ran while one was open for 0% of the time, Pallas kernels for 25%

profile of v1, /device:TPU:9, one launch (start us, length us, event | category | flops | bytes accessed | tf_op | source)
XLA Modules:
  0.0 63.0 jit_solution(7390790073462092865)
XLA Ops:
  0.6 0.7 %collective-permute-start.2 = (f32[2,2,256,256]{3,2,1,0:T(8,128)}, f32[2,2,256,256]{3,2,1,0:T(8,128)S(1)}, u32[]{:S(2)}, u32[]{:S(2)}) collective-permute-start(f32[2,2,256,256]{3,2,1,0:T(8,128)} %own_probe_ref.1), channel_id=1, source_target_pairs={{0,1},{1,0},{2,3},{3,2},{4,5},{5,4},{6,7},{7,6},{8,9},{9,8},{10,11... | collective-permute-start | bytes 3145736 | tf_op jit(solution)/shard_map/ppermute | solution.py:350
  1.4 3.1 %collective-permute-start = (s32[1]{0:T(128)}, s32[1]{0:T(128)}, u32[]{:S(2)}, u32[]{:S(2)}) collective-permute-start(s32[1]{0:T(128)} %param.11), channel_id=1, source_target_pairs={{0,2},{2,4},{4,6},{6,8},{8,10},{10,12},{12,14},{14,16},{16,18},{18... | collective-permute-start | bytes 20 | tf_op jit(solution)/shard_map/ppermute | solution.py:350
  4.5 2.1 %collective-permute-done.received_ref.scan_ref = s32[1]{0:T(128)} collective-permute-done((s32[1]{0:T(128)}, s32[1]{0:T(128)}, u32[]{:S(2)}, u32[]{:S(2)}) %collective-permute-start) | collective-permute-done | bytes 36 | tf_op jit(solution)/shard_map/ppermute | solution.py:350
  6.7 3.1 %select_kernel.1 = f32[2,128,256]{2,1,0:T(8,128)} custom-call(s32[1]{0:T(128)} %collective-permute-done.received_ref.scan_ref, s32[2,8192]{1,0:T(2,128)} %bitcast.1, f32[2,128,2048]{2,1,0:T(8,128)} %object_ref.7), custom_call_target="tpu_custom_call" | custom-call | flops 1000000 | bytes 1000000 | tf_op jit(solution)/shard_map/select_kernel/pallas_call | solution.py:360
  9.8 2.1 %collective-permute-start.3 = (f32[2,128,256]{2,1,0:T(8,128)}, f32[2,128,256]{2,1,0:T(8,128)S(1)}, u32[]{:S(2)}, u32[]{:S(2)}) collective-permute-start(f32[2,128,256]{2,1,0:T(8,128)} %select_kernel.1), channel_id=1, source_target_pairs={{2,0},{4,2},{6,4},{8,6},{10,8},{12,10},{14,12},{16,14},{18,16},{20... | collective-permute-start | bytes 786440 | tf_op jit(solution)/shard_map/ppermute | solution.py:350
  11.9 5.5 %collective-permute-done.3.received_ref = f32[2,128,256]{2,1,0:T(8,128)S(1)} collective-permute-done((f32[2,128,256]{2,1,0:T(8,128)}, f32[2,128,256]{2,1,0:T(8,128)S(1)}, u32[]{:S(2)}, u32[]{:S(2)}) %collective-permute-start.3) | collective-permute-done | bytes 262176 | tf_op jit(solution)/shard_map/ppermute | solution.py:350
  17.4 0.0 copy-start.3
  17.4 3.1 %collective-permute-start.4 = (f32[2,128,256]{2,1,0:T(8,128)S(1)}, f32[2,128,256]{2,1,0:T(8,128)S(1)}, u32[]{:S(2)}, u32[]{:S(2)}) collective-permute-start(f32[2,128,256]{2,1,0:T(8,128)S(1)} %collective-permute-done.3.received_ref), channel_id=1, source_target_pairs={{0,1},{1,0},{2,3},{3,2},{4,5},{5,4},{6,7},{7,6},{8,9},{9,8},{10,11... | collective-permute-start | bytes 786440 | tf_op jit(solution)/shard_map/ppermute | solution.py:350
  21.8 0.1 collective-permute-start.1
  21.9 1.3 %collective-permute-done.1.swapped_ref = s32[1]{0:T(128)} collective-permute-done((s32[1]{0:T(128)}, s32[1]{0:T(128)}, u32[]{:S(2)}, u32[]{:S(2)}) %collective-permute-start.1) | collective-permute-done | bytes 36 | tf_op jit(solution)/shard_map/ppermute | solution.py:350
  23.2 0.0 collective-permute-done.2.other_probe_ref
  23.2 0.0 copy-start
  23.2 1.0 %copy-done = f32[2,2,256,256]{3,2,1,0:T(8,128)} copy-done((f32[2,2,256,256]{3,2,1,0:T(8,128)}, f32[2,2,256,256]{3,2,1,0:T(8,128)S(1)}, u32[]{:S(2)}) %copy-start) | copy-done | bytes 1048600
  24.2 6.6 %prepare_kernel.1 = (f32[4,2,256,256]{3,2,1,0:T(8,128)}, f32[256,256]{1,0:T(8,128)}, f32[2,128,256]{2,1,0:T(8,128)}, f32[256,256]{1,0:T(8,128)}, f32[128,256]{1,...) custom-call(s32[1]{0:T(128)S(6)} %copy.13.own_scan_ref, s32[1]{0:T(128)} %collective-permute-done.received_ref.scan_ref, ...), custom_call_target="tpu_custom_call" | custom-call | flops 5000000 | bytes 5000000 | tf_op jit(solution)/shard_map/prepare_kernel/pallas_call | solution.py:365
  30.8 0.0 collective-permute-done.4.swapped_ref
  30.8 0.0 copy-start.4
  30.8 0.0 copy-done.3
  30.8 0.7 %copy-done.4 = f32[2,128,256]{2,1,0:T(8,128)} copy-done((f32[2,128,256]{2,1,0:T(8,128)}, f32[2,128,256]{2,1,0:T(8,128)S(1)}, u32[]{:S(2)}) %copy-start.4) | copy-done | bytes 262168
  31.5 8.1 %wave_kernel.1 = (f32[264,256]{1,0:T(8,128)}, f32[2,128,256]{2,1,0:T(8,128)}) custom-call(s32[1]{0:T(128)S(6)} %copy.14.count_ref, s32[8]{0:T(128)} %get-tuple-element.15.place_ref, f32[2,128,256]{2,1,0:T(8,128)} %get-tuple-element.16.window_ref, f32[2,128,256]{2,1,0:T(8,128)} %copy-done.3, f32[2,128,256]{2,1,0:T(8,128)} %copy-done.4, ...), custom_call_target="tpu_custom_call" | custom-call | flops 5000000 | bytes 5000000 | tf_op jit(solution)/shard_map/wave_kernel/pallas_call | solution.py:382
  39.6 2.2 %collective-permute-start.5 = (f32[264,256]{1,0:T(8,128)}, f32[264,256]{1,0:T(8,128)S(1)}, u32[]{:S(2)}, u32[]{:S(2)}) collective-permute-start(f32[264,256]{1,0:T(8,128)} %get-tuple-element.25), channel_id=1, source_target_pairs={{0,2},{2,4},{4,6},{6,8},{8,10},{10,12},{12,14},{14,16},{16,18},{18... | collective-permute-start | bytes 811016 | tf_op jit(solution)/shard_map/ppermute | solution.py:350
  41.9 6.8 %collective-permute-done.5.received_ref = f32[264,256]{1,0:T(8,128)S(1)} collective-permute-done((f32[264,256]{1,0:T(8,128)}, f32[264,256]{1,0:T(8,128)S(1)}, u32[]{:S(2)}, u32[]{:S(2)}) %collective-permute-start.5) | collective-permute-done | bytes 270368 | tf_op jit(solution)/shard_map/ppermute | solution.py:350
  48.6 0.0 copy-start.1
  48.6 3.4 %collective-permute-start.6 = (f32[264,256]{1,0:T(8,128)S(1)}, f32[264,256]{1,0:T(8,128)S(1)}, u32[]{:S(2)}, u32[]{:S(2)}) collective-permute-start(f32[264,256]{1,0:T(8,128)S(1)} %collective-permute-done.5.received_ref), channel_id=1, source_target_pairs={{0,1},{1,0},{2,3},{3,2},{4,5},{5,4},{6,7},{7,6},{8,9},{9,8},{10,11... | collective-permute-start | bytes 811016 | tf_op jit(solution)/shard_map/ppermute | solution.py:350
  52.1 5.9 %base_kernel.1 = (f32[2,128,2048]{2,1,0:T(8,128)}, f32[2,128,2048]{2,1,0:T(8,128)}, f32[2,128,2048]{2,1,0:T(8,128)}, f32[128,2048]{1,0:T(8,128)}) custom-call(s32[1]{0:T(128)S(6)} %copy.14.count_ref, s32[8]{0:T(128)} %get-tuple-element.15.place_ref, f32[2,128,2048]{2,1,0:T(8,128)} %object_ref.7, f32[2,128,256]{2,1,0:T(8,128)} %get-tuple-element.20.keep_ref, ...), custom_call_target="tpu_custom_call" | custom-call | flops 5000000 | bytes 5000000 | tf_op jit(solution)/shard_map/base_kernel/pallas_call | solution.py:394
  57.9 0.0 collective-permute-done.6.swapped_ref
  57.9 0.0 copy-start.2
  58.0 0.0 copy-done.1
  58.0 0.7 %copy-done.2 = f32[264,256]{1,0:T(8,128)} copy-done((f32[264,256]{1,0:T(8,128)}, f32[264,256]{1,0:T(8,128)S(1)}, u32[]{:S(2)}) %copy-start.2) | copy-done | bytes 270360
  58.6 4.3 %final_kernel.1 = (f32[2,128,2048]{2,1,0:T(8,128)}, f32[2,128,2048]{2,1,0:T(8,128)}) custom-call(s32[8]{0:T(128)} %get-tuple-element.15.place_ref, f32[2,128,2048]{2,1,0:T(8,128)} %object_ref.7, f32[2,128,2048]{2,1,0:T(8,128)} %get-tuple-element.21.total_ref, ...), custom_call_target="tpu_custom_call", output_to_operand_aliasing={{0}: (8, {}), {1}: (9, {})} | custom-call | flops 1000000 | bytes 1000000 | tf_op jit(solution)/shard_map/final_kernel/pallas_call | solution.py:408
Async XLA Ops:
  0.6 22.6 %collective-permute-start.2 = (f32[2,2,256,256]{3,2,1,0:T(8,128)}, f32[2,2,256,256]{3,2,1,0:T(8,128)S(1)}, u32[]{:S(2)}, u32[]{:S(2)}) collective-permute-start(f32[2,2,256,256]{3,2,1,0:T(8,128)} %own_probe_ref.1), channel_id=1, source_target_pairs={{0,1},{1,0},{2,3},{3,2},{4,5},{5,4},{6,7},{7,6},{8,9},{9,8},{10,11... | collective-permute-start | bytes 3145736 | tf_op jit(solution)/shard_map/ppermute | solution.py:350
  1.4 5.3 %collective-permute-start = (s32[1]{0:T(128)}, s32[1]{0:T(128)}, u32[]{:S(2)}, u32[]{:S(2)}) collective-permute-start(s32[1]{0:T(128)} %param.11), channel_id=1, source_target_pairs={{0,2},{2,4},{4,6},{6,8},{8,10},{10,12},{12,14},{14,16},{16,18},{18... | collective-permute-start | bytes 20 | tf_op jit(solution)/shard_map/ppermute | solution.py:350
  9.8 7.6 %collective-permute-start.3 = (f32[2,128,256]{2,1,0:T(8,128)}, f32[2,128,256]{2,1,0:T(8,128)S(1)}, u32[]{:S(2)}, u32[]{:S(2)}) collective-permute-start(f32[2,128,256]{2,1,0:T(8,128)} %select_kernel.1), channel_id=1, source_target_pairs={{2,0},{4,2},{6,4},{8,6},{10,8},{12,10},{14,12},{16,14},{18,16},{20... | collective-permute-start | bytes 786440 | tf_op jit(solution)/shard_map/ppermute | solution.py:350
  17.4 13.4 %copy-start.3 = (f32[2,128,256]{2,1,0:T(8,128)}, f32[2,128,256]{2,1,0:T(8,128)S(1)}, u32[]{:S(2)}) copy-start(f32[2,128,256]{2,1,0:T(8,128)S(1)} %collective-permute-done.3.received_ref) | copy-start | bytes 786436
  17.4 13.4 %collective-permute-start.4 = (f32[2,128,256]{2,1,0:T(8,128)S(1)}, f32[2,128,256]{2,1,0:T(8,128)S(1)}, u32[]{:S(2)}, u32[]{:S(2)}) collective-permute-start(f32[2,128,256]{2,1,0:T(8,128)S(1)} %collective-permute-done.3.received_ref), channel_id=1, source_target_pairs={{0,1},{1,0},{2,3},{3,2},{4,5},{5,4},{6,7},{7,6},{8,9},{9,8},{10,11... | collective-permute-start | bytes 786440 | tf_op jit(solution)/shard_map/ppermute | solution.py:350
  21.8 1.4 %collective-permute-start.1 = (s32[1]{0:T(128)}, s32[1]{0:T(128)}, u32[]{:S(2)}, u32[]{:S(2)}) collective-permute-start(s32[1]{0:T(128)} %collective-permute-done.received_ref.scan_ref), channel_id=1, source_target_pairs={{0,1},{1,0},{2,3},{3,2},{4,5},{5,4},{6,7},{7,6},{8,9},{9,8},{10,11... | collective-permute-start | bytes 20 | tf_op jit(solution)/shard_map/ppermute | solution.py:350
  23.2 1.0 %copy-start = (f32[2,2,256,256]{3,2,1,0:T(8,128)}, f32[2,2,256,256]{3,2,1,0:T(8,128)S(1)}, u32[]{:S(2)}) copy-start(f32[2,2,256,256]{3,2,1,0:T(8,128)S(1)} %collective-permute-done.2.other_probe_ref) | copy-start | bytes 3145732
  30.8 0.7 %copy-start.4 = (f32[2,128,256]{2,1,0:T(8,128)}, f32[2,128,256]{2,1,0:T(8,128)S(1)}, u32[]{:S(2)}) copy-start(f32[2,128,256]{2,1,0:T(8,128)S(1)} %collective-permute-done.4.swapped_ref) | copy-start | bytes 786436
  39.6 9.0 %collective-permute-start.5 = (f32[264,256]{1,0:T(8,128)}, f32[264,256]{1,0:T(8,128)S(1)}, u32[]{:S(2)}, u32[]{:S(2)}) collective-permute-start(f32[264,256]{1,0:T(8,128)} %get-tuple-element.25), channel_id=1, source_target_pairs={{0,2},{2,4},{4,6},{6,8},{8,10},{10,12},{12,14},{14,16},{16,18},{18... | collective-permute-start | bytes 811016 | tf_op jit(solution)/shard_map/ppermute | solution.py:350
  48.6 9.3 %copy-start.1 = (f32[264,256]{1,0:T(8,128)}, f32[264,256]{1,0:T(8,128)S(1)}, u32[]{:S(2)}) copy-start(f32[264,256]{1,0:T(8,128)S(1)} %collective-permute-done.5.received_ref) | copy-start | bytes 811012
  48.6 9.3 %collective-permute-start.6 = (f32[264,256]{1,0:T(8,128)S(1)}, f32[264,256]{1,0:T(8,128)S(1)}, u32[]{:S(2)}, u32[]{:S(2)}) collective-permute-start(f32[264,256]{1,0:T(8,128)S(1)} %collective-permute-done.5.received_ref), channel_id=1, source_target_pairs={{0,1},{1,0},{2,3},{3,2},{4,5},{5,4},{6,7},{7,6},{8,9},{9,8},{10,11... | collective-permute-start | bytes 811016 | tf_op jit(solution)/shard_map/ppermute | solution.py:350
  57.9 0.7 %copy-start.2 = (f32[264,256]{1,0:T(8,128)}, f32[264,256]{1,0:T(8,128)S(1)}, u32[]{:S(2)}) copy-start(f32[264,256]{1,0:T(8,128)S(1)} %collective-permute-done.6.swapped_ref) | copy-start | bytes 811012

commit v2 on v1

--- a/solution.py
+++ b/solution.py
@@ -7,6 +7,7 @@
 from jax.experimental import pallas as pl
 from jax.experimental.pallas import tpu as pltpu
 from jax.sharding import PartitionSpec as P
+
 
 FLOOR = 0.25
 ALPHA = 0.5
@@ -59,6 +60,15 @@
     return jnp.where(lane < shift, third, first), second
 
 
+def stage_kernel(object_ref, table_ref, staged_ref, held_ref, sems):
+    first = pltpu.make_async_copy(object_ref, staged_ref, sems.at[0])
+    second = pltpu.make_async_copy(table_ref, held_ref, sems.at[1])
+    first.start()
+    second.start()
+    first.wait()
+    second.wait()
+
+
 def select_kernel(scan_ref, table_ref, object_ref, out_ref):
     _, col = lookup(table_ref, scan_ref[0])
     low, high = strip_window(object_ref, col)
@@ -71,16 +81,14 @@
 
 
 def prepare_kernel(
-    own_scan_ref, received_ref, swapped_ref, table_ref, object_ref, own_probe_ref, other_probe_ref,
-    amplitude_ref, probe_ref, factor_ref, window_ref, light_ref, nearer_ref, farther_ref, place_ref, rows_ref,
+    scan_ref, count_ref, table_ref, object_ref, own_probe_ref, other_probe_ref, amplitude_ref,
+    probe_ref, factor_ref, window_ref, light_ref, total_ref, place_ref, rows_ref,
 ):
     modes = own_probe_ref.shape[0]
     height = object_ref.shape[1]
     frame = own_probe_ref.shape[2]
-    tile = lax.axis_index("tile")
-    core = lax.axis_index("mode")
-    row, col = lookup(table_ref, own_scan_ref[0])
-    row = row - tile * height
+    row, col = lookup(table_ref, scan_ref[0])
+    row = row - lax.axis_index("tile") * height
     shift = col % LANES
     total = jnp.zeros((frame, frame), jnp.float32)
     for index in range(2 * modes):
@@ -89,28 +97,15 @@
             value = source[index % modes, part]
             total = total + value * value
             probe_ref[index, part] = rolled(value, row, shift)
+    total_ref[...] = total
     light_ref[...] = rolled(total, row, shift)
     low, high = strip_window(object_ref, col)
     window_ref[:, :, :LANES] = low
     window_ref[:, :, LANES:] = high
-    nearer_scan = jnp.where(core == 0, received_ref[0], swapped_ref[0])
-    farther_scan = jnp.where(core == 0, swapped_ref[0], received_ref[0])
-    row1, col1 = lookup(table_ref, nearer_scan)
-    row2, col2 = lookup(table_ref, farther_scan)
-    row1 = row1 - (tile - 1) * height
-    row2 = row2 - (tile - 2) * height
-    row1 = jnp.where(tile < 1, 0, row1)
-    row2 = jnp.where(tile < 2, 0, row2)
-    nearer_ref[...] = rolled(total, row1, col1 % LANES)[height:]
-    farther_ref[...] = rolled(total, row2, col2 % LANES)[:height]
     place_ref[0] = row
     place_ref[1] = col
-    place_ref[2] = row1
-    place_ref[3] = col1
-    place_ref[4] = row2
-    place_ref[5] = col2
-    place_ref[6] = 0
-    place_ref[7] = 0
+    place_ref[2] = count_ref[0]
+    place_ref[3] = 0
     source = lax.broadcasted_iota(jnp.int32, (frame, frame), 0)
     target = lax.broadcasted_iota(jnp.int32, (frame, frame), 1)
     half = frame // 2
@@ -150,7 +145,7 @@
 
 
 def wave_kernel(
-    count_ref, place_ref, window_ref, received_ref, swapped_ref, probe_ref, amplitude_ref, light_ref,
+    place_ref, window_ref, received_ref, swapped_ref, probe_ref, amplitude_ref, light_ref,
     matrix_ref, send_ref, keep_ref, patch_ref, far_ref,
 ):
     modes, _, frame, _ = probe_ref.shape
@@ -207,7 +202,7 @@
         probe_re, probe_im = probe_ref[mode, 0], probe_ref[mode, 1]
         grad_re = grad_re + (probe_re * back_re + probe_im * back_im)
         grad_im = grad_im + (probe_re * back_im - probe_im * back_re)
-    live = (count_ref[0] > 0).astype(jnp.float32)
+    live = (place_ref[2] > 0).astype(jnp.float32)
     grad_re = (grad_re - light_ref[...] * patch_ref[0]) * live
     grad_im = (grad_im - light_ref[...] * patch_ref[1]) * live
     send_ref[:height] = jnp.where(core == 0, grad_re[height:], grad_re[:height])
@@ -228,12 +223,14 @@
 
 
 def base_kernel(
-    count_ref, place_ref, object_ref, keep_ref, light_ref, updated_ref, gradient_ref, total_ref, weight_ref,
-    new_ref, sems,
+    place_ref, received_ref, swapped_ref, table_ref, object_ref, keep_ref, light_ref, plain_ref,
+    updated_ref, gradient_ref, total_ref, weight_ref, nearer_ref, farther_ref, others_ref, new_ref, sems,
 ):
     height, breadth = object_ref.shape[1:]
+    tile = lax.axis_index("tile")
+    core = lax.axis_index("mode")
     row, col = place_ref[0], place_ref[1]
-    live = (count_ref[0] > 0).astype(jnp.float32)
+    live = (place_ref[2] > 0).astype(jnp.float32)
     total_ref[...] = jnp.zeros_like(total_ref)
     weight_ref[...] = jnp.zeros_like(weight_ref)
     new_ref[...] = object_ref[...]
@@ -255,6 +252,16 @@
     second = pltpu.make_async_copy(new_ref, updated_ref, sems.at[1])
     first.start()
     second.start()
+    row1, col1 = lookup(table_ref, jnp.where(core == 0, received_ref[0], swapped_ref[0]))
+    row2, col2 = lookup(table_ref, jnp.where(core == 0, swapped_ref[0], received_ref[0]))
+    row1 = jnp.where(tile < 1, 0, row1 - (tile - 1) * height)
+    row2 = jnp.where(tile < 2, 0, row2 - (tile - 2) * height)
+    nearer_ref[...] = rolled(plain_ref[...], row1, col1 % LANES)[height:]
+    farther_ref[...] = rolled(plain_ref[...], row2, col2 % LANES)[:height]
+    others_ref[0] = col1
+    others_ref[1] = row2
+    others_ref[2] = col2
+    others_ref[3] = 0
     first.wait()
     second.wait()
 
@@ -267,7 +274,7 @@
     height, breadth = object_ref.shape[1:]
     blocks = breadth // LANES
     core = lax.axis_index("mode")
-    col1, row2, col2 = place_ref[3], place_ref[4], place_ref[5]
+    col1, row2, col2 = place_ref[0], place_ref[1], place_ref[2]
     lane = lax.broadcasted_iota(jnp.int32, (height, LANES), 1)
     level = lax.broadcasted_iota(jnp.int32, (height, LANES), 0)
     start1, start2 = col1 // LANES, col2 // LANES
@@ -318,7 +325,7 @@
             two.wait()
 
 
-def call(kernel, out_shape, in_specs, out_specs, scratch=(), cost=1, aliases=None):
+def call(kernel, out_shape, in_specs, out_specs, scratch=(), mebibytes=16, aliases=None):
     return pl.pallas_call(
         kernel,
         out_shape=out_shape,
@@ -326,8 +333,8 @@
         out_specs=out_specs,
         scratch_shapes=list(scratch),
         input_output_aliases=aliases or {},
-        cost_estimate=pl.CostEstimate(flops=cost * 1000000, bytes_accessed=cost * 1000000, transcendentals=0),
-        name=kernel.__name__,
+        compiler_params=pltpu.CompilerParams(vmem_limit_bytes=mebibytes << 20),
+        cost_estimate=pl.CostEstimate(flops=5000000, bytes_accessed=5000000, transcendentals=0),
     )
 
 
@@ -349,7 +356,7 @@
     def move(value, pairs):
         return lax.ppermute(value, AXES, pairs)
 
-    def shards(object_tiles, probe_modes, amplitudes, scan_offsets, slot_scan, slot_count):
+    def step(object_tiles, probe_modes, amplitudes, scan_offsets, slot_scan, slot_count):
         height, breadth = object_tiles.shape[1:]
         modes, _, frame, _ = probe_modes.shape
         assert slot_scan.shape[0] == 1 and frame == 2 * height and height == LANES
@@ -357,55 +364,63 @@
         matrix = jnp.asarray(matrices(frame))
         received_scan = move(slot_scan, up)
         other_probe = move(probe_modes, swap)
+        staged, table = call(
+            stage_kernel,
+            (shape(*object_tiles.shape), shape(*table.shape, dtype=jnp.int32)),
+            [space(pl.ANY)] * 2,
+            [space(VMEM)] * 2,
+            [pltpu.SemaphoreType.DMA((2,))],
+            mebibytes=8,
+        )(object_tiles, table)
         window = call(
             select_kernel, shape(2, height, frame), [space(SMEM), space(VMEM), space(VMEM)], space(VMEM)
-        )(received_scan, table, object_tiles)
+        )(received_scan, table, staged)
         received = move(window, down)
         swapped_scan = move(received_scan, swap)
-        probe, amplitude, own_window, light, nearer, farther, place = call(
+        probe, amplitude, own_window, light, plain, place = call(
             prepare_kernel,
             (
                 shape(2 * modes, 2, frame, frame),
                 shape(frame, frame),
                 shape(2, height, frame),
                 shape(frame, frame),
-                shape(height, frame),
-                shape(height, frame),
-                shape(8, dtype=jnp.int32),
+                shape(frame, frame),
+                shape(4, dtype=jnp.int32),
             ),
-            [space(SMEM)] * 3 + [space(VMEM)] * 5,
-            [space(VMEM)] * 6 + [space(SMEM)],
+            [space(SMEM)] * 2 + [space(VMEM)] * 5,
+            [space(VMEM)] * 5 + [space(SMEM)],
             [pltpu.VMEM((frame // LANES, frame, LANES), jnp.float32)],
-            cost=5,
-        )(slot_scan, received_scan, swapped_scan, table, object_tiles, probe_modes, other_probe, amplitudes)
+        )(slot_scan, slot_count, table, staged, probe_modes, other_probe, amplitudes)
         swapped = move(received, swap)
         send, keep = call(
             wave_kernel,
             (shape(2 * height + 8, frame), shape(2, height, frame)),
-            [space(SMEM)] * 2 + [space(VMEM)] * 7,
+            [space(SMEM)] + [space(VMEM)] * 7,
             [space(VMEM)] * 2,
             [
                 pltpu.VMEM((2, frame, frame), jnp.float32),
                 pltpu.VMEM((2 * modes, 2, frame, frame), jnp.float32),
             ],
-            cost=5,
-        )(slot_count, place, own_window, received, swapped, probe, amplitude, light, matrix)
+            mebibytes=24,
+        )(place, own_window, received, swapped, probe, amplitude, light, matrix)
         received_change = move(send, up)
-        updated, gradient, total, weight = call(
+        updated, gradient, total, weight, nearer, farther, others = call(
             base_kernel,
             (
                 shape(2, height, breadth),
                 shape(2, height, breadth),
                 shape(2, height, breadth),
                 shape(height, breadth),
+                shape(height, frame),
+                shape(height, frame),
+                shape(4, dtype=jnp.int32),
             ),
-            [space(SMEM)] * 2 + [space(VMEM)] * 3,
-            [space(pl.ANY)] * 2 + [space(VMEM)] * 2,
+            [space(SMEM)] * 3 + [space(VMEM)] * 5,
+            [space(pl.ANY)] * 2 + [space(VMEM)] * 4 + [space(SMEM)],
             [pltpu.VMEM((2, height, breadth), jnp.float32), pltpu.SemaphoreType.DMA((2,))],
-            cost=5,
-        )(slot_count, place, object_tiles, keep, light)
+        )(place, received_scan, swapped_scan, table, staged, keep, light, plain)
         swapped_change = move(received_change, swap)
-        updated, gradient = call(
+        return call(
             final_kernel,
             (shape(2, height, breadth), shape(2, height, breadth)),
             [space(SMEM)] + [space(VMEM)] * 7 + [space(pl.ANY)] * 2,
@@ -416,11 +431,10 @@
                 pltpu.SemaphoreType.DMA((12,)),
             ],
             aliases={8: 0, 9: 1},
-        )(place, object_tiles, total, weight, nearer, farther, received_change, swapped_change, updated, gradient)
-        return (updated, gradient)
+        )(others, staged, total, weight, nearer, farther, received_change, swapped_change, updated, gradient)
 
     return jax.shard_map(
-        shards,
+        step,
         mesh=mesh,
         in_specs=(
             P(None, "tile", None),

time: 63.2 us -> 49.4 us (0.78)
  Pallas kernels: 28 us -> 16.5 us
  waiting for transfers between devices: 15.7 us -> 12.1 us
  starting transfers between devices: 14.8 us -> 16.1 us
    pallas_call x5 -> x6, Pallas kernels: 28 us -> 16.5 us  [the longest x1 5.9 us: step(): call(wave_kernel, (shape(2 * height + 8, frame), shape(2, height, frame))...]
    ppermute x7, waiting for transfers between devices: 15.7 us -> 12.1 us  [move(): return lax.ppermute(value, AXES, pairs)]
    ppermute x7, starting transfers between devices: 14.8 us -> 16.1 us  [move(): return lax.ppermute(value, AXES, pairs)]
  transfers between devices with their start and end apart: 7 -> 7, of which waited for: 4 -> 3; matrix products, arithmetic and copies ran while one was open for 0% -> 0% of each run, Pallas kernels for 25% -> 17%
where the time goes in v2:
time: 49.4 us; the launch traced here: 49.1 us
  Pallas kernels  16.5 us (33%)
  starting transfers between devices  16.1 us (33%)
  waiting for transfers between devices  12.1 us (24%)
  local copies, waits for them, and re-layouts  2.44 us (5%)
  between operations  2.07 us (4%)
    ppermute x7, starting transfers between devices, move(): return lax.ppermute(value, AXES, pairs)  16.1 us
    ppermute x7, waiting for transfers between devices, move(): return lax.ppermute(value, AXES, pairs)  12.1 us
    pallas_call x1, Pallas kernels, step(): call(wave_kernel, (shape(2 * height + 8, frame), shape(2, height, frame))...  5.9 us
    pallas_call x1, Pallas kernels, step(): call(base_kernel, (shape(2, height, breadth), shape(2, height, breadth),...  5.03 us
    unnamed x10, local copies, waits for them, and re-layouts  2.44 us
    pallas_call x1, Pallas kernels, step(): call(final_kernel, (shape(2, height, breadth), shape(2, height, breadth))...  2.21 us
    pallas_call x1, Pallas kernels, step(): call(prepare_kernel, (shape(2 * modes, 2, frame, frame), shape(frame, fra...  2.18 us
  transfers between devices with their start and end apart: 7, of which 3 were waited for; matrix products, arithmetic and copies ran while one was open for 0% of the time, Pallas kernels for 17%

profile of v2, /device:TPU:9, one launch (start us, length us, event | category | flops | bytes accessed | tf_op | source)
XLA Modules:
  0.0 49.1 jit_solution(8692035539445918604)
XLA Ops:
  0.6 0.7 %collective-permute-start = (f32[2,2,256,256]{3,2,1,0:T(8,128)}, f32[2,2,256,256]{3,2,1,0:T(8,128)S(1)}, u32[]{:S(2)}, u32[]{:S(2)}) collective-permute-start(f32[2,2,256,256]{3,2,1,0:T(8,128)} %own_probe_ref.1), channel_id=1, source_target_pairs={{0,1},{1,0},{2,3},{3,2},{4,5},{5,4},{6,7},{7,6},{8,9},{9,8},{10,11... | collective-permute-start | bytes 3145736 | tf_op jit(solution)/shard_map/ppermute | solution.py:357
  1.4 3.1 %collective-permute-start.1 = (s32[1]{0:T(128)}, s32[1]{0:T(128)}, u32[]{:S(2)}, u32[]{:S(2)}) collective-permute-start(s32[1]{0:T(128)} %param.11), channel_id=1, source_target_pairs={{0,2},{2,4},{4,6},{6,8},{8,10},{10,12},{12,14},{14,16},{16,18},{18... | collective-permute-start | bytes 20 | tf_op jit(solution)/shard_map/ppermute | solution.py:357
  4.5 0.0 copy-start
  4.5 1.6 %copy-done = f32[2,128,2048]{2,1,0:T(8,128)S(1)} copy-done((f32[2,128,2048]{2,1,0:T(8,128)S(1)}, f32[2,128,2048]{2,1,0:T(8,128)}, u32[]{:S(2)}) %copy-start) | copy-done | bytes 2097176
  6.1 0.0 copy-start.4
  6.1 0.8 %copy-done.4 = s32[8192,2]{0,1:T(2,128)S(1)} copy-done((s32[8192,2]{0,1:T(2,128)S(1)}, s32[8192,2]{0,1:T(2,128)}, u32[]{:S(2)}) %copy-start.4) | copy-done | bytes 65560
  7.0 0.0 copy-start.1
  7.0 0.0 copy-start.3
  7.0 0.2 shard_map.86
  7.2 0.0 collective-permute-done.1.scan_ref.received_ref
  7.2 0.9 %shard_map.88 = f32[2,128,256]{2,1,0:T(8,128)S(1)} custom-call(s32[1]{0:T(128)} %collective-permute-done.1.scan_ref.received_ref, s32[2,8192]{1,0:T(2,128)S(1)} %get-tuple-element.19.table_ref, f32[2,128,2048]{2,1,0:T(8,128)S(1)} %get-tuple-element.20.object_ref), custom_call_target="tpu_custom_call" | custom-call | flops 5000000 | bytes 5000000 | tf_op jit(solution)/shard_map/pallas_call | solution.py:375
  8.2 3.0 %collective-permute-start.3 = (f32[2,128,256]{2,1,0:T(8,128)S(1)}, f32[2,128,256]{2,1,0:T(8,128)S(1)}, u32[]{:S(2)}, u32[]{:S(2)}) collective-permute-start(f32[2,128,256]{2,1,0:T(8,128)S(1)} %shard_map.88), channel_id=1, source_target_pairs={{2,0},{4,2},{6,4},{8,6},{10,8},{12,10},{14,12},{16,14},{18,16},{20... | collective-permute-start | bytes 786440 | tf_op jit(solution)/shard_map/ppermute | solution.py:357
  11.2 4.4 %collective-permute-done.3.received_ref = f32[2,128,256]{2,1,0:T(8,128)S(1)} collective-permute-done((f32[2,128,256]{2,1,0:T(8,128)S(1)}, f32[2,128,256]{2,1,0:T(8,128)S(1)}, u32[]{:S(2)}, u32[]{:S(2)}) %collective-permute-start.3) | collective-permute-done | bytes 262176 | tf_op jit(solution)/shard_map/ppermute | solution.py:357
  15.6 2.2 %collective-permute-start.4 = (f32[2,128,256]{2,1,0:T(8,128)S(1)}, f32[2,128,256]{2,1,0:T(8,128)S(1)}, u32[]{:S(2)}, u32[]{:S(2)}) collective-permute-start(f32[2,128,256]{2,1,0:T(8,128)S(1)} %collective-permute-done.3.received_ref), channel_id=1, source_target_pairs={{0,1},{1,0},{2,3},{3,2},{4,5},{5,4},{6,7},{7,6},{8,9},{9,8},{10,11... | collective-permute-start | bytes 786440 | tf_op jit(solution)/shard_map/ppermute | solution.py:357
  19.1 0.0 copy-start.2
  19.1 0.0 collective-permute-done.other_probe_ref
  19.1 0.0 copy-done.1
  19.1 0.0 copy-done.3
  19.2 2.2 %shard_map.87 = (f32[4,2,256,256]{3,2,1,0:T(8,128)S(1)}, f32[256,256]{1,0:T(8,128)S(1)}, f32[2,128,256]{2,1,0:T(8,128)S(1)}, f32[256,256]{1,0:T(8,128)S(1)}, f32[256,256]{1,0:T(8,128)S(1)}, /*index=5*/s32[4]{0:T(128)S(1)}) custom-call(s32[1]{0:T(128)S(6)} %copy.13.scan_ref, s32[1]{0:T(128)S(6)} %copy.14.count_ref, ...), custom_call_target="tpu_custom_call" | custom-call | flops 5000000 | bytes 5000000 | tf_op jit(solution)/shard_map/pallas_call | solution.py:380
  21.3 0.0 collective-permute-done.4.swapped_ref
  21.4 0.0 copy-done.2
  21.4 5.9 %shard_map.89 = (f32[264,256]{1,0:T(8,128)S(1)}, f32[2,128,256]{2,1,0:T(8,128)S(1)}) custom-call(s32[4]{0:T(128)S(1)} %get-tuple-element.21.place_ref, f32[2,128,256]{2,1,0:T(8,128)S(1)} %get-tuple-element.22.window_ref, f32[2,128,256]{2,1,0:T(8,128)S(1)} %collective-permute-done.3.received_ref, f32[2,128,256]{2,1,0:T(8,128)S(1)} %collective-permute-done.4.swapped_ref, ...), custom_call_target="tpu_custom_call" | custom-call | flops 5000000 | bytes 5000000 | tf_op jit(solution)/shard_map/pallas_call | solution.py:395
  27.3 2.7 %collective-permute-start.5 = (f32[264,256]{1,0:T(8,128)S(1)}, f32[264,256]{1,0:T(8,128)S(1)}, u32[]{:S(2)}, u32[]{:S(2)}) collective-permute-start(f32[264,256]{1,0:T(8,128)S(1)} %get-tuple-element.33), channel_id=1, source_target_pairs={{0,2},{2,4},{4,6},{6,8},{8,10},{10,12},{12,14},{14,16},{16,18},{18... | collective-permute-start | bytes 811016 | tf_op jit(solution)/shard_map/ppermute | solution.py:357
  29.9 6.3 %collective-permute-done.5.received_ref = f32[264,256]{1,0:T(8,128)S(1)} collective-permute-done((f32[264,256]{1,0:T(8,128)S(1)}, f32[264,256]{1,0:T(8,128)S(1)}, u32[]{:S(2)}, u32[]{:S(2)}) %collective-permute-start.5) | collective-permute-done | bytes 270368 | tf_op jit(solution)/shard_map/ppermute | solution.py:357
  36.2 4.3 %collective-permute-start.6 = (f32[264,256]{1,0:T(8,128)S(1)}, f32[264,256]{1,0:T(8,128)S(1)}, u32[]{:S(2)}, u32[]{:S(2)}) collective-permute-start(f32[264,256]{1,0:T(8,128)S(1)} %collective-permute-done.5.received_ref), channel_id=1, source_target_pairs={{0,1},{1,0},{2,3},{3,2},{4,5},{5,4},{6,7},{7,6},{8,9},{9,8},{10,11... | collective-permute-start | bytes 811016 | tf_op jit(solution)/shard_map/ppermute | solution.py:357
  40.5 0.0 collective-permute-start.2
  40.5 1.3 %collective-permute-done.2.swapped_ref = s32[1]{0:T(128)} collective-permute-done((s32[1]{0:T(128)}, s32[1]{0:T(128)}, u32[]{:S(2)}, u32[]{:S(2)}) %collective-permute-start.2) | collective-permute-done | bytes 36 | tf_op jit(solution)/shard_map/ppermute | solution.py:357
  41.9 5.0 %shard_map.90 = (f32[2,128,2048]{2,1,0:T(8,128)}, f32[2,128,2048]{2,1,0:T(8,128)}, f32[2,128,2048]{2,1,0:T(8,128)S(1)}, f32[128,2048]{1,0:T(8,128)S(1)}, f32[128...) custom-call(s32[4]{0:T(128)S(1)} %get-tuple-element.21.place_ref, ...), custom_call_target="tpu_custom_call" | custom-call | flops 5000000 | bytes 5000000 | tf_op jit(solution)/shard_map/pallas_call | solution.py:407
  46.9 0.0 collective-permute-done.6.swapped_ref
  46.9 2.2 %shard_map.91 = (f32[2,128,2048]{2,1,0:T(8,128)}, f32[2,128,2048]{2,1,0:T(8,128)}) custom-call(s32[4]{0:T(128)S(1)} %get-tuple-element.28.place_ref, f32[2,128,2048]{2,1,0:T(8,128)S(1)} %get-tuple-element.20.object_ref, f32[2,128,2048]{2,1,0:T(8,128)S(1)} %get-tuple-element.29.total_ref, ...), custom_call_target="tpu_custom_call", output_to_operand_aliasing={{0}: (8, {}), {1}: (9, {})} | custom-call | flops 5000000 | bytes 5000000 | tf_op jit(solution)/shard_map/pallas_call | solution.py:423
Async XLA Ops:
  0.6 18.5 %collective-permute-start = (f32[2,2,256,256]{3,2,1,0:T(8,128)}, f32[2,2,256,256]{3,2,1,0:T(8,128)S(1)}, u32[]{:S(2)}, u32[]{:S(2)}) collective-permute-start(f32[2,2,256,256]{3,2,1,0:T(8,128)} %own_probe_ref.1), channel_id=1, source_target_pairs={{0,1},{1,0},{2,3},{3,2},{4,5},{5,4},{6,7},{7,6},{8,9},{9,8},{10,11... | collective-permute-start | bytes 3145736 | tf_op jit(solution)/shard_map/ppermute | solution.py:357
  1.4 5.8 %collective-permute-start.1 = (s32[1]{0:T(128)}, s32[1]{0:T(128)}, u32[]{:S(2)}, u32[]{:S(2)}) collective-permute-start(s32[1]{0:T(128)} %param.11), channel_id=1, source_target_pairs={{0,2},{2,4},{4,6},{6,8},{8,10},{10,12},{12,14},{14,16},{16,18},{18... | collective-permute-start | bytes 20 | tf_op jit(solution)/shard_map/ppermute | solution.py:357
  4.5 1.6 %copy-start = (f32[2,128,2048]{2,1,0:T(8,128)S(1)}, f32[2,128,2048]{2,1,0:T(8,128)}, u32[]{:S(2)}) copy-start(f32[2,128,2048]{2,1,0:T(8,128)} %object_ref.1) | copy-start | bytes 6291460
  6.1 0.8 %copy-start.4 = (s32[8192,2]{0,1:T(2,128)S(1)}, s32[8192,2]{0,1:T(2,128)}, u32[]{:S(2)}) copy-start(s32[8192,2]{0,1:T(2,128)} %param.10) | copy-start | bytes 196612
  7.0 12.2 %copy-start.1 = (f32[2,2,256,256]{3,2,1,0:T(8,128)S(1)}, f32[2,2,256,256]{3,2,1,0:T(8,128)}, u32[]{:S(2)}) copy-start(f32[2,2,256,256]{3,2,1,0:T(8,128)} %own_probe_ref.1) | copy-start | bytes 3145732
  7.0 12.2 %copy-start.3 = (f32[1,256,256]{2,1,0:T(8,128)S(1)}, f32[1,256,256]{2,1,0:T(8,128)}, u32[]{:S(2)}) copy-start(f32[1,256,256]{2,1,0:T(8,128)} %amplitude_ref.1) | copy-start | bytes 786436
  8.2 7.5 %collective-permute-start.3 = (f32[2,128,256]{2,1,0:T(8,128)S(1)}, f32[2,128,256]{2,1,0:T(8,128)S(1)}, u32[]{:S(2)}, u32[]{:S(2)}) collective-permute-start(f32[2,128,256]{2,1,0:T(8,128)S(1)} %shard_map.88), channel_id=1, source_target_pairs={{2,0},{4,2},{6,4},{8,6},{10,8},{12,10},{14,12},{16,14},{18,16},{20... | collective-permute-start | bytes 786440 | tf_op jit(solution)/shard_map/ppermute | solution.py:357
  15.6 5.7 %collective-permute-start.4 = (f32[2,128,256]{2,1,0:T(8,128)S(1)}, f32[2,128,256]{2,1,0:T(8,128)S(1)}, u32[]{:S(2)}, u32[]{:S(2)}) collective-permute-start(f32[2,128,256]{2,1,0:T(8,128)S(1)} %collective-permute-done.3.received_ref), channel_id=1, source_target_pairs={{0,1},{1,0},{2,3},{3,2},{4,5},{5,4},{6,7},{7,6},{8,9},{9,8},{10,11... | collective-permute-start | bytes 786440 | tf_op jit(solution)/shard_map/ppermute | solution.py:357
  19.1 2.2 %copy-start.2 = (bf16[8,256,256]{2,1,0:T(8,128)(2,1)S(1)}, bf16[8,256,256]{2,1,0:T(8,128)(2,1)}, u32[]{:S(2)}) copy-start(bf16[8,256,256]{2,1,0:T(8,128)(2,1)} %constant.2.clone.matrix_ref) | copy-start | bytes 3145732
  27.3 8.9 %collective-permute-start.5 = (f32[264,256]{1,0:T(8,128)S(1)}, f32[264,256]{1,0:T(8,128)S(1)}, u32[]{:S(2)}, u32[]{:S(2)}) collective-permute-start(f32[264,256]{1,0:T(8,128)S(1)} %get-tuple-element.33), channel_id=1, source_target_pairs={{0,2},{2,4},{4,6},{6,8},{8,10},{10,12},{12,14},{14,16},{16,18},{18... | collective-permute-start | bytes 811016 | tf_op jit(solution)/shard_map/ppermute | solution.py:357
  36.2 10.7 %collective-permute-start.6 = (f32[264,256]{1,0:T(8,128)S(1)}, f32[264,256]{1,0:T(8,128)S(1)}, u32[]{:S(2)}, u32[]{:S(2)}) collective-permute-start(f32[264,256]{1,0:T(8,128)S(1)} %collective-permute-done.5.received_ref), channel_id=1, source_target_pairs={{0,1},{1,0},{2,3},{3,2},{4,5},{5,4},{6,7},{7,6},{8,9},{9,8},{10,11... | collective-permute-start | bytes 811016 | tf_op jit(solution)/shard_map/ppermute | solution.py:357
  40.5 1.4 %collective-permute-start.2 = (s32[1]{0:T(128)}, s32[1]{0:T(128)}, u32[]{:S(2)}, u32[]{:S(2)}) collective-permute-start(s32[1]{0:T(128)} %collective-permute-done.1.scan_ref.received_ref), channel_id=1, source_target_pairs={{0,1},{1,0},{2,3},{3,2},{4,5},{5,4},{6,7},{7,6},{8,9},{9,8},{10,11... | collective-permute-start | bytes 20 | tf_op jit(solution)/shard_map/ppermute | solution.py:357

commit v3 on v2

v3 whole, which is shorter than its diff:
```python
import math

import jax
import jax.numpy as jnp
import numpy as np
from jax import lax
from jax.experimental import pallas as pl
from jax.experimental.pallas import tpu as pltpu
from jax.sharding import PartitionSpec as P


FLOOR = 0.25
ALPHA = 0.5
LANES = 128
AXES = ("tile", "mode")
VMEM = pltpu.VMEM
SMEM = pltpu.SMEM


def split(value):
    high = value.astype(jnp.bfloat16)
    low = (value - high.astype(jnp.float32)).astype(jnp.bfloat16)
    return high, low


def matrices(frame):
    half = frame // 2
    pixel = np.arange(half)[:, None]
    wave = np.arange(half)[None, :]
    blocks = []
    for parity in (0, 1):
        phase = 2.0 * math.pi * (pixel * (2 * wave + parity) % frame) / frame
        cos, sin = np.cos(phase) / math.sqrt(frame), np.sin(phase) / math.sqrt(frame)
        forward = np.block([[cos, -sin], [sin, cos]])
        for table in (forward, forward.T):
            high = table.astype(jnp.bfloat16)
            blocks.append(high)
            blocks.append((table - high.astype(np.float64)).astype(jnp.bfloat16))
    return np.stack(blocks)


def lookup(table_ref, scan):
    base = pl.multiple_of((scan // LANES) * LANES, LANES)
    chunk = table_ref[:, pl.ds(base, LANES)].astype(jnp.float32)
    lane = lax.broadcasted_iota(jnp.int32, chunk.shape, 1)
    picked = jnp.where(lane == scan - base, chunk, 0.0)
    row = jnp.sum(picked[0:1]).astype(jnp.int32)
    col = jnp.sum(picked[1:2]).astype(jnp.int32)
    return row, col


def strip_window(object_ref, col):
    blocks = object_ref.shape[2] // LANES
    block, shift = col // LANES, col % LANES
    first = object_ref[:, :, pl.ds(pl.multiple_of(block * LANES, LANES), LANES)]
    second = object_ref[:, :, pl.ds(pl.multiple_of((block + 1) * LANES, LANES), LANES)]
    last = jnp.minimum(block + 2, blocks - 1)
    third = object_ref[:, :, pl.ds(pl.multiple_of(last * LANES, LANES), LANES)]
    lane = lax.broadcasted_iota(jnp.int32, first.shape, 2)
    return jnp.where(lane < shift, third, first), second


def stage_kernel(table_ref, held_ref, sem):
    copy = pltpu.make_async_copy(table_ref, held_ref, sem)
    copy.start()
    copy.wait()


def load_kernel(probe_ref, matrix_ref, held_probe_ref, held_matrix_ref, sems):
    for copy in fetch([(probe_ref, held_probe_ref), (matrix_ref, held_matrix_ref)], sems):
        copy.wait()


def fetch(pairs, sems, first=0):
    copies = [pltpu.make_async_copy(a, b, sems.at[first + index]) for index, (a, b) in enumerate(pairs)]
    for copy in copies:
        copy.start()
    return copies


def select_kernel(own_scan_ref, scan_ref, table_ref, object_ref, out_ref, own_ref, got_ref, third_ref, sems):
    odd = lax.axis_index("tile") % 2 == 1
    for copy in fetch([(own_scan_ref, own_ref), (scan_ref, got_ref)], sems):
        copy.wait()
    scan = jnp.where(odd & (lax.axis_index("mode") == 1), own_ref[0], got_ref[0])
    _, col = lookup(table_ref, scan)
    blocks = object_ref.shape[2] // LANES
    block, shift = col // LANES, col % LANES
    last = jnp.minimum(block + 2, blocks - 1)
    pairs = [
        (object_ref.at[:, :, pl.ds(pl.multiple_of(block * LANES, LANES), 2 * LANES)], out_ref),
        (object_ref.at[:, :, pl.ds(pl.multiple_of(last * LANES, LANES), LANES)], third_ref),
    ]
    for copy in fetch(pairs, sems, 2):
        copy.wait()
    lane = lax.broadcasted_iota(jnp.int32, third_ref.shape, 2)
    out_ref[:, :, :LANES] = jnp.where(lane < shift, third_ref[...], out_ref[:, :, :LANES])


def slots(own_ref, received_ref, swapped_ref):
    first = lax.axis_index("mode") == 0
    odd = lax.axis_index("tile") % 2 == 1
    own, got, other = own_ref[0], received_ref[0], swapped_ref[0]
    above = jnp.where(first, got, other)
    further = jnp.where(first, other, got)
    return jnp.where(odd, further, own), above, jnp.where(odd, own, further)


def within(table_ref, scan, strip, height):
    row, col = lookup(table_ref, scan)
    return jnp.clip(row - strip * height, 0, height - 1), col


def roll_into(out_ref, value, row, col, tall_ref):
    frame = value.shape[0]
    half = frame // 2
    turned = pltpu.roll(value, col, 1)
    for index in range(frame // LANES):
        at = slice(index * LANES, (index + 1) * LANES)
        tall_ref[index, :half] = turned[half:, at]
        tall_ref[index, half:] = turned[:, at]
        out_ref[:, at] = tall_ref[index, pl.ds(half - row, frame), :]


def reorder_kernel(own_ref, received_ref, swapped_ref, factor_ref, rows_ref):
    frame = own_ref.shape[1]
    odd = lax.axis_index("tile") % 2 == 1
    moved = jnp.where(lax.axis_index("mode") == 0, received_ref[0], swapped_ref[0])
    value = jnp.where(odd, moved, own_ref[0])
    source = lax.broadcasted_iota(jnp.int32, (frame, frame), 0)
    target = lax.broadcasted_iota(jnp.int32, (frame, frame), 1)
    half = frame // 2
    order = jnp.where(target < half, 2 * target, 2 * target - frame + 1)
    pick = jnp.where(source == order, 1.0, 0.0).astype(jnp.bfloat16)
    high = value.astype(jnp.bfloat16)
    rest = value - high.astype(jnp.float32)
    middle = rest.astype(jnp.bfloat16)
    low = (rest - middle.astype(jnp.float32)).astype(jnp.bfloat16)
    columns = jnp.dot(high, pick, preferred_element_type=jnp.float32)
    columns = columns + jnp.dot(middle, pick, preferred_element_type=jnp.float32)
    columns = columns + jnp.dot(low, pick, preferred_element_type=jnp.float32)
    for index in range(frame // LANES):
        at = slice(index * LANES, (index + 1) * LANES)
        rows_ref[index] = columns[:, at]
        factor_ref[:half, at] = rows_ref[index, pl.ds(0, half, stride=2), :]
        factor_ref[half:, at] = rows_ref[index, pl.ds(1, half, stride=2), :]


def prepare_kernel(
    scan_ref, received_ref, swapped_ref, count_ref, table_ref, object_ref, own_probe_ref, other_probe_ref, matrix_ref,
    gradient_ref, probe_ref, window_ref, light_ref, total_ref, strip_ref, place_ref,
    zero_ref, tall_ref, own_ref, got_ref, other_ref, live_ref, sems,
):
    pairs = [(scan_ref, own_ref), (received_ref, got_ref), (swapped_ref, other_ref), (count_ref, live_ref)]
    scalars = fetch(pairs, sems)
    zero_ref[...] = jnp.zeros_like(zero_ref)
    step = zero_ref.shape[0]
    copies = []
    for part in range(2):
        for at in range(0, object_ref.shape[1], step):
            copies += fetch([(zero_ref, gradient_ref.at[part, at : at + step])], sems, len(pairs) + len(copies))
    for copy in scalars:
        copy.wait()
    modes = own_probe_ref.shape[0]
    height = object_ref.shape[1]
    frame = own_probe_ref.shape[2]
    tile = lax.axis_index("tile")
    odd = tile % 2
    scan, _, _ = slots(own_ref, got_ref, other_ref)
    row, col = within(table_ref, scan, tile - 2 * odd, height)
    shift = col % LANES
    total = jnp.zeros((frame, frame), jnp.float32)
    for index in range(2 * modes):
        source = own_probe_ref if index < modes else other_probe_ref
        for part in range(2):
            value = source[index % modes, part]
            total = total + value * value
            roll_into(probe_ref.at[index, part], value, row, shift, tall_ref.at[index, part])
    total_ref[...] = total
    roll_into(light_ref, total, row, shift, tall_ref.at[0, 0])
    low, high = strip_window(object_ref, col)
    window_ref[:, :, :LANES] = low
    window_ref[:, :, LANES:] = high
    place_ref[0] = row
    place_ref[1] = col
    place_ref[2] = jnp.where(odd == 1, (tile >= 2).astype(jnp.int32), live_ref[0])
    place_ref[3] = jnp.where(odd == 1, 0, row)
    place_ref[4] = jnp.where(odd == 1, row, height)
    for index in range(5, 8):
        place_ref[index] = 0
    transform_rows(probe_ref, 0, window_ref, matrix_ref, strip_ref)
    for copy in copies:
        copy.wait()


def right(value, high, low):
    first, second = split(value)
    return jnp.dot(
        jnp.concatenate([first, second, first], axis=1),
        jnp.concatenate([high, high, low], axis=0),
        preferred_element_type=jnp.float32,
    )


def left(high, low, value):
    first, second = split(value)
    return jnp.dot(
        jnp.concatenate([high, high, low], axis=1),
        jnp.concatenate([first, second, first], axis=0),
        preferred_element_type=jnp.float32,
    )


def transform_rows(probe_ref, start, window_ref, matrix_ref, out_ref):
    modes = probe_ref.shape[0]
    height, frame = window_ref.shape[1:]
    half = frame // 2
    sums, differences = [], []
    for mode in range(modes):
        probe_re = probe_ref[mode, 0, pl.ds(start, height), :]
        probe_im = probe_ref[mode, 1, pl.ds(start, height), :]
        wave_re = probe_re * window_ref[0] - probe_im * window_ref[1]
        wave_im = probe_re * window_ref[1] + probe_im * window_ref[0]
        for pieces, sign in ((sums, 1.0), (differences, -1.0)):
            pieces.append(
                jnp.concatenate(
                    [wave_re[:, :half] + sign * wave_re[:, half:], wave_im[:, :half] + sign * wave_im[:, half:]],
                    axis=1,
                )
            )
    even = right(jnp.concatenate(sums, axis=0), matrix_ref[0], matrix_ref[1])
    odd = right(jnp.concatenate(differences, axis=0), matrix_ref[4], matrix_ref[5])
    for mode in range(modes):
        at = slice(mode * height, (mode + 1) * height)
        out_ref[mode, 0] = jnp.concatenate([even[at, :half], odd[at, :half]], axis=1)
        out_ref[mode, 1] = jnp.concatenate([even[at, half:], odd[at, half:]], axis=1)


def strip_kernel(received_ref, probe_ref, matrix_ref, out_ref):
    height = received_ref.shape[1]
    start = pl.multiple_of((1 - lax.axis_index("mode")) * height, height)
    transform_rows(probe_ref, start, received_ref, matrix_ref, out_ref)


def wave_kernel(
    place_ref, window_ref, received_ref, swapped_ref, own_ref, first_ref, probe_ref, amplitude_ref, light_ref,
    matrix_ref, send_ref, keep_ref, patch_ref, far_ref, second_ref,
):
    modes, _, frame, _ = probe_ref.shape
    height = window_ref.shape[1]
    half = frame // 2
    core = lax.axis_index("mode")
    low, high = place_ref[3], place_ref[4]
    transform_rows(probe_ref, pl.multiple_of(core * height, height), swapped_ref, matrix_ref, second_ref)
    level = lax.broadcasted_iota(jnp.int32, (height, frame), 0)

    def assemble(own, got, given):
        nearer = jnp.where(core == 0, got, given)
        farther = jnp.where(core == 0, given, got)
        return jnp.where((level >= low) & (level < high), own, farther), nearer

    for part in range(2):
        top, bottom = assemble(window_ref[part], received_ref[part], swapped_ref[part])
        patch_ref[part, :height] = top
        patch_ref[part, height:] = bottom
    intensity = jnp.zeros((frame, frame), jnp.float32)
    for mode in range(modes):
        top_re, bottom_re = assemble(own_ref[mode, 0], first_ref[mode, 0], second_ref[mode, 0])
        top_im, bottom_im = assemble(own_ref[mode, 1], first_ref[mode, 1], second_ref[mode, 1])
        added = jnp.concatenate([top_re + bottom_re, top_im + bottom_im], axis=0)
        taken = jnp.concatenate([top_re - bottom_re, top_im - bottom_im], axis=0)
        even = left(matrix_ref[2], matrix_ref[3], added)
        odd = left(matrix_ref[6], matrix_ref[7], taken)
        far_ref[mode, 0] = even
        far_ref[mode, 1] = odd
        squares = jnp.concatenate(
            [even[:half] * even[:half] + even[half:] * even[half:], odd[:half] * odd[:half] + odd[half:] * odd[half:]],
            axis=0,
        )
        intensity = intensity + squares
    factor = amplitude_ref[...] * lax.rsqrt(jnp.maximum(intensity, FLOOR))
    grad_re = jnp.zeros((frame, frame), jnp.float32)
    grad_im = jnp.zeros((frame, frame), jnp.float32)
    even_factor = jnp.concatenate([factor[:half], factor[:half]], axis=0)
    odd_factor = jnp.concatenate([factor[half:], factor[half:]], axis=0)
    evens, odds = [], []
    for mode in range(modes):
        even = left(matrix_ref[0], matrix_ref[1], far_ref[mode, 0] * even_factor)
        odd = left(matrix_ref[4], matrix_ref[5], far_ref[mode, 1] * odd_factor)
        top, bottom = even + odd, even - odd
        mid_re = jnp.concatenate([top[:half], bottom[:half]], axis=0)
        mid_im = jnp.concatenate([top[half:], bottom[half:]], axis=0)
        evens.append(jnp.concatenate([mid_re[:, :half], mid_im[:, :half]], axis=1))
        odds.append(jnp.concatenate([mid_re[:, half:], mid_im[:, half:]], axis=1))
    even = right(jnp.concatenate(evens, axis=0), matrix_ref[2], matrix_ref[3])
    odd = right(jnp.concatenate(odds, axis=0), matrix_ref[6], matrix_ref[7])
    fores, afts = even + odd, even - odd
    for mode in range(modes):
        fore = fores[mode * frame : (mode + 1) * frame]
        aft = afts[mode * frame : (mode + 1) * frame]
        back_re = jnp.concatenate([fore[:, :half], aft[:, :half]], axis=1)
        back_im = jnp.concatenate([fore[:, half:], aft[:, half:]], axis=1)
        probe_re, probe_im = probe_ref[mode, 0], probe_ref[mode, 1]
        grad_re = grad_re + (probe_re * back_re + probe_im * back_im)
        grad_im = grad_im + (probe_re * back_im - probe_im * back_re)
    live = (place_ref[2] > 0).astype(jnp.float32)
    grad_re = (grad_re - light_ref[...] * patch_ref[0]) * live
    grad_im = (grad_im - light_ref[...] * patch_ref[1]) * live
    send_ref[:height] = jnp.where(core == 0, grad_re[height:], grad_re[:height])
    send_ref[height : 2 * height] = jnp.where(core == 0, grad_im[height:], grad_im[:height])
    send_ref[2 * height :] = jnp.full((8, frame), live, jnp.float32)
    keep_ref[0] = grad_re[:height]
    keep_ref[1] = grad_im[:height]


def covers(col, block, low, high, lane):
    start, shift = col // LANES, col % LANES
    distance = block - start
    value = jnp.where(distance == 1, high, low)
    first = jnp.where(distance == 0, shift, jnp.where(distance == 1, 0, LANES))
    last = jnp.where(distance == 2, shift, 0)
    keep = (lane >= first) | (lane < last)
    return jnp.where(keep, value, 0.0)


def base_kernel(
    place_ref, scan_ref, received_ref, swapped_ref, table_ref, object_ref, keep_ref, light_ref, plain_ref,
    old_gradient_ref,
    updated_ref, gradient_ref, total_ref, weight_ref, first_ref, second_ref, others_ref, new_ref, tall_ref, turned_ref,
    own_ref, got_ref, other_ref, sems, fills,
):
    del old_gradient_ref
    height, breadth = object_ref.shape[1:]
    tile = lax.axis_index("tile")
    core = lax.axis_index("mode")
    col = place_ref[1]
    fill = pltpu.make_async_copy(object_ref, updated_ref, fills.at[0])
    fill.start()
    scalars = fetch([(scan_ref, own_ref), (received_ref, got_ref), (swapped_ref, other_ref)], fills, 1)
    live = (place_ref[2] > 0).astype(jnp.float32)
    total_ref[...] = jnp.zeros_like(total_ref)
    weight_ref[...] = jnp.zeros_like(weight_ref)
    lane = lax.broadcasted_iota(jnp.int32, (height, LANES), 1)
    level = lax.broadcasted_iota(jnp.int32, (height, LANES), 0)
    kept = (level >= place_ref[3]) & (level < place_ref[4])
    for slot in range(3):
        block = jnp.minimum(col // LANES + slot, breadth // LANES - 1)
        at = pl.ds(pl.multiple_of(block * LANES, LANES), LANES)
        light = covers(col, block, light_ref[:height, :LANES], light_ref[:height, LANES:], lane)
        weight = jnp.where(kept, light * live, 0.0)
        weight_ref[:, at] = weight
        scale = 1.0 / (weight + ALPHA)
        for part in range(2):
            change = covers(col, block, keep_ref[part, :, :LANES], keep_ref[part, :, LANES:], lane)
            change = jnp.where(kept, change, 0.0)
            total_ref[part, :, at] = change
            new_ref[slot, part] = object_ref[part, :, at] + change * scale
    odd = tile % 2
    for copy in scalars:
        copy.wait()
    _, above, third = slots(own_ref, got_ref, other_ref)
    places = []
    for scan, strip, far in ((above, tile - 1, False), (third, tile - 2 + 2 * odd, True)):
        row, start = within(table_ref, scan, strip, height)
        index = int(far)
        roll_into(turned_ref.at[index], plain_ref[...], row, start % LANES, tall_ref.at[index])
        turned = turned_ref[index]
        begin = jnp.where(odd == 1, row, 0) if far else 0
        end = jnp.where(odd == 1, height, row) if far else height
        places.append((start, begin, end, turned[:height] if far else turned[height:]))
    for slot, out_ref in ((0, first_ref), (1, second_ref)):
        direct = core == slot
        near, far = places
        out_ref[...] = jnp.where(direct, near[3], far[3])
        for index in range(3):
            others_ref[4 * slot + index] = jnp.where(direct, near[index], far[index])
        others_ref[4 * slot + 3] = 0
    fill.wait()
    copies = []
    for slot in range(3):
        block = jnp.minimum(col // LANES + slot, breadth // LANES - 1)
        at = pl.ds(pl.multiple_of(block * LANES, LANES), LANES)
        copies.append(write(slot, col, block, at, total_ref.at[:, :, at], new_ref, gradient_ref, updated_ref, sems))
    finish(copies)


def write(slot, col, block, at, source, new_ref, gradient_ref, updated_ref, sems):
    fresh = col // LANES + slot == block
    one = pltpu.make_async_copy(source, gradient_ref.at[:, :, at], sems.at[2 * slot])
    two = pltpu.make_async_copy(new_ref.at[slot], updated_ref.at[:, :, at], sems.at[2 * slot + 1])

    @pl.when(fresh)
    def _():
        one.start()
        two.start()

    return fresh, one, two


def finish(copies):
    for fresh, one, two in copies:

        @pl.when(fresh)
        def _(one=one, two=two):
            one.wait()
            two.wait()


def add_windows(windows, main, object_ref, total_ref, weight_ref, updated_ref, gradient_ref, new_ref, sum_ref, sems):
    height, breadth = object_ref.shape[1:]
    lane = lax.broadcasted_iota(jnp.int32, (height, LANES), 1)
    level = lax.broadcasted_iota(jnp.int32, (height, LANES), 0)
    col = windows[main][0]
    copies = []
    for slot in range(3):
        block = jnp.minimum(col // LANES + slot, breadth // LANES - 1)
        at = pl.ds(pl.multiple_of(block * LANES, LANES), LANES)
        weight = weight_ref[:, at]
        sums = [total_ref[0, :, at], total_ref[1, :, at]]
        for start, begin, end, light_ref, change_ref in windows:
            inside = (level >= begin) & (level < end)
            live = change_ref[2 * height : 2 * height + 1, :1]
            light = covers(start, block, light_ref[:, :LANES], light_ref[:, LANES:], lane)
            weight = weight + jnp.where(inside, light, 0.0) * live
            for part in range(2):
                rows = slice(part * height, (part + 1) * height)
                change = covers(start, block, change_ref[rows, :LANES], change_ref[rows, LANES:], lane)
                sums[part] = sums[part] + jnp.where(inside, change, 0.0)
        scale = 1.0 / (weight + ALPHA)
        for part in range(2):
            sum_ref[slot, part] = sums[part]
            new_ref[slot, part] = object_ref[part, :, at] + sums[part] * scale
        copies.append(write(slot, col, block, at, sum_ref.at[slot], new_ref, gradient_ref, updated_ref, sems))
    finish(copies)


def first_kernel(
    others_ref, object_ref, total_ref, weight_ref, first_ref, received_ref, old_updated_ref, old_gradient_ref,
    updated_ref, gradient_ref, new_ref, sum_ref, sems,
):
    del old_updated_ref, old_gradient_ref
    windows = [(others_ref[0], others_ref[1], others_ref[2], first_ref, received_ref)]
    add_windows(windows, 0, object_ref, total_ref, weight_ref, updated_ref, gradient_ref, new_ref, sum_ref, sems)


def second_kernel(
    others_ref, object_ref, total_ref, weight_ref, first_ref, second_ref, received_ref, swapped_ref,
    old_updated_ref, old_gradient_ref, updated_ref, gradient_ref, new_ref, sum_ref, sems,
):
    del old_updated_ref, old_gradient_ref
    windows = [
        (others_ref[0], others_ref[1], others_ref[2], first_ref, received_ref),
        (others_ref[4], others_ref[5], others_ref[6], second_ref, swapped_ref),
    ]
    add_windows(windows, 1, object_ref, total_ref, weight_ref, updated_ref, gradient_ref, new_ref, sum_ref, sems)


def call(kernel, out_shape, in_specs, out_specs, scratch=(), mebibytes=16, aliases=None):
    return pl.pallas_call(
        kernel,
        out_shape=out_shape,
        in_specs=in_specs,
        out_specs=out_specs,
        scratch_shapes=list(scratch),
        input_output_aliases=aliases or {},
        compiler_params=pltpu.CompilerParams(vmem_limit_bytes=mebibytes << 20),
        cost_estimate=pl.CostEstimate(flops=5000000, bytes_accessed=5000000, transcendentals=0),
    )


def in_hbm(value):
    return pltpu.with_memory_space_constraint(value, pltpu.HBM)


def space(where):
    return pl.BlockSpec(memory_space=where)


def shape(*dims, dtype=jnp.float32):
    return jax.ShapeDtypeStruct(dims, dtype)


def solution(mesh):
    tiles, cores = mesh.shape["tile"], mesh.shape["mode"]
    up = [(2 * t, 2 * (t + 1)) for t in range(tiles - 1)] + [(2 * t + 1, 2 * (t + 2) + 1) for t in range(tiles - 2)]
    gather = [(2 * t, 2 * (t ^ 1)) for t in range(tiles)]
    gather += [(2 * t + 1, 2 * (t - 2) + 1) for t in range(2, tiles, 2)]
    gather += [(2 * t + 1, 2 * (t + 2) + 1) for t in range(1, tiles - 2, 2)]
    spread = [(target, source) for source, target in gather]
    onward = [(2 * t, 2 * (t + 2)) for t in range(1, tiles - 2, 2)]
    swap = [(2 * t + core, 2 * t + 1 - core) for t in range(tiles) for core in range(2)]
    assert cores == 2 and tiles % 2 == 0

    def move(value, pairs):
        return lax.ppermute(value, AXES, pairs)

    def step(object_tiles, probe_modes, amplitudes, scan_offsets, slot_scan, slot_count):
        height, breadth = object_tiles.shape[1:]
        modes, _, frame, _ = probe_modes.shape
        assert slot_scan.shape[0] == 1 and frame == 2 * height and height == LANES
        table = scan_offsets.T
        matrix = jnp.asarray(matrices(frame))
        received_scan = move(slot_scan, up)
        other_probe = move(probe_modes, swap)
        received_amplitude = move(amplitudes, onward)
        scalar = pltpu.SMEM((1,), jnp.int32)
        staged = object_tiles
        table = call(
            stage_kernel,
            shape(*table.shape, dtype=jnp.int32),
            [space(pltpu.HBM)],
            space(VMEM),
            [pltpu.SemaphoreType.DMA],
            mebibytes=8,
        )(in_hbm(table))
        window = call(
            select_kernel,
            shape(2, height, frame),
            [space(pl.ANY)] * 2 + [space(VMEM), space(pl.ANY)],
            space(VMEM),
            [scalar, scalar, pltpu.VMEM((2, height, LANES), jnp.float32), pltpu.SemaphoreType.DMA((4,))],
        )(slot_scan, received_scan, table, in_hbm(object_tiles))
        received = move(window, gather)
        swapped_scan = move(received_scan, swap)
        swapped_amplitude = move(received_amplitude, swap)
        own_probe, matrix = call(
            load_kernel,
            (shape(*probe_modes.shape), shape(*matrix.shape, dtype=matrix.dtype)),
            [space(pltpu.HBM)] * 2,
            [space(VMEM)] * 2,
            [pltpu.SemaphoreType.DMA((2,))],
            mebibytes=8,
        )(in_hbm(probe_modes), in_hbm(matrix))
        strip = shape(2 * modes, 2, height, frame)
        whole = shape(2, height, breadth)
        gradient, probe, own_window, light, plain, own_strip, place = call(
            prepare_kernel,
            (
                whole,
                shape(2 * modes, 2, frame, frame),
                shape(2, height, frame),
                shape(frame, frame),
                shape(frame, frame),
                strip,
                shape(8, dtype=jnp.int32),
            ),
            [space(pl.ANY)] * 4 + [space(VMEM)] * 5,
            [space(pl.ANY)] + [space(VMEM)] * 5 + [space(SMEM)],
            [
                pltpu.VMEM((height // 8, breadth), jnp.float32),
                pltpu.VMEM((2 * modes, 2, frame // LANES, frame + height, LANES), jnp.float32),
                scalar,
                scalar,
                scalar,
                scalar,
                pltpu.SemaphoreType.DMA((20,)),
            ],
        )(slot_scan, received_scan, swapped_scan, slot_count, table, staged, own_probe, other_probe, matrix)
        swapped = move(received, swap)
        amplitude = call(
            reorder_kernel,
            shape(frame, frame),
            [space(VMEM)] * 3,
            space(VMEM),
            [pltpu.VMEM((frame // LANES, frame, LANES), jnp.float32)],
        )(amplitudes, received_amplitude, swapped_amplitude)
        first_strip = call(strip_kernel, strip, [space(VMEM)] * 3, space(VMEM))(received, probe, matrix)
        send, keep = call(
            wave_kernel,
            (shape(2 * height + 8, frame), shape(2, height, frame)),
            [space(SMEM)] + [space(VMEM)] * 9,
            [space(VMEM)] * 2,
            [
                pltpu.VMEM((2, frame, frame), jnp.float32),
                pltpu.VMEM((2 * modes, 2, frame, frame), jnp.float32),
                pltpu.VMEM((2 * modes, 2, height, frame), jnp.float32),
            ],
            mebibytes=24,
        )(place, own_window, received, swapped, own_strip, first_strip, probe, amplitude, light, matrix)
        received_change = move(send, spread)
        blocks = pltpu.VMEM((3, 2, height, LANES), jnp.float32)
        semaphores = pltpu.SemaphoreType.DMA((6,))
        updated, gradient, total, weight, first, second, others = call(
            base_kernel,
            (
                whole,
                whole,
                whole,
                shape(height, breadth),
                shape(height, frame),
                shape(height, frame),
                shape(8, dtype=jnp.int32),
            ),
            [space(SMEM)] + [space(pl.ANY)] * 3 + [space(VMEM)] * 5 + [space(pl.ANY)],
            [space(pl.ANY)] * 2 + [space(VMEM)] * 4 + [space(SMEM)],
            [
                blocks,
                pltpu.VMEM((2, frame // LANES, frame + height, LANES), jnp.float32),
                pltpu.VMEM((2, frame, frame), jnp.float32),
                scalar,
                scalar,
                scalar,
                semaphores,
                pltpu.SemaphoreType.DMA((4,)),
            ],
            aliases={9: 1},
        )(place, slot_scan, received_scan, swapped_scan, table, staged, keep, light, plain, gradient)
        swapped_change = move(received_change, swap)
        updated, gradient = call(
            first_kernel,
            (whole, whole),
            [space(SMEM)] + [space(VMEM)] * 5 + [space(pl.ANY)] * 2,
            [space(pl.ANY)] * 2,
            [blocks, blocks, semaphores],
            aliases={6: 0, 7: 1},
        )(others, staged, total, weight, first, received_change, updated, gradient)
        return call(
            second_kernel,
            (whole, whole),
            [space(SMEM)] + [space(VMEM)] * 7 + [space(pl.ANY)] * 2,
            [space(pl.ANY)] * 2,
            [blocks, blocks, semaphores],
            aliases={8: 0, 9: 1},
        )(others, staged, total, weight, first, second, received_change, swapped_change, updated, gradient)

    return jax.shard_map(
        step,
        mesh=mesh,
        in_specs=(
            P(None, "tile", None),
            P("mode", None, None, None),
            P("tile", None, None),
            P(),
            P("tile"),
            P("tile"),
        ),
        out_specs=(P(None, "tile", None), P(None, "tile", None)),
        check_vma=False,
    )
```

time: 49.4 us -> 52.5 us (1.063)
  Pallas kernels: 16.5 us -> 22.6 us
  waiting for transfers between devices: 12.1 us -> 8.72 us
  starting transfers between devices: 16.1 us -> 18.7 us
  local copies, waits for them, and re-layouts: 2.44 us -> 0.01 us
    pallas_call x5 -> x9, Pallas kernels: 10.6 us -> 18 us  [the longest x1 4.66 us: step(): call(base_kernel, (whole, whole, whole, shape(height, breadth), shape(hei...]
    ppermute x7 -> x9, waiting for transfers between devices: 12.1 us -> 8.72 us  [move(): return lax.ppermute(value, AXES, pairs)]
    ppermute x7 -> x9, starting transfers between devices: 16.1 us -> 18.7 us  [move(): return lax.ppermute(value, AXES, pairs)]
    unnamed x10 -> x4, local copies, waits for them, and re-layouts: 2.44 us -> 0.01 us
    pallas_call x1, Pallas kernels: 5.9 us -> 4.53 us  [step(): call(wave_kernel, (shape(2 * height + 8, frame), shape(2, height, frame))...]
  transfers between devices with their start and end apart: 7 -> 9, of which waited for: 3 -> 4; matrix products, arithmetic and copies ran while one was open for 0% -> 0% of each run, Pallas kernels for 17% -> 31%
where the time goes in v3:
time: 52.5 us; the launch traced here: 52.2 us
  Pallas kernels  22.6 us (43%)
  starting transfers between devices  18.7 us (36%)
  waiting for transfers between devices  8.72 us (17%)
  between operations  2.11 us (4%)
    ppermute x9, starting transfers between devices, move(): return lax.ppermute(value, AXES, pairs)  18.7 us
    ppermute x9, waiting for transfers between devices, move(): return lax.ppermute(value, AXES, pairs)  8.72 us
    pallas_call x1, Pallas kernels, step(): call(base_kernel, (whole, whole, whole, shape(height, breadth), shape(hei...  4.66 us
    pallas_call x1, Pallas kernels, step(): call(wave_kernel, (shape(2 * height + 8, frame), shape(2, height, frame))...  4.53 us
    pallas_call x1, Pallas kernels, step(): call(prepare_kernel, (whole, shape(2 * modes, 2, frame, frame), shape(2,...  4.46 us
    pallas_call x1, Pallas kernels, step(): call(select_kernel, shape(2, height, frame), [space(pl.ANY)] * 2 + [space...  2.34 us
    pallas_call x1, Pallas kernels, step(): call(second_kernel, (whole, whole), [space(SMEM)] + [space(VMEM)] * 7 + [...  1.66 us
    pallas_call x1, Pallas kernels, step(): call(load_kernel, (shape(*probe_modes.shape), shape(*matrix.shape, dtype=...  1.57 us
  transfers between devices with their start and end apart: 9, of which 4 were waited for; matrix products, arithmetic and copies ran while one was open for 0% of the time, Pallas kernels for 31%

profile of v3, /device:TPU:9, one launch (start us, length us, event | category | flops | bytes accessed | tf_op | source)
XLA Modules:
  0.0 52.2 jit_solution(17372211195264341555)
XLA Ops:
  0.6 0.7 %collective-permute-start.2 = (f32[2,2,256,256]{3,2,1,0:T(8,128)}, f32[2,2,256,256]{3,2,1,0:T(8,128)S(1)}, u32[]{:S(2)}, u32[]{:S(2)}) collective-permute-start(f32[2,2,256,256]{3,2,1,0:T(8,128)} %probe_ref.1), channel_id=1, source_target_pairs={{0,1},{1,0},{2,3},{3,2},{4,5},{5,4},{6,7},{7,6},{8,9},{9,8},{10,11... | collective-permute-start | bytes 3145736 | tf_op jit(solution)/shard_map/ppermute | solution.py:495
  1.4 0.7 %collective-permute-start.5 = (f32[1,256,256]{2,1,0:T(8,128)}, f32[1,256,256]{2,1,0:T(8,128)S(1)}, u32[]{:S(2)}, u32[]{:S(2)}) collective-permute-start(f32[1,256,256]{2,1,0:T(8,128)} %own_ref.1), channel_id=1, source_target_pairs={{2,6},{6,10},{10,14},{14,18},{18,22},{22,26},{26,30}} | collective-permute-start | bytes 786440 | tf_op jit(solution)/shard_map/ppermute | solution.py:495
  2.0 3.1 %collective-permute-start = (s32[1]{0:T(128)}, s32[1]{0:T(128)}, u32[]{:S(2)}, u32[]{:S(2)}) collective-permute-start(s32[1]{0:T(128)} %param.11), channel_id=1, source_target_pairs={{0,2},{2,4},{4,6},{6,8},{8,10},{10,12},{12,14},{14,16},{16,18},{18... | collective-permute-start | bytes 20 | tf_op jit(solution)/shard_map/ppermute | solution.py:495
  5.9 0.8 %shard_map.86.table_ref = s32[2,8192]{1,0:T(2,128)S(1)} custom-call(s32[2,8192]{1,0:T(2,128)} %bitcast.1), custom_call_target="tpu_custom_call" | custom-call | flops 5000000 | bytes 5000000 | tf_op jit(solution)/shard_map/pallas_call | solution.py:508
  6.7 0.0 copy-start.1
  6.7 0.8 %collective-permute-done.received_ref.scan_ref = s32[1]{0:T(128)} collective-permute-done((s32[1]{0:T(128)}, s32[1]{0:T(128)}, u32[]{:S(2)}, u32[]{:S(2)}) %collective-permute-start) | collective-permute-done | bytes 36 | tf_op jit(solution)/shard_map/ppermute | solution.py:495
  7.5 2.3 %shard_map.89 = f32[2,128,256]{2,1,0:T(8,128)S(1)} custom-call(s32[1]{0:T(128)S(6)} %copy.19.scan_ref.own_scan_ref, s32[1]{0:T(128)} %collective-permute-done.received_ref.scan_ref, s32[2,8192]{1,0:T(2,128)S(1)} %shard_map.86.table_ref, f32[2,128,2048]{2,1,0:T(8,128)} %object_ref.9), custom_call_target="tpu_custom_call" | custom-call | flops 5000000 | bytes 5000000 | tf_op jit(solution)/shard_map/pallas_call | solution.py:516
  9.8 0.0 copy-start
  9.9 2.5 %collective-permute-start.3 = (f32[2,128,256]{2,1,0:T(8,128)S(1)}, f32[2,128,256]{2,1,0:T(8,128)S(1)}, u32[]{:S(2)}, u32[]{:S(2)}) collective-permute-start(f32[2,128,256]{2,1,0:T(8,128)S(1)} %shard_map.89), channel_id=1, source_target_pairs={{0,2},{2,0},{4,6},{6,4},{8,10},{10,8},{12,14},{14,12},{16,18},{18,... | collective-permute-start | bytes 786440 | tf_op jit(solution)/shard_map/ppermute | solution.py:495
  12.3 0.0 collective-permute-done.5.received_ref
  12.3 4.0 %collective-permute-start.6 = (f32[1,256,256]{2,1,0:T(8,128)S(1)}, f32[1,256,256]{2,1,0:T(8,128)S(1)}, u32[]{:S(2)}, u32[]{:S(2)}) collective-permute-start(f32[1,256,256]{2,1,0:T(8,128)S(1)} %collective-permute-done.5.received_ref), channel_id=1, source_target_pairs={{0,1},{1,0},{2,3},{3,2},{4,5},{5,4},{6,7},{7,6},{8,9},{9,8},{10,11... | collective-permute-start | bytes 786440 | tf_op jit(solution)/shard_map/ppermute | solution.py:495
  16.3 0.8 %collective-permute-done.3.received_ref = f32[2,128,256]{2,1,0:T(8,128)S(1)} collective-permute-done((f32[2,128,256]{2,1,0:T(8,128)S(1)}, f32[2,128,256]{2,1,0:T(8,128)S(1)}, u32[]{:S(2)}, u32[]{:S(2)}) %collective-permute-start.3) | collective-permute-done | bytes 262176 | tf_op jit(solution)/shard_map/ppermute | solution.py:495
  17.1 5.3 %collective-permute-start.4 = (f32[2,128,256]{2,1,0:T(8,128)S(1)}, f32[2,128,256]{2,1,0:T(8,128)S(1)}, u32[]{:S(2)}, u32[]{:S(2)}) collective-permute-start(f32[2,128,256]{2,1,0:T(8,128)S(1)} %collective-permute-done.3.received_ref), channel_id=1, source_target_pairs={{0,1},{1,0},{2,3},{3,2},{4,5},{5,4},{6,7},{7,6},{8,9},{9,8},{10,11... | collective-permute-start | bytes 786440 | tf_op jit(solution)/shard_map/ppermute | solution.py:495
  23.1 1.6 %shard_map.87 = (f32[2,2,256,256]{3,2,1,0:T(8,128)S(1)}, bf16[8,256,256]{2,1,0:T(8,128)(2,1)S(1)}) custom-call(f32[2,2,256,256]{3,2,1,0:T(8,128)} %probe_ref.1, bf16[8,256,256]{2,1,0:T(8,128)(2,1)} %constant.2.clone.matrix_ref), custom_call_target="tpu_custom_call" | custom-call | flops 5000000 | bytes 5000000 | tf_op jit(solution)/shard_map/pallas_call | solution.py:526
  24.6 0.1 collective-permute-start.1
  24.7 0.0 collective-permute-done.6.swapped_ref
  24.7 0.0 copy-done.1
  24.7 0.3 shard_map.91.amplitude_ref
  25.0 1.0 %collective-permute-done.1.swapped_ref = s32[1]{0:T(128)} collective-permute-done((s32[1]{0:T(128)}, s32[1]{0:T(128)}, u32[]{:S(2)}, u32[]{:S(2)}) %collective-permute-start.1) | collective-permute-done | bytes 36 | tf_op jit(solution)/shard_map/ppermute | solution.py:495
  26.1 0.0 collective-permute-done.2.other_probe_ref
  26.1 0.0 copy-done
  26.1 4.5 %shard_map.88 = (f32[2,128,2048]{2,1,0:T(8,128)}, f32[4,2,256,256]{3,2,1,0:T(8,128)S(1)}, f32[2,128,256]{2,1,0:T(8,128)S(1)}, f32[256,256]{1,0:T(8,128)S(1)}, f3...) custom-call(s32[1]{0:T(128)S(6)} %copy.19.scan_ref.own_scan_ref, ...), custom_call_target="tpu_custom_call" | custom-call | flops 5000000 | bytes 5000000 | tf_op jit(solution)/shard_map/pallas_call | solution.py:536
  30.5 0.6 %shard_map.90.first_ref = f32[4,2,128,256]{3,2,1,0:T(8,128)S(1)} custom-call(f32[2,128,256]{2,1,0:T(8,128)S(1)} %collective-permute-done.3.received_ref, f32[4,2,256,256]{3,2,1,0:T(8,128)S(1)} %get-tuple-element.27.probe_ref, bf16[8,256,256]{2,1,0:T(8,128)(2,1)S(1)} %get-tuple-element.23.matrix_ref), custom_call_target="tpu_custom_call" | custom-call | flops 5000000 | bytes 5000000 | tf_op jit(solution)/shard_map/pallas_call | solution.py:567
  31.2 0.0 collective-permute-done.4.swapped_ref
  31.2 4.5 %shard_map.92 = (f32[264,256]{1,0:T(8,128)S(1)}, f32[2,128,256]{2,1,0:T(8,128)S(1)}) custom-call(s32[8]{0:T(128)S(1)} %get-tuple-element.24.place_ref, f32[2,128,256]{2,1,0:T(8,128)S(1)} %get-tuple-element.25.window_ref, f32[2,128,256]{2,1,0:T(8,128)S(1)} %collective-permute-done.3.received_ref, f32[2,128,256]{2,1,0:T(8,128)S(1)} %collective-permute-done.4.swapped_ref, ...), custom_call_target="tpu_custom_call" | custom-call | flops 5000000 | bytes 5000000 | tf_op jit(solution)/shard_map/pallas_call | solution.py:568
  35.7 1.9 %collective-permute-start.7 = (f32[264,256]{1,0:T(8,128)S(1)}, f32[264,256]{1,0:T(8,128)S(1)}, u32[]{:S(2)}, u32[]{:S(2)}) collective-permute-start(f32[264,256]{1,0:T(8,128)S(1)} %get-tuple-element.37), channel_id=1, source_target_pairs={{2,0},{0,2},{6,4},{4,6},{10,8},{8,10},{14,12},{12,14},{18,16},{16,... | collective-permute-start | bytes 811016 | tf_op jit(solution)/shard_map/ppermute | solution.py:495
  37.7 6.2 %collective-permute-done.7.received_ref = f32[264,256]{1,0:T(8,128)S(1)} collective-permute-done((f32[264,256]{1,0:T(8,128)S(1)}, f32[264,256]{1,0:T(8,128)S(1)}, u32[]{:S(2)}, u32[]{:S(2)}) %collective-permute-start.7) | collective-permute-done | bytes 270368 | tf_op jit(solution)/shard_map/ppermute | solution.py:495
  43.8 0.4 collective-permute-start.8
  44.3 4.7 %shard_map.93 = (f32[2,128,2048]{2,1,0:T(8,128)}, f32[2,128,2048]{2,1,0:T(8,128)}, f32[2,128,2048]{2,1,0:T(8,128)S(1)}, f32[128,2048]{1,0:T(8,128)S(1)}, f32[128...) custom-call(s32[8]{0:T(128)S(1)} %get-tuple-element.24.place_ref, ...), custom_call_target="tpu_custom_call", output_to_operand_aliasing={{1}: (9, {})} | custom-call | flops 5000000 | bytes 5000000 | tf_op jit(solution)/shard_map/pallas_call | solution.py:583
  48.9 1.6 %shard_map.94 = (f32[2,128,2048]{2,1,0:T(8,128)}, f32[2,128,2048]{2,1,0:T(8,128)}) custom-call(s32[8]{0:T(128)S(1)} %get-tuple-element.32.others_ref, f32[2,128,2048]{2,1,0:T(8,128)S(1)} %copy-done, f32[2,128,2048]{2,1,0:T(8,128)S(1)} %get-tuple-element.33.total_ref, ...), custom_call_target="tpu_custom_call", output_to_operand_aliasing={{0}: (6, {}), {1}: (7, {})} | custom-call | flops 5000000 | bytes 5000000 | tf_op jit(solution)/shard_map/pallas_call | solution.py:609
  50.5 0.0 collective-permute-done.8.swapped_ref
  50.5 1.7 %shard_map.95 = (f32[2,128,2048]{2,1,0:T(8,128)}, f32[2,128,2048]{2,1,0:T(8,128)}) custom-call(s32[8]{0:T(128)S(1)} %get-tuple-element.32.others_ref, f32[2,128,2048]{2,1,0:T(8,128)S(1)} %copy-done, f32[2,128,2048]{2,1,0:T(8,128)S(1)} %get-tuple-element.33.total_ref, ...), custom_call_target="tpu_custom_call", output_to_operand_aliasing={{0}: (8, {}), {1}: (9, {})} | custom-call | flops 5000000 | bytes 5000000 | tf_op jit(solution)/shard_map/pallas_call | solution.py:617
Async XLA Ops:
  0.6 25.4 %collective-permute-start.2 = (f32[2,2,256,256]{3,2,1,0:T(8,128)}, f32[2,2,256,256]{3,2,1,0:T(8,128)S(1)}, u32[]{:S(2)}, u32[]{:S(2)}) collective-permute-start(f32[2,2,256,256]{3,2,1,0:T(8,128)} %probe_ref.1), channel_id=1, source_target_pairs={{0,1},{1,0},{2,3},{3,2},{4,5},{5,4},{6,7},{7,6},{8,9},{9,8},{10,11... | collective-permute-start | bytes 3145736 | tf_op jit(solution)/shard_map/ppermute | solution.py:495
  1.4 10.9 %collective-permute-start.5 = (f32[1,256,256]{2,1,0:T(8,128)}, f32[1,256,256]{2,1,0:T(8,128)S(1)}, u32[]{:S(2)}, u32[]{:S(2)}) collective-permute-start(f32[1,256,256]{2,1,0:T(8,128)} %own_ref.1), channel_id=1, source_target_pairs={{2,6},{6,10},{10,14},{14,18},{18,22},{22,26},{26,30}} | collective-permute-start | bytes 786440 | tf_op jit(solution)/shard_map/ppermute | solution.py:495
  2.0 5.5 %collective-permute-start = (s32[1]{0:T(128)}, s32[1]{0:T(128)}, u32[]{:S(2)}, u32[]{:S(2)}) collective-permute-start(s32[1]{0:T(128)} %param.11), channel_id=1, source_target_pairs={{0,2},{2,4},{4,6},{6,8},{8,10},{10,12},{12,14},{14,16},{16,18},{18... | collective-permute-start | bytes 20 | tf_op jit(solution)/shard_map/ppermute | solution.py:495
  6.7 18.0 %copy-start.1 = (f32[1,256,256]{2,1,0:T(8,128)S(1)}, f32[1,256,256]{2,1,0:T(8,128)}, u32[]{:S(2)}) copy-start(f32[1,256,256]{2,1,0:T(8,128)} %own_ref.1) | copy-start | bytes 786436
  9.8 16.2 %copy-start = (f32[2,128,2048]{2,1,0:T(8,128)S(1)}, f32[2,128,2048]{2,1,0:T(8,128)}, u32[]{:S(2)}) copy-start(f32[2,128,2048]{2,1,0:T(8,128)} %object_ref.9) | copy-start | bytes 6291460
  9.9 7.2 %collective-permute-start.3 = (f32[2,128,256]{2,1,0:T(8,128)S(1)}, f32[2,128,256]{2,1,0:T(8,128)S(1)}, u32[]{:S(2)}, u32[]{:S(2)}) collective-permute-start(f32[2,128,256]{2,1,0:T(8,128)S(1)} %shard_map.89), channel_id=1, source_target_pairs={{0,2},{2,0},{4,6},{6,4},{8,10},{10,8},{12,14},{14,12},{16,18},{18,... | collective-permute-start | bytes 786440 | tf_op jit(solution)/shard_map/ppermute | solution.py:495
  12.3 12.4 %collective-permute-start.6 = (f32[1,256,256]{2,1,0:T(8,128)S(1)}, f32[1,256,256]{2,1,0:T(8,128)S(1)}, u32[]{:S(2)}, u32[]{:S(2)}) collective-permute-start(f32[1,256,256]{2,1,0:T(8,128)S(1)} %collective-permute-done.5.received_ref), channel_id=1, source_target_pairs={{0,1},{1,0},{2,3},{3,2},{4,5},{5,4},{6,7},{7,6},{8,9},{9,8},{10,11... | collective-permute-start | bytes 786440 | tf_op jit(solution)/shard_map/ppermute | solution.py:495
  17.1 14.1 %collective-permute-start.4 = (f32[2,128,256]{2,1,0:T(8,128)S(1)}, f32[2,128,256]{2,1,0:T(8,128)S(1)}, u32[]{:S(2)}, u32[]{:S(2)}) collective-permute-start(f32[2,128,256]{2,1,0:T(8,128)S(1)} %collective-permute-done.3.received_ref), channel_id=1, source_target_pairs={{0,1},{1,0},{2,3},{3,2},{4,5},{5,4},{6,7},{7,6},{8,9},{9,8},{10,11... | collective-permute-start | bytes 786440 | tf_op jit(solution)/shard_map/ppermute | solution.py:495
  24.6 1.4 %collective-permute-start.1 = (s32[1]{0:T(128)}, s32[1]{0:T(128)}, u32[]{:S(2)}, u32[]{:S(2)}) collective-permute-start(s32[1]{0:T(128)} %collective-permute-done.received_ref.scan_ref), channel_id=1, source_target_pairs={{0,1},{1,0},{2,3},{3,2},{4,5},{5,4},{6,7},{7,6},{8,9},{9,8},{10,11... | collective-permute-start | bytes 20 | tf_op jit(solution)/shard_map/ppermute | solution.py:495
  35.7 8.1 %collective-permute-start.7 = (f32[264,256]{1,0:T(8,128)S(1)}, f32[264,256]{1,0:T(8,128)S(1)}, u32[]{:S(2)}, u32[]{:S(2)}) collective-permute-start(f32[264,256]{1,0:T(8,128)S(1)} %get-tuple-element.37), channel_id=1, source_target_pairs={{2,0},{0,2},{6,4},{4,6},{10,8},{8,10},{14,12},{12,14},{18,16},{16,... | collective-permute-start | bytes 811016 | tf_op jit(solution)/shard_map/ppermute | solution.py:495
  43.8 6.7 %collective-permute-start.8 = (f32[264,256]{1,0:T(8,128)S(1)}, f32[264,256]{1,0:T(8,128)S(1)}, u32[]{:S(2)}, u32[]{:S(2)}) collective-permute-start(f32[264,256]{1,0:T(8,128)S(1)} %collective-permute-done.7.received_ref), channel_id=1, source_target_pairs={{0,1},{1,0},{2,3},{3,2},{4,5},{5,4},{6,7},{7,6},{8,9},{9,8},{10,11... | collective-permute-start | bytes 811016 | tf_op jit(solution)/shard_map/ppermute | solution.py:495

commit v4 on v3

--- a/solution.py
+++ b/solution.py
@@ -60,15 +60,13 @@
     return jnp.where(lane < shift, third, first), second
 
 
-def stage_kernel(table_ref, held_ref, sem):
-    copy = pltpu.make_async_copy(table_ref, held_ref, sem)
-    copy.start()
-    copy.wait()
-
-
-def load_kernel(probe_ref, matrix_ref, held_probe_ref, held_matrix_ref, sems):
-    for copy in fetch([(probe_ref, held_probe_ref), (matrix_ref, held_matrix_ref)], sems):
-        copy.wait()
+def stage_kernel(object_ref, table_ref, staged_ref, held_ref, sems):
+    first = pltpu.make_async_copy(object_ref, staged_ref, sems.at[0])
+    second = pltpu.make_async_copy(table_ref, held_ref, sems.at[1])
+    first.start()
+    second.start()
+    first.wait()
+    second.wait()
 
 
 def fetch(pairs, sems, first=0):
@@ -78,23 +76,13 @@
     return copies
 
 
-def select_kernel(own_scan_ref, scan_ref, table_ref, object_ref, out_ref, own_ref, got_ref, third_ref, sems):
+def select_kernel(own_scan_ref, scan_ref, table_ref, object_ref, out_ref):
     odd = lax.axis_index("tile") % 2 == 1
-    for copy in fetch([(own_scan_ref, own_ref), (scan_ref, got_ref)], sems):
-        copy.wait()
-    scan = jnp.where(odd & (lax.axis_index("mode") == 1), own_ref[0], got_ref[0])
+    scan = jnp.where(odd & (lax.axis_index("mode") == 1), own_scan_ref[0], scan_ref[0])
     _, col = lookup(table_ref, scan)
-    blocks = object_ref.shape[2] // LANES
-    block, shift = col // LANES, col % LANES
-    last = jnp.minimum(block + 2, blocks - 1)
-    pairs = [
-        (object_ref.at[:, :, pl.ds(pl.multiple_of(block * LANES, LANES), 2 * LANES)], out_ref),
-        (object_ref.at[:, :, pl.ds(pl.multiple_of(last * LANES, LANES), LANES)], third_ref),
-    ]
-    for copy in fetch(pairs, sems, 2):
-        copy.wait()
-    lane = lax.broadcasted_iota(jnp.int32, third_ref.shape, 2)
-    out_ref[:, :, :LANES] = jnp.where(lane < shift, third_ref[...], out_ref[:, :, :LANES])
+    low, high = strip_window(object_ref, col)
+    out_ref[:, :, :LANES] = low
+    out_ref[:, :, LANES:] = high
 
 
 def slots(own_ref, received_ref, swapped_ref):
@@ -104,6 +92,16 @@
     above = jnp.where(first, got, other)
     further = jnp.where(first, other, got)
     return jnp.where(odd, further, own), above, jnp.where(odd, own, further)
+
+
+def keep_scalars(out_ref, values):
+    for index, value in enumerate(values):
+        row = jnp.full((1, out_ref.shape[1]), value, jnp.int32)
+        out_ref[index : index + 1] = row.astype(jnp.float32)
+
+
+def scalar_of(ref, index):
+    return jnp.max(ref[index : index + 1]).astype(jnp.int32)
 
 
 def within(table_ref, scan, strip, height):
@@ -147,11 +145,11 @@
 
 
 def prepare_kernel(
-    scan_ref, received_ref, swapped_ref, count_ref, table_ref, object_ref, own_probe_ref, other_probe_ref, matrix_ref,
+    scan_ref, received_ref, swapped_ref, table_ref, object_ref, own_probe_ref, other_probe_ref, matrix_ref,
     gradient_ref, probe_ref, window_ref, light_ref, total_ref, strip_ref, place_ref,
-    zero_ref, tall_ref, own_ref, got_ref, other_ref, live_ref, sems,
+    zero_ref, tall_ref, own_ref, got_ref, other_ref, sems,
 ):
-    pairs = [(scan_ref, own_ref), (received_ref, got_ref), (swapped_ref, other_ref), (count_ref, live_ref)]
+    pairs = [(scan_ref, own_ref), (received_ref, got_ref), (swapped_ref, other_ref)]
     scalars = fetch(pairs, sems)
     zero_ref[...] = jnp.zeros_like(zero_ref)
     step = zero_ref.shape[0]
@@ -159,35 +157,29 @@
     for part in range(2):
         for at in range(0, object_ref.shape[1], step):
             copies += fetch([(zero_ref, gradient_ref.at[part, at : at + step])], sems, len(pairs) + len(copies))
+    modes = own_probe_ref.shape[0]
+    sources = [ref.at[mode, part] for ref in (own_probe_ref, other_probe_ref) for mode in range(modes) for part in range(2)]
+    total = sources[0][...] * sources[0][...]
+    for source in sources[1:]:
+        total = total + source[...] * source[...]
+    total_ref[...] = total
     for copy in scalars:
         copy.wait()
-    modes = own_probe_ref.shape[0]
     height = object_ref.shape[1]
-    frame = own_probe_ref.shape[2]
     tile = lax.axis_index("tile")
     odd = tile % 2
     scan, _, _ = slots(own_ref, got_ref, other_ref)
     row, col = within(table_ref, scan, tile - 2 * odd, height)
     shift = col % LANES
-    total = jnp.zeros((frame, frame), jnp.float32)
-    for index in range(2 * modes):
-        source = own_probe_ref if index < modes else other_probe_ref
-        for part in range(2):
-            value = source[index % modes, part]
-            total = total + value * value
-            roll_into(probe_ref.at[index, part], value, row, shift, tall_ref.at[index, part])
-    total_ref[...] = total
-    roll_into(light_ref, total, row, shift, tall_ref.at[0, 0])
+    for index, source in enumerate(sources):
+        mode, part = divmod(index, 2)
+        roll_into(probe_ref.at[mode, part], source[...], row, shift, tall_ref.at[mode, part])
+    roll_into(light_ref, total_ref[...], row, shift, tall_ref.at[0, 0])
     low, high = strip_window(object_ref, col)
     window_ref[:, :, :LANES] = low
     window_ref[:, :, LANES:] = high
-    place_ref[0] = row
-    place_ref[1] = col
-    place_ref[2] = jnp.where(odd == 1, (tile >= 2).astype(jnp.int32), live_ref[0])
-    place_ref[3] = jnp.where(odd == 1, 0, row)
-    place_ref[4] = jnp.where(odd == 1, row, height)
-    for index in range(5, 8):
-        place_ref[index] = 0
+    live = jnp.where(odd == 1, (tile >= 2).astype(jnp.int32), 1)
+    keep_scalars(place_ref, (jnp.where(odd == 1, 0, row), jnp.where(odd == 1, row, height), live))
     transform_rows(probe_ref, 0, window_ref, matrix_ref, strip_ref)
     for copy in copies:
         copy.wait()
@@ -250,7 +242,7 @@
     height = window_ref.shape[1]
     half = frame // 2
     core = lax.axis_index("mode")
-    low, high = place_ref[3], place_ref[4]
+    low, high = place_ref[0:1, :1].astype(jnp.int32), place_ref[1:2, :1].astype(jnp.int32)
     transform_rows(probe_ref, pl.multiple_of(core * height, height), swapped_ref, matrix_ref, second_ref)
     level = lax.broadcasted_iota(jnp.int32, (height, frame), 0)
 
@@ -303,12 +295,12 @@
         probe_re, probe_im = probe_ref[mode, 0], probe_ref[mode, 1]
         grad_re = grad_re + (probe_re * back_re + probe_im * back_im)
         grad_im = grad_im + (probe_re * back_im - probe_im * back_re)
-    live = (place_ref[2] > 0).astype(jnp.float32)
+    live = place_ref[2:3, :1]
     grad_re = (grad_re - light_ref[...] * patch_ref[0]) * live
     grad_im = (grad_im - light_ref[...] * patch_ref[1]) * live
     send_ref[:height] = jnp.where(core == 0, grad_re[height:], grad_re[:height])
     send_ref[height : 2 * height] = jnp.where(core == 0, grad_im[height:], grad_im[:height])
-    send_ref[2 * height :] = jnp.full((8, frame), live, jnp.float32)
+    send_ref[2 * height :] = jnp.broadcast_to(live, (8, frame))
     keep_ref[0] = grad_re[:height]
     keep_ref[1] = grad_im[:height]
 
@@ -333,16 +325,21 @@
     height, breadth = object_ref.shape[1:]
     tile = lax.axis_index("tile")
     core = lax.axis_index("mode")
-    col = place_ref[1]
     fill = pltpu.make_async_copy(object_ref, updated_ref, fills.at[0])
     fill.start()
     scalars = fetch([(scan_ref, own_ref), (received_ref, got_ref), (swapped_ref, other_ref)], fills, 1)
-    live = (place_ref[2] > 0).astype(jnp.float32)
     total_ref[...] = jnp.zeros_like(total_ref)
     weight_ref[...] = jnp.zeros_like(weight_ref)
+    for copy in scalars:
+        copy.wait()
+    odd = tile % 2
+    main, above, third = slots(own_ref, got_ref, other_ref)
+    _, col = within(table_ref, main, tile, height)
+    live = place_ref[2:3, :1]
+    start, stop = place_ref[0:1, :1].astype(jnp.int32), place_ref[1:2, :1].astype(jnp.int32)
     lane = lax.broadcasted_iota(jnp.int32, (height, LANES), 1)
     level = lax.broadcasted_iota(jnp.int32, (height, LANES), 0)
-    kept = (level >= place_ref[3]) & (level < place_ref[4])
+    kept = (level >= start) & (level < stop)
     for slot in range(3):
         block = jnp.minimum(col // LANES + slot, breadth // LANES - 1)
         at = pl.ds(pl.multiple_of(block * LANES, LANES), LANES)
@@ -355,10 +352,6 @@
             change = jnp.where(kept, change, 0.0)
             total_ref[part, :, at] = change
             new_ref[slot, part] = object_ref[part, :, at] + change * scale
-    odd = tile % 2
-    for copy in scalars:
-        copy.wait()
-    _, above, third = slots(own_ref, got_ref, other_ref)
     places = []
     for scan, strip, far in ((above, tile - 1, False), (third, tile - 2 + 2 * odd, True)):
         row, start = within(table_ref, scan, strip, height)
@@ -368,13 +361,13 @@
         begin = jnp.where(odd == 1, row, 0) if far else 0
         end = jnp.where(odd == 1, height, row) if far else height
         places.append((start, begin, end, turned[:height] if far else turned[height:]))
+    chosen = []
     for slot, out_ref in ((0, first_ref), (1, second_ref)):
         direct = core == slot
         near, far = places
         out_ref[...] = jnp.where(direct, near[3], far[3])
-        for index in range(3):
-            others_ref[4 * slot + index] = jnp.where(direct, near[index], far[index])
-        others_ref[4 * slot + 3] = 0
+        chosen += [jnp.where(direct, near[index], far[index]) for index in range(3)]
+    keep_scalars(others_ref, chosen)
     fill.wait()
     copies = []
     for slot in range(3):
@@ -439,7 +432,7 @@
     updated_ref, gradient_ref, new_ref, sum_ref, sems,
 ):
     del old_updated_ref, old_gradient_ref
-    windows = [(others_ref[0], others_ref[1], others_ref[2], first_ref, received_ref)]
+    windows = [(*(scalar_of(others_ref, index) for index in range(3)), first_ref, received_ref)]
     add_windows(windows, 0, object_ref, total_ref, weight_ref, updated_ref, gradient_ref, new_ref, sum_ref, sems)
 
 
@@ -449,8 +442,8 @@
 ):
     del old_updated_ref, old_gradient_ref
     windows = [
-        (others_ref[0], others_ref[1], others_ref[2], first_ref, received_ref),
-        (others_ref[4], others_ref[5], others_ref[6], second_ref, swapped_ref),
+        (*(scalar_of(others_ref, index) for index in range(3)), first_ref, received_ref),
+        (*(scalar_of(others_ref, index) for index in range(3, 6)), second_ref, swapped_ref),
     ]
     add_windows(windows, 1, object_ref, total_ref, weight_ref, updated_ref, gradient_ref, new_ref, sum_ref, sems)
 
@@ -468,10 +461,6 @@
     )
 
 
-def in_hbm(value):
-    return pltpu.with_memory_space_constraint(value, pltpu.HBM)
-
-
 def space(where):
     return pl.BlockSpec(memory_space=where)
 
@@ -504,33 +493,21 @@
         other_probe = move(probe_modes, swap)
         received_amplitude = move(amplitudes, onward)
         scalar = pltpu.SMEM((1,), jnp.int32)
-        staged = object_tiles
-        table = call(
+        staged, table = call(
             stage_kernel,
-            shape(*table.shape, dtype=jnp.int32),
-            [space(pltpu.HBM)],
-            space(VMEM),
-            [pltpu.SemaphoreType.DMA],
-            mebibytes=8,
-        )(in_hbm(table))
-        window = call(
-            select_kernel,
-            shape(2, height, frame),
-            [space(pl.ANY)] * 2 + [space(VMEM), space(pl.ANY)],
-            space(VMEM),
-            [scalar, scalar, pltpu.VMEM((2, height, LANES), jnp.float32), pltpu.SemaphoreType.DMA((4,))],
-        )(slot_scan, received_scan, table, in_hbm(object_tiles))
-        received = move(window, gather)
-        swapped_scan = move(received_scan, swap)
-        swapped_amplitude = move(received_amplitude, swap)
-        own_probe, matrix = call(
-            load_kernel,
-            (shape(*probe_modes.shape), shape(*matrix.shape, dtype=matrix.dtype)),
+            (shape(*object_tiles.shape), shape(*table.shape, dtype=jnp.int32)),
             [space(pltpu.HBM)] * 2,
             [space(VMEM)] * 2,
             [pltpu.SemaphoreType.DMA((2,))],
             mebibytes=8,
-        )(in_hbm(probe_modes), in_hbm(matrix))
+        )(pltpu.with_memory_space_constraint(object_tiles, pltpu.HBM), pltpu.with_memory_space_constraint(table, pltpu.HBM))
+        window = call(
+            select_kernel, shape(2, height, frame), [space(SMEM)] * 2 + [space(VMEM)] * 2, space(VMEM)
+        )(slot_scan, received_scan, table, staged)
+        received = move(window, gather)
+        swapped_scan = move(received_scan, swap)
+        swapped_amplitude = move(received_amplitude, swap)
+        scalar = pltpu.SMEM((1,), jnp.int32)
         strip = shape(2 * modes, 2, height, frame)
         whole = shape(2, height, breadth)
         gradient, probe, own_window, light, plain, own_strip, place = call(
@@ -542,20 +519,19 @@
                 shape(frame, frame),
                 shape(frame, frame),
                 strip,
-                shape(8, dtype=jnp.int32),
+                shape(8, LANES),
             ),
-            [space(pl.ANY)] * 4 + [space(VMEM)] * 5,
-            [space(pl.ANY)] + [space(VMEM)] * 5 + [space(SMEM)],
+            [space(pl.ANY)] * 3 + [space(VMEM)] * 5,
+            [space(pl.ANY)] + [space(VMEM)] * 6,
             [
                 pltpu.VMEM((height // 8, breadth), jnp.float32),
                 pltpu.VMEM((2 * modes, 2, frame // LANES, frame + height, LANES), jnp.float32),
                 scalar,
                 scalar,
                 scalar,
-                scalar,
-                pltpu.SemaphoreType.DMA((20,)),
+                pltpu.SemaphoreType.DMA((19,)),
             ],
-        )(slot_scan, received_scan, swapped_scan, slot_count, table, staged, own_probe, other_probe, matrix)
+        )(slot_scan, received_scan, swapped_scan, table, staged, probe_modes, other_probe, matrix)
         swapped = move(received, swap)
         amplitude = call(
             reorder_kernel,
@@ -568,7 +544,7 @@
         send, keep = call(
             wave_kernel,
             (shape(2 * height + 8, frame), shape(2, height, frame)),
-            [space(SMEM)] + [space(VMEM)] * 9,
+            [space(VMEM)] * 10,
             [space(VMEM)] * 2,
             [
                 pltpu.VMEM((2, frame, frame), jnp.float32),
@@ -589,10 +565,10 @@
                 shape(height, breadth),
                 shape(height, frame),
                 shape(height, frame),
-                shape(8, dtype=jnp.int32),
+                shape(8, LANES),
             ),
-            [space(SMEM)] + [space(pl.ANY)] * 3 + [space(VMEM)] * 5 + [space(pl.ANY)],
-            [space(pl.ANY)] * 2 + [space(VMEM)] * 4 + [space(SMEM)],
+            [space(VMEM)] + [space(pl.ANY)] * 3 + [space(VMEM)] * 5 + [space(pl.ANY)],
+            [space(pl.ANY)] * 2 + [space(VMEM)] * 5,
             [
                 blocks,
                 pltpu.VMEM((2, frame // LANES, frame + height, LANES), jnp.float32),
@@ -609,7 +585,7 @@
         updated, gradient = call(
             first_kernel,
             (whole, whole),
-            [space(SMEM)] + [space(VMEM)] * 5 + [space(pl.ANY)] * 2,
+            [space(VMEM)] * 6 + [space(pl.ANY)] * 2,
             [space(pl.ANY)] * 2,
             [blocks, blocks, semaphores],
             aliases={6: 0, 7: 1},
@@ -617,7 +593,7 @@
         return call(
             second_kernel,
             (whole, whole),
-            [space(SMEM)] + [space(VMEM)] * 7 + [space(pl.ANY)] * 2,
+            [space(VMEM)] * 8 + [space(pl.ANY)] * 2,
             [space(pl.ANY)] * 2,
             [blocks, blocks, semaphores],
             aliases={8: 0, 9: 1},

time: 52.5 us -> 45.6 us (0.87)
  Pallas kernels: 22.6 us -> 17 us
  waiting for transfers between devices: 8.72 us -> 8.03 us
  between operations: 2.11 us -> 1.45 us
    pallas_call x5 -> x4, Pallas kernels: 7.98 us -> 5.02 us  [the longest x1 1.65 us: step(): call(stage_kernel, (shape(*object_tiles.shape), shape(*table.shape, dtype...]
    pallas_call x1, Pallas kernels: 4.66 us -> 3.45 us  [step(): call(base_kernel, (whole, whole, whole, shape(height, breadth), shape(hei...]
    pallas_call x1, Pallas kernels: 4.46 us -> 3.61 us  [step(): call(prepare_kernel, (whole, shape(2 * modes, 2, frame, frame), shape(2,...]
    ppermute x9, waiting for transfers between devices: 8.72 us -> 8.03 us  [move(): return lax.ppermute(value, AXES, pairs)]
    pallas_call x1, Pallas kernels: 4.53 us -> 3.98 us  [step(): call(wave_kernel, (shape(2 * height + 8, frame), shape(2, height, frame))...]
  transfers between devices with their start and end apart: 9 -> 9, of which waited for: 4 -> 3; matrix products, arithmetic and copies ran while one was open for 0% -> 0% of each run, Pallas kernels for 31% -> 26%
where the time goes in v4:
time: 45.6 us; the launch traced here: 45.1 us
  starting transfers between devices  18.6 us (41%)
  Pallas kernels  17 us (37%)
  waiting for transfers between devices  8.03 us (18%)
  between operations  1.45 us (3%)
    ppermute x9, starting transfers between devices, move(): return lax.ppermute(value, AXES, pairs)  18.6 us
    ppermute x9, waiting for transfers between devices, move(): return lax.ppermute(value, AXES, pairs)  8.03 us
    pallas_call x1, Pallas kernels, step(): call(wave_kernel, (shape(2 * height + 8, frame), shape(2, height, frame))...  3.98 us
    pallas_call x1, Pallas kernels, step(): call(prepare_kernel, (whole, shape(2 * modes, 2, frame, frame), shape(2,...  3.61 us
    pallas_call x1, Pallas kernels, step(): call(base_kernel, (whole, whole, whole, shape(height, breadth), shape(hei...  3.45 us
    pallas_call x1, Pallas kernels, step(): call(stage_kernel, (shape(*object_tiles.shape), shape(*table.shape, dtype...  1.65 us
    pallas_call x1, Pallas kernels, step(): call(second_kernel, (whole, whole), [space(VMEM)] * 8 + [space(pl.ANY)] *...  1.25 us
    pallas_call x1, Pallas kernels, step(): call(first_kernel, (whole, whole), [space(VMEM)] * 6 + [space(pl.ANY)] *...  1.13 us
  transfers between devices with their start and end apart: 9, of which 3 were waited for; matrix products, arithmetic and copies ran while one was open for 0% of the time, Pallas kernels for 26%

profile of v4, /device:TPU:9, one launch (start us, length us, event | category | flops | bytes accessed | tf_op | source)
XLA Modules:
  0.0 45.1 jit_solution(15079304145693644353)
XLA Ops:
  0.6 0.7 %collective-permute-start.2 = (f32[2,2,256,256]{3,2,1,0:T(8,128)}, f32[2,2,256,256]{3,2,1,0:T(8,128)S(1)}, u32[]{:S(2)}, u32[]{:S(2)}) collective-permute-start(f32[2,2,256,256]{3,2,1,0:T(8,128)} %own_probe_ref.1), channel_id=1, source_target_pairs={{0,1},{1,0},{2,3},{3,2},{4,5},{5,4},{6,7},{7,6},{8,9},{9,8},{10,11... | collective-permute-start | bytes 3145736 | tf_op jit(solution)/shard_map/ppermute | solution.py:484
  1.4 0.7 %collective-permute-start.5 = (f32[1,256,256]{2,1,0:T(8,128)}, f32[1,256,256]{2,1,0:T(8,128)S(1)}, u32[]{:S(2)}, u32[]{:S(2)}) collective-permute-start(f32[1,256,256]{2,1,0:T(8,128)} %own_ref.1), channel_id=1, source_target_pairs={{2,6},{6,10},{10,14},{14,18},{18,22},{22,26},{26,30}} | collective-permute-start | bytes 786440 | tf_op jit(solution)/shard_map/ppermute | solution.py:484
  2.0 3.1 %collective-permute-start = (s32[1]{0:T(128)}, s32[1]{0:T(128)}, u32[]{:S(2)}, u32[]{:S(2)}) collective-permute-start(s32[1]{0:T(128)} %param.11), channel_id=1, source_target_pairs={{0,2},{2,4},{4,6},{6,8},{8,10},{10,12},{12,14},{14,16},{16,18},{18... | collective-permute-start | bytes 20 | tf_op jit(solution)/shard_map/ppermute | solution.py:484
  5.9 0.0 copy-start.2
  5.9 1.7 %shard_map.77 = (f32[2,128,2048]{2,1,0:T(8,128)S(1)}, s32[2,8192]{1,0:T(2,128)S(1)}) custom-call(f32[2,128,2048]{2,1,0:T(8,128)} %object_ref.1, s32[2,8192]{1,0:T(2,128)} %bitcast.1), custom_call_target="tpu_custom_call" | custom-call | flops 5000000 | bytes 5000000 | tf_op jit(solution)/shard_map/pallas_call | solution.py:496
  7.5 0.0 copy-start
  7.5 0.0 copy-start.1
  7.6 0.0 collective-permute-done.received_ref.scan_ref
  7.6 1.0 %shard_map.79 = f32[2,128,256]{2,1,0:T(8,128)S(1)} custom-call(s32[1]{0:T(128)S(6)} %copy.18.scan_ref.own_scan_ref, s32[1]{0:T(128)} %collective-permute-done.received_ref.scan_ref, s32[2,8192]{1,0:T(2,128)S(1)} %get-tuple-element.22.table_ref, f32[2,128,2048]{2,1,0:T(8,128)S(1)} %get-tuple-element.23.object_ref), custom_call_target="tpu_custom_call" | custom-call | flops 5000000 | bytes 5000000 | tf_op jit(solution)/shard_map/pallas_call | solution.py:504
  8.6 3.0 %collective-permute-start.3 = (f32[2,128,256]{2,1,0:T(8,128)S(1)}, f32[2,128,256]{2,1,0:T(8,128)S(1)}, u32[]{:S(2)}, u32[]{:S(2)}) collective-permute-start(f32[2,128,256]{2,1,0:T(8,128)S(1)} %shard_map.79), channel_id=1, source_target_pairs={{0,2},{2,0},{4,6},{6,4},{8,10},{10,8},{12,14},{14,12},{16,18},{18,... | collective-permute-start | bytes 786440 | tf_op jit(solution)/shard_map/ppermute | solution.py:484
  11.6 0.0 collective-permute-done.5.received_ref
  11.6 3.2 %collective-permute-start.6 = (f32[1,256,256]{2,1,0:T(8,128)S(1)}, f32[1,256,256]{2,1,0:T(8,128)S(1)}, u32[]{:S(2)}, u32[]{:S(2)}) collective-permute-start(f32[1,256,256]{2,1,0:T(8,128)S(1)} %collective-permute-done.5.received_ref), channel_id=1, source_target_pairs={{0,1},{1,0},{2,3},{3,2},{4,5},{5,4},{6,7},{7,6},{8,9},{9,8},{10,11... | collective-permute-start | bytes 786440 | tf_op jit(solution)/shard_map/ppermute | solution.py:484
  14.9 0.8 %collective-permute-done.3.received_ref = f32[2,128,256]{2,1,0:T(8,128)S(1)} collective-permute-done((f32[2,128,256]{2,1,0:T(8,128)S(1)}, f32[2,128,256]{2,1,0:T(8,128)S(1)}, u32[]{:S(2)}, u32[]{:S(2)}) %collective-permute-start.3) | collective-permute-done | bytes 262176 | tf_op jit(solution)/shard_map/ppermute | solution.py:484
  15.7 5.2 %collective-permute-start.4 = (f32[2,128,256]{2,1,0:T(8,128)S(1)}, f32[2,128,256]{2,1,0:T(8,128)S(1)}, u32[]{:S(2)}, u32[]{:S(2)}) collective-permute-start(f32[2,128,256]{2,1,0:T(8,128)S(1)} %collective-permute-done.3.received_ref), channel_id=1, source_target_pairs={{0,1},{1,0},{2,3},{3,2},{4,5},{5,4},{6,7},{7,6},{8,9},{9,8},{10,11... | collective-permute-start | bytes 786440 | tf_op jit(solution)/shard_map/ppermute | solution.py:484
  20.9 0.0 collective-permute-start.1
  20.9 0.0 collective-permute-done.6.swapped_ref
  20.9 0.0 copy-done.2
  20.9 0.3 shard_map.81.amplitude_ref
  21.2 1.2 %collective-permute-done.1.swapped_ref = s32[1]{0:T(128)} collective-permute-done((s32[1]{0:T(128)}, s32[1]{0:T(128)}, u32[]{:S(2)}, u32[]{:S(2)}) %collective-permute-start.1) | collective-permute-done | bytes 36 | tf_op jit(solution)/shard_map/ppermute | solution.py:484
  22.4 0.0 collective-permute-done.2.other_probe_ref
  22.4 0.0 copy-done.1
  22.4 3.6 %shard_map.78 = (f32[2,128,2048]{2,1,0:T(8,128)}, f32[4,2,256,256]{3,2,1,0:T(8,128)S(1)}, f32[2,128,256]{2,1,0:T(8,128)S(1)}, f32[256,256]{1,0:T(8,128)S(1)}, f3...) custom-call(s32[1]{0:T(128)S(6)} %copy.18.scan_ref.own_scan_ref, ...), custom_call_target="tpu_custom_call" | custom-call | flops 5000000 | bytes 5000000 | tf_op jit(solution)/shard_map/pallas_call | solution.py:513
  26.1 0.6 %shard_map.80.first_ref = f32[4,2,128,256]{3,2,1,0:T(8,128)S(1)} custom-call(f32[2,128,256]{2,1,0:T(8,128)S(1)} %collective-permute-done.3.received_ref, f32[4,2,256,256]{3,2,1,0:T(8,128)S(1)} %get-tuple-element.27.probe_ref, bf16[8,256,256]{2,1,0:T(8,128)(2,1)S(1)} %copy-done), custom_call_target="tpu_custom_call" | custom-call | flops 5000000 | bytes 5000000 | tf_op jit(solution)/shard_map/pallas_call | solution.py:543
  26.7 0.0 collective-permute-done.4.swapped_ref
  26.7 4.0 %shard_map.82 = (f32[264,256]{1,0:T(8,128)S(1)}, f32[2,128,256]{2,1,0:T(8,128)S(1)}) custom-call(f32[8,128]{1,0:T(8,128)S(1)} %get-tuple-element.24.place_ref, f32[2,128,256]{2,1,0:T(8,128)S(1)} %get-tuple-element.25.window_ref, f32[2,128,256]{2,1,0:T(8,128)S(1)} %collective-permute-done.3.received_ref, ...), custom_call_target="tpu_custom_call" | custom-call | flops 5000000 | bytes 5000000 | tf_op jit(solution)/shard_map/pallas_call | solution.py:544
  30.7 2.1 %collective-permute-start.7 = (f32[264,256]{1,0:T(8,128)S(1)}, f32[264,256]{1,0:T(8,128)S(1)}, u32[]{:S(2)}, u32[]{:S(2)}) collective-permute-start(f32[264,256]{1,0:T(8,128)S(1)} %get-tuple-element.37), channel_id=1, source_target_pairs={{2,0},{0,2},{6,4},{4,6},{10,8},{8,10},{14,12},{12,14},{18,16},{16,... | collective-permute-start | bytes 811016 | tf_op jit(solution)/shard_map/ppermute | solution.py:484
  32.8 6.0 %collective-permute-done.7.received_ref = f32[264,256]{1,0:T(8,128)S(1)} collective-permute-done((f32[264,256]{1,0:T(8,128)S(1)}, f32[264,256]{1,0:T(8,128)S(1)}, u32[]{:S(2)}, u32[]{:S(2)}) %collective-permute-start.7) | collective-permute-done | bytes 270368 | tf_op jit(solution)/shard_map/ppermute | solution.py:484
  38.8 0.4 collective-permute-start.8
  39.2 3.5 %shard_map.83 = (f32[2,128,2048]{2,1,0:T(8,128)}, f32[2,128,2048]{2,1,0:T(8,128)}, f32[2,128,2048]{2,1,0:T(8,128)S(1)}, f32[128,2048]{1,0:T(8,128)S(1)}, f32[128...) custom-call(f32[8,128]{1,0:T(8,128)S(1)} %get-tuple-element.24.place_ref, ...), custom_call_target="tpu_custom_call", output_to_operand_aliasing={{1}: (9, {})} | custom-call | flops 5000000 | bytes 5000000 | tf_op jit(solution)/shard_map/pallas_call | solution.py:559
  42.7 1.1 %shard_map.84 = (f32[2,128,2048]{2,1,0:T(8,128)}, f32[2,128,2048]{2,1,0:T(8,128)}) custom-call(f32[8,128]{1,0:T(8,128)S(1)} %get-tuple-element.32.others_ref, f32[2,128,2048]{2,1,0:T(8,128)S(1)} %get-tuple-element.23.object_ref, f32[2,128,2048]{2,1,0:T(8,128)S(1)} %get-tuple-element.33.total_ref, ...), custom_call_target="tpu_custom_call", output_to_operand_aliasing={{0}: (6, {}), {1}: (7, {})} | custom-call | flops 5000000 | bytes 5000000 | tf_op jit(solution)/shard_map/pallas_call | solution.py:585
  43.8 0.0 collective-permute-done.8.swapped_ref
  43.8 1.2 %shard_map.85 = (f32[2,128,2048]{2,1,0:T(8,128)}, f32[2,128,2048]{2,1,0:T(8,128)}) custom-call(f32[8,128]{1,0:T(8,128)S(1)} %get-tuple-element.32.others_ref, f32[2,128,2048]{2,1,0:T(8,128)S(1)} %get-tuple-element.23.object_ref, f32[2,128,2048]{2,1,0:T(8,128)S(1)} %get-tuple-element.33.total_ref, ...), custom_call_target="tpu_custom_call", output_to_operand_aliasing={{0}: (8, {}), {1}: (9, {})} | custom-call | flops 5000000 | bytes 5000000 | tf_op jit(solution)/shard_map/pallas_call | solution.py:593
  (1 shorter events, 0.0 us)
Async XLA Ops:
  0.6 21.8 %collective-permute-start.2 = (f32[2,2,256,256]{3,2,1,0:T(8,128)}, f32[2,2,256,256]{3,2,1,0:T(8,128)S(1)}, u32[]{:S(2)}, u32[]{:S(2)}) collective-permute-start(f32[2,2,256,256]{3,2,1,0:T(8,128)} %own_probe_ref.1), channel_id=1, source_target_pairs={{0,1},{1,0},{2,3},{3,2},{4,5},{5,4},{6,7},{7,6},{8,9},{9,8},{10,11... | collective-permute-start | bytes 3145736 | tf_op jit(solution)/shard_map/ppermute | solution.py:484
  1.4 10.2 %collective-permute-start.5 = (f32[1,256,256]{2,1,0:T(8,128)}, f32[1,256,256]{2,1,0:T(8,128)S(1)}, u32[]{:S(2)}, u32[]{:S(2)}) collective-permute-start(f32[1,256,256]{2,1,0:T(8,128)} %own_ref.1), channel_id=1, source_target_pairs={{2,6},{6,10},{10,14},{14,18},{18,22},{22,26},{26,30}} | collective-permute-start | bytes 786440 | tf_op jit(solution)/shard_map/ppermute | solution.py:484
  2.0 5.5 %collective-permute-start = (s32[1]{0:T(128)}, s32[1]{0:T(128)}, u32[]{:S(2)}, u32[]{:S(2)}) collective-permute-start(s32[1]{0:T(128)} %param.11), channel_id=1, source_target_pairs={{0,2},{2,4},{4,6},{6,8},{8,10},{10,12},{12,14},{14,16},{16,18},{18... | collective-permute-start | bytes 20 | tf_op jit(solution)/shard_map/ppermute | solution.py:484
  5.9 15.1 %copy-start.2 = (f32[1,256,256]{2,1,0:T(8,128)S(1)}, f32[1,256,256]{2,1,0:T(8,128)}, u32[]{:S(2)}) copy-start(f32[1,256,256]{2,1,0:T(8,128)} %own_ref.1) | copy-start | bytes 786436
  7.5 14.9 %copy-start = (bf16[8,256,256]{2,1,0:T(8,128)(2,1)S(1)}, bf16[8,256,256]{2,1,0:T(8,128)(2,1)}, u32[]{:S(2)}) copy-start(bf16[8,256,256]{2,1,0:T(8,128)(2,1)} %constant.2.clone.matrix_ref) | copy-start | bytes 3145732
  7.5 14.9 %copy-start.1 = (f32[2,2,256,256]{3,2,1,0:T(8,128)S(1)}, f32[2,2,256,256]{3,2,1,0:T(8,128)}, u32[]{:S(2)}) copy-start(f32[2,2,256,256]{3,2,1,0:T(8,128)} %own_probe_ref.1) | copy-start | bytes 3145732
  8.6 7.1 %collective-permute-start.3 = (f32[2,128,256]{2,1,0:T(8,128)S(1)}, f32[2,128,256]{2,1,0:T(8,128)S(1)}, u32[]{:S(2)}, u32[]{:S(2)}) collective-permute-start(f32[2,128,256]{2,1,0:T(8,128)S(1)} %shard_map.79), channel_id=1, source_target_pairs={{0,2},{2,0},{4,6},{6,4},{8,10},{10,8},{12,14},{14,12},{16,18},{18,... | collective-permute-start | bytes 786440 | tf_op jit(solution)/shard_map/ppermute | solution.py:484
  11.6 9.3 %collective-permute-start.6 = (f32[1,256,256]{2,1,0:T(8,128)S(1)}, f32[1,256,256]{2,1,0:T(8,128)S(1)}, u32[]{:S(2)}, u32[]{:S(2)}) collective-permute-start(f32[1,256,256]{2,1,0:T(8,128)S(1)} %collective-permute-done.5.received_ref), channel_id=1, source_target_pairs={{0,1},{1,0},{2,3},{3,2},{4,5},{5,4},{6,7},{7,6},{8,9},{9,8},{10,11... | collective-permute-start | bytes 786440 | tf_op jit(solution)/shard_map/ppermute | solution.py:484
  15.7 11.0 %collective-permute-start.4 = (f32[2,128,256]{2,1,0:T(8,128)S(1)}, f32[2,128,256]{2,1,0:T(8,128)S(1)}, u32[]{:S(2)}, u32[]{:S(2)}) collective-permute-start(f32[2,128,256]{2,1,0:T(8,128)S(1)} %collective-permute-done.3.received_ref), channel_id=1, source_target_pairs={{0,1},{1,0},{2,3},{3,2},{4,5},{5,4},{6,7},{7,6},{8,9},{9,8},{10,11... | collective-permute-start | bytes 786440 | tf_op jit(solution)/shard_map/ppermute | solution.py:484
  20.9 1.5 %collective-permute-start.1 = (s32[1]{0:T(128)}, s32[1]{0:T(128)}, u32[]{:S(2)}, u32[]{:S(2)}) collective-permute-start(s32[1]{0:T(128)} %collective-permute-done.received_ref.scan_ref), channel_id=1, source_target_pairs={{0,1},{1,0},{2,3},{3,2},{4,5},{5,4},{6,7},{7,6},{8,9},{9,8},{10,11... | collective-permute-start | bytes 20 | tf_op jit(solution)/shard_map/ppermute | solution.py:484
  30.7 8.1 %collective-permute-start.7 = (f32[264,256]{1,0:T(8,128)S(1)}, f32[264,256]{1,0:T(8,128)S(1)}, u32[]{:S(2)}, u32[]{:S(2)}) collective-permute-start(f32[264,256]{1,0:T(8,128)S(1)} %get-tuple-element.37), channel_id=1, source_target_pairs={{2,0},{0,2},{6,4},{4,6},{10,8},{8,10},{14,12},{12,14},{18,16},{16,... | collective-permute-start | bytes 811016 | tf_op jit(solution)/shard_map/ppermute | solution.py:484
  38.8 5.0 %collective-permute-start.8 = (f32[264,256]{1,0:T(8,128)S(1)}, f32[264,256]{1,0:T(8,128)S(1)}, u32[]{:S(2)}, u32[]{:S(2)}) collective-permute-start(f32[264,256]{1,0:T(8,128)S(1)} %collective-permute-done.7.received_ref), channel_id=1, source_target_pairs={{0,1},{1,0},{2,3},{3,2},{4,5},{5,4},{6,7},{7,6},{8,9},{9,8},{10,11... | collective-permute-start | bytes 811016 | tf_op jit(solution)/shard_map/ppermute | solution.py:484

commit v5 on v4

--- a/solution.py
+++ b/solution.py
@@ -14,7 +14,6 @@
 LANES = 128
 AXES = ("tile", "mode")
 VMEM = pltpu.VMEM
-SMEM = pltpu.SMEM
 
 
 def split(value):
@@ -76,9 +75,13 @@
     return copies
 
 
+def scan_of(ref):
+    return jnp.max(ref[...].astype(jnp.float32)).astype(jnp.int32)
+
+
 def select_kernel(own_scan_ref, scan_ref, table_ref, object_ref, out_ref):
     odd = lax.axis_index("tile") % 2 == 1
-    scan = jnp.where(odd & (lax.axis_index("mode") == 1), own_scan_ref[0], scan_ref[0])
+    scan = jnp.where(odd & (lax.axis_index("mode") == 1), scan_of(own_scan_ref), scan_of(scan_ref))
     _, col = lookup(table_ref, scan)
     low, high = strip_window(object_ref, col)
     out_ref[:, :, :LANES] = low
@@ -88,7 +91,7 @@
 def slots(own_ref, received_ref, swapped_ref):
     first = lax.axis_index("mode") == 0
     odd = lax.axis_index("tile") % 2 == 1
-    own, got, other = own_ref[0], received_ref[0], swapped_ref[0]
+    own, got, other = scan_of(own_ref), scan_of(received_ref), scan_of(swapped_ref)
     above = jnp.where(first, got, other)
     further = jnp.where(first, other, got)
     return jnp.where(odd, further, own), above, jnp.where(odd, own, further)
@@ -147,28 +150,24 @@
 def prepare_kernel(
     scan_ref, received_ref, swapped_ref, table_ref, object_ref, own_probe_ref, other_probe_ref, matrix_ref,
     gradient_ref, probe_ref, window_ref, light_ref, total_ref, strip_ref, place_ref,
-    zero_ref, tall_ref, own_ref, got_ref, other_ref, sems,
+    zero_ref, tall_ref, sems,
 ):
-    pairs = [(scan_ref, own_ref), (received_ref, got_ref), (swapped_ref, other_ref)]
-    scalars = fetch(pairs, sems)
     zero_ref[...] = jnp.zeros_like(zero_ref)
     step = zero_ref.shape[0]
     copies = []
     for part in range(2):
         for at in range(0, object_ref.shape[1], step):
-            copies += fetch([(zero_ref, gradient_ref.at[part, at : at + step])], sems, len(pairs) + len(copies))
+            copies += fetch([(zero_ref, gradient_ref.at[part, at : at + step])], sems, len(copies))
     modes = own_probe_ref.shape[0]
     sources = [ref.at[mode, part] for ref in (own_probe_ref, other_probe_ref) for mode in range(modes) for part in range(2)]
     total = sources[0][...] * sources[0][...]
     for source in sources[1:]:
         total = total + source[...] * source[...]
     total_ref[...] = total
-    for copy in scalars:
-        copy.wait()
     height = object_ref.shape[1]
     tile = lax.axis_index("tile")
     odd = tile % 2
-    scan, _, _ = slots(own_ref, got_ref, other_ref)
+    scan, _, _ = slots(scan_ref, received_ref, swapped_ref)
     row, col = within(table_ref, scan, tile - 2 * odd, height)
     shift = col % LANES
     for index, source in enumerate(sources):
@@ -318,8 +317,7 @@
 def base_kernel(
     place_ref, scan_ref, received_ref, swapped_ref, table_ref, object_ref, keep_ref, light_ref, plain_ref,
     old_gradient_ref,
-    updated_ref, gradient_ref, total_ref, weight_ref, first_ref, second_ref, others_ref, new_ref, tall_ref, turned_ref,
-    own_ref, got_ref, other_ref, sems, fills,
+    updated_ref, gradient_ref, total_ref, weight_ref, first_ref, second_ref, others_ref, new_ref, tall_ref, turned_ref, sems, fills,
 ):
     del old_gradient_ref
     height, breadth = object_ref.shape[1:]
@@ -327,13 +325,10 @@
     core = lax.axis_index("mode")
     fill = pltpu.make_async_copy(object_ref, updated_ref, fills.at[0])
     fill.start()
-    scalars = fetch([(scan_ref, own_ref), (received_ref, got_ref), (swapped_ref, other_ref)], fills, 1)
     total_ref[...] = jnp.zeros_like(total_ref)
     weight_ref[...] = jnp.zeros_like(weight_ref)
-    for copy in scalars:
-        copy.wait()
     odd = tile % 2
-    main, above, third = slots(own_ref, got_ref, other_ref)
+    main, above, third = slots(scan_ref, received_ref, swapped_ref)
     _, col = within(table_ref, main, tile, height)
     live = place_ref[2:3, :1]
     start, stop = place_ref[0:1, :1].astype(jnp.int32), place_ref[1:2, :1].astype(jnp.int32)
@@ -486,13 +481,13 @@
     def step(object_tiles, probe_modes, amplitudes, scan_offsets, slot_scan, slot_count):
         height, breadth = object_tiles.shape[1:]
         modes, _, frame, _ = probe_modes.shape
-        assert slot_scan.shape[0] == 1 and frame == 2 * height and height == LANES
+        assert slot_scan.shape == (1,) and frame == 2 * height and height == LANES
         table = scan_offsets.T
         matrix = jnp.asarray(matrices(frame))
+        slot_scan = slot_scan.reshape(1, 1)
         received_scan = move(slot_scan, up)
         other_probe = move(probe_modes, swap)
         received_amplitude = move(amplitudes, onward)
-        scalar = pltpu.SMEM((1,), jnp.int32)
         staged, table = call(
             stage_kernel,
             (shape(*object_tiles.shape), shape(*table.shape, dtype=jnp.int32)),
@@ -502,12 +497,11 @@
             mebibytes=8,
         )(pltpu.with_memory_space_constraint(object_tiles, pltpu.HBM), pltpu.with_memory_space_constraint(table, pltpu.HBM))
         window = call(
-            select_kernel, shape(2, height, frame), [space(SMEM)] * 2 + [space(VMEM)] * 2, space(VMEM)
+            select_kernel, shape(2, height, frame), [space(VMEM)] * 4, space(VMEM)
         )(slot_scan, received_scan, table, staged)
         received = move(window, gather)
         swapped_scan = move(received_scan, swap)
         swapped_amplitude = move(received_amplitude, swap)
-        scalar = pltpu.SMEM((1,), jnp.int32)
         strip = shape(2 * modes, 2, height, frame)
         whole = shape(2, height, breadth)
         gradient, probe, own_window, light, plain, own_strip, place = call(
@@ -521,15 +515,12 @@
                 strip,
                 shape(8, LANES),
             ),
-            [space(pl.ANY)] * 3 + [space(VMEM)] * 5,
+            [space(VMEM)] * 8,
             [space(pl.ANY)] + [space(VMEM)] * 6,
             [
                 pltpu.VMEM((height // 8, breadth), jnp.float32),
                 pltpu.VMEM((2 * modes, 2, frame // LANES, frame + height, LANES), jnp.float32),
-                scalar,
-                scalar,
-                scalar,
-                pltpu.SemaphoreType.DMA((19,)),
+                pltpu.SemaphoreType.DMA((16,)),
             ],
         )(slot_scan, received_scan, swapped_scan, table, staged, probe_modes, other_probe, matrix)
         swapped = move(received, swap)
@@ -567,17 +558,14 @@
                 shape(height, frame),
                 shape(8, LANES),
             ),
-            [space(VMEM)] + [space(pl.ANY)] * 3 + [space(VMEM)] * 5 + [space(pl.ANY)],
+            [space(VMEM)] * 9 + [space(pl.ANY)],
             [space(pl.ANY)] * 2 + [space(VMEM)] * 5,
             [
                 blocks,
                 pltpu.VMEM((2, frame // LANES, frame + height, LANES), jnp.float32),
                 pltpu.VMEM((2, frame, frame), jnp.float32),
-                scalar,
-                scalar,
-                scalar,
                 semaphores,
-                pltpu.SemaphoreType.DMA((4,)),
+                pltpu.SemaphoreType.DMA((1,)),
             ],
             aliases={9: 1},
         )(place, slot_scan, received_scan, swapped_scan, table, staged, keep, light, plain, gradient)

time: 45.6 us -> 46.5 us (1.020)
  Pallas kernels: 17 us -> 18.1 us
    pallas_call x1, Pallas kernels: 3.61 us -> 4.32 us  [step(): call(prepare_kernel, (whole, shape(2 * modes, 2, frame, frame), shape(2,...]
  transfers between devices with their start and end apart: 9 -> 9, of which waited for: 3 -> 3; matrix products, arithmetic and copies ran while one was open for 0% -> 0% of each run, Pallas kernels for 26% -> 28%
where the time goes in v5:
time: 46.5 us; the launch traced here: 46 us
  starting transfers between devices  18.6 us (40%)
  Pallas kernels  18.1 us (39%)
  waiting for transfers between devices  7.88 us (17%)
  between operations  1.45 us (3%)
    ppermute x9, starting transfers between devices, move(): return lax.ppermute(value, AXES, pairs)  18.6 us
    ppermute x9, waiting for transfers between devices, move(): return lax.ppermute(value, AXES, pairs)  7.88 us
    pallas_call x1, Pallas kernels, step(): call(prepare_kernel, (whole, shape(2 * modes, 2, frame, frame), shape(2,...  4.32 us
    pallas_call x1, Pallas kernels, step(): call(wave_kernel, (shape(2 * height + 8, frame), shape(2, height, frame))...  3.98 us
    pallas_call x1, Pallas kernels, step(): call(base_kernel, (whole, whole, whole, shape(height, breadth), shape(hei...  3.9 us
    pallas_call x1, Pallas kernels, step(): call(stage_kernel, (shape(*object_tiles.shape), shape(*table.shape, dtype...  1.65 us
    pallas_call x1, Pallas kernels, step(): call(second_kernel, (whole, whole), [space(VMEM)] * 8 + [space(pl.ANY)] *...  1.25 us
    pallas_call x1, Pallas kernels, step(): call(first_kernel, (whole, whole), [space(VMEM)] * 6 + [space(pl.ANY)] *...  1.13 us
  transfers between devices with their start and end apart: 9, of which 3 were waited for; matrix products, arithmetic and copies ran while one was open for 0% of the time, Pallas kernels for 28%

profile of v5, /device:TPU:9, one launch (start us, length us, event | category | flops | bytes accessed | tf_op | source)
XLA Modules:
  0.0 46.0 jit_solution(5095927231981304913)
XLA Ops:
  0.6 0.7 %collective-permute-start.2 = (f32[2,2,256,256]{3,2,1,0:T(8,128)}, f32[2,2,256,256]{3,2,1,0:T(8,128)S(1)}, u32[]{:S(2)}, u32[]{:S(2)}) collective-permute-start(f32[2,2,256,256]{3,2,1,0:T(8,128)} %own_probe_ref.1), channel_id=1, source_target_pairs={{0,1},{1,0},{2,3},{3,2},{4,5},{5,4},{6,7},{7,6},{8,9},{9,8},{10,11... | collective-permute-start | bytes 3145736 | tf_op jit(solution)/shard_map/ppermute | solution.py:479
  1.4 0.7 %collective-permute-start.5 = (f32[1,256,256]{2,1,0:T(8,128)}, f32[1,256,256]{2,1,0:T(8,128)S(1)}, u32[]{:S(2)}, u32[]{:S(2)}) collective-permute-start(f32[1,256,256]{2,1,0:T(8,128)} %own_ref.1), channel_id=1, source_target_pairs={{2,6},{6,10},{10,14},{14,18},{18,22},{22,26},{26,30}} | collective-permute-start | bytes 786440 | tf_op jit(solution)/shard_map/ppermute | solution.py:479
  2.0 3.1 %collective-permute-start = (s32[1,1]{1,0:T(1,128)}, s32[1,1]{1,0:T(1,128)}, u32[]{:S(2)}, u32[]{:S(2)}) collective-permute-start(s32[1,1]{1,0:T(1,128)} %bitcast), channel_id=1, source_target_pairs={{0,2},{2,4},{4,6},{6,8},{8,10},{10,12},{12,14},{14,16},{16,18},{18... | collective-permute-start | bytes 20 | tf_op jit(solution)/shard_map/ppermute | solution.py:479
  5.9 0.0 copy-start.2
  5.9 1.7 %shard_map.77 = (f32[2,128,2048]{2,1,0:T(8,128)S(1)}, s32[2,8192]{1,0:T(2,128)S(1)}) custom-call(f32[2,128,2048]{2,1,0:T(8,128)} %object_ref.1, s32[2,8192]{1,0:T(2,128)} %bitcast.5), custom_call_target="tpu_custom_call" | custom-call | flops 5000000 | bytes 5000000 | tf_op jit(solution)/shard_map/pallas_call | solution.py:491
  7.5 0.0 copy-start
  7.5 0.0 copy-start.1
  7.6 0.0 collective-permute-done.received_ref.scan_ref
  7.6 0.9 %shard_map.79 = f32[2,128,256]{2,1,0:T(8,128)S(1)} custom-call(s32[1,1]{1,0:T(1,128)} %bitcast.3.own_scan_ref, s32[1,1]{1,0:T(1,128)} %collective-permute-done.received_ref.scan_ref, s32[2,8192]{1,0:T(2,128)S(1)} %get-tuple-element.22.table_ref, f32[2,128,2048]{2,1,0:T(8,128)S(1)} %get-tuple-element.23.object_ref), custom_call_target="tpu_custom_call" | custom-call | flops 5000000 | bytes 5000000 | tf_op jit(solution)/shard_map/pallas_call | solution.py:499
  8.5 3.0 %collective-permute-start.3 = (f32[2,128,256]{2,1,0:T(8,128)S(1)}, f32[2,128,256]{2,1,0:T(8,128)S(1)}, u32[]{:S(2)}, u32[]{:S(2)}) collective-permute-start(f32[2,128,256]{2,1,0:T(8,128)S(1)} %shard_map.79), channel_id=1, source_target_pairs={{0,2},{2,0},{4,6},{6,4},{8,10},{10,8},{12,14},{14,12},{16,18},{18,... | collective-permute-start | bytes 786440 | tf_op jit(solution)/shard_map/ppermute | solution.py:479
  11.5 0.0 collective-permute-done.5.received_ref
  11.6 3.2 %collective-permute-start.6 = (f32[1,256,256]{2,1,0:T(8,128)S(1)}, f32[1,256,256]{2,1,0:T(8,128)S(1)}, u32[]{:S(2)}, u32[]{:S(2)}) collective-permute-start(f32[1,256,256]{2,1,0:T(8,128)S(1)} %collective-permute-done.5.received_ref), channel_id=1, source_target_pairs={{0,1},{1,0},{2,3},{3,2},{4,5},{5,4},{6,7},{7,6},{8,9},{9,8},{10,11... | collective-permute-start | bytes 786440 | tf_op jit(solution)/shard_map/ppermute | solution.py:479
  14.8 0.8 %collective-permute-done.3.received_ref = f32[2,128,256]{2,1,0:T(8,128)S(1)} collective-permute-done((f32[2,128,256]{2,1,0:T(8,128)S(1)}, f32[2,128,256]{2,1,0:T(8,128)S(1)}, u32[]{:S(2)}, u32[]{:S(2)}) %collective-permute-start.3) | collective-permute-done | bytes 262176 | tf_op jit(solution)/shard_map/ppermute | solution.py:479
  15.6 5.2 %collective-permute-start.4 = (f32[2,128,256]{2,1,0:T(8,128)S(1)}, f32[2,128,256]{2,1,0:T(8,128)S(1)}, u32[]{:S(2)}, u32[]{:S(2)}) collective-permute-start(f32[2,128,256]{2,1,0:T(8,128)S(1)} %collective-permute-done.3.received_ref), channel_id=1, source_target_pairs={{0,1},{1,0},{2,3},{3,2},{4,5},{5,4},{6,7},{7,6},{8,9},{9,8},{10,11... | collective-permute-start | bytes 786440 | tf_op jit(solution)/shard_map/ppermute | solution.py:479
  20.9 0.0 collective-permute-start.1
  20.9 0.0 collective-permute-done.6.swapped_ref
  20.9 0.0 copy-done.2
  20.9 0.3 shard_map.81.amplitude_ref
  21.2 1.0 %collective-permute-done.1.swapped_ref = s32[1,1]{1,0:T(1,128)} collective-permute-done((s32[1,1]{1,0:T(1,128)}, s32[1,1]{1,0:T(1,128)}, u32[]{:S(2)}, u32[]{:S(2)}) %collective-permute-start.1) | collective-permute-done | bytes 36 | tf_op jit(solution)/shard_map/ppermute | solution.py:479
  22.2 0.0 collective-permute-done.2.other_probe_ref
  22.2 0.0 copy-done
  22.2 4.3 %shard_map.78 = (f32[2,128,2048]{2,1,0:T(8,128)}, f32[4,2,256,256]{3,2,1,0:T(8,128)S(1)}, f32[2,128,256]{2,1,0:T(8,128)S(1)}, f32[256,256]{1,0:T(8,128)S(1)}, f3...) custom-call(s32[1,1]{1,0:T(1,128)} %bitcast.2.scan_ref, ...), custom_call_target="tpu_custom_call" | custom-call | flops 5000000 | bytes 5000000 | tf_op jit(solution)/shard_map/pallas_call | solution.py:507
  26.6 0.6 %shard_map.80.first_ref = f32[4,2,128,256]{3,2,1,0:T(8,128)S(1)} custom-call(f32[2,128,256]{2,1,0:T(8,128)S(1)} %collective-permute-done.3.received_ref, f32[4,2,256,256]{3,2,1,0:T(8,128)S(1)} %get-tuple-element.27.probe_ref, bf16[8,256,256]{2,1,0:T(8,128)(2,1)S(1)} %copy-done), custom_call_target="tpu_custom_call" | custom-call | flops 5000000 | bytes 5000000 | tf_op jit(solution)/shard_map/pallas_call | solution.py:534
  27.2 0.0 collective-permute-done.4.swapped_ref
  27.2 4.0 %shard_map.82 = (f32[264,256]{1,0:T(8,128)S(1)}, f32[2,128,256]{2,1,0:T(8,128)S(1)}) custom-call(f32[8,128]{1,0:T(8,128)S(1)} %get-tuple-element.24.place_ref, f32[2,128,256]{2,1,0:T(8,128)S(1)} %get-tuple-element.25.window_ref, f32[2,128,256]{2,1,0:T(8,128)S(1)} %collective-permute-done.3.received_ref, ...), custom_call_target="tpu_custom_call" | custom-call | flops 5000000 | bytes 5000000 | tf_op jit(solution)/shard_map/pallas_call | solution.py:535
  31.2 2.1 %collective-permute-start.7 = (f32[264,256]{1,0:T(8,128)S(1)}, f32[264,256]{1,0:T(8,128)S(1)}, u32[]{:S(2)}, u32[]{:S(2)}) collective-permute-start(f32[264,256]{1,0:T(8,128)S(1)} %get-tuple-element.37), channel_id=1, source_target_pairs={{2,0},{0,2},{6,4},{4,6},{10,8},{8,10},{14,12},{12,14},{18,16},{16,... | collective-permute-start | bytes 811016 | tf_op jit(solution)/shard_map/ppermute | solution.py:479
  33.3 6.0 %collective-permute-done.7.received_ref = f32[264,256]{1,0:T(8,128)S(1)} collective-permute-done((f32[264,256]{1,0:T(8,128)S(1)}, f32[264,256]{1,0:T(8,128)S(1)}, u32[]{:S(2)}, u32[]{:S(2)}) %collective-permute-start.7) | collective-permute-done | bytes 270368 | tf_op jit(solution)/shard_map/ppermute | solution.py:479
  39.3 0.4 collective-permute-start.8
  39.7 3.9 %shard_map.83 = (f32[2,128,2048]{2,1,0:T(8,128)}, f32[2,128,2048]{2,1,0:T(8,128)}, f32[2,128,2048]{2,1,0:T(8,128)S(1)}, f32[128,2048]{1,0:T(8,128)S(1)}, f32[128...) custom-call(f32[8,128]{1,0:T(8,128)S(1)} %get-tuple-element.24.place_ref, ...), custom_call_target="tpu_custom_call", output_to_operand_aliasing={{1}: (9, {})} | custom-call | flops 5000000 | bytes 5000000 | tf_op jit(solution)/shard_map/pallas_call | solution.py:550
  43.6 1.1 %shard_map.84 = (f32[2,128,2048]{2,1,0:T(8,128)}, f32[2,128,2048]{2,1,0:T(8,128)}) custom-call(f32[8,128]{1,0:T(8,128)S(1)} %get-tuple-element.32.others_ref, f32[2,128,2048]{2,1,0:T(8,128)S(1)} %get-tuple-element.23.object_ref, f32[2,128,2048]{2,1,0:T(8,128)S(1)} %get-tuple-element.33.total_ref, ...), custom_call_target="tpu_custom_call", output_to_operand_aliasing={{0}: (6, {}), {1}: (7, {})} | custom-call | flops 5000000 | bytes 5000000 | tf_op jit(solution)/shard_map/pallas_call | solution.py:573
  44.8 0.0 collective-permute-done.8.swapped_ref
  44.8 1.2 %shard_map.85 = (f32[2,128,2048]{2,1,0:T(8,128)}, f32[2,128,2048]{2,1,0:T(8,128)}) custom-call(f32[8,128]{1,0:T(8,128)S(1)} %get-tuple-element.32.others_ref, f32[2,128,2048]{2,1,0:T(8,128)S(1)} %get-tuple-element.23.object_ref, f32[2,128,2048]{2,1,0:T(8,128)S(1)} %get-tuple-element.33.total_ref, ...), custom_call_target="tpu_custom_call", output_to_operand_aliasing={{0}: (8, {}), {1}: (9, {})} | custom-call | flops 5000000 | bytes 5000000 | tf_op jit(solution)/shard_map/pallas_call | solution.py:581
  (1 shorter events, 0.0 us)
Async XLA Ops:
  0.6 21.6 %collective-permute-start.2 = (f32[2,2,256,256]{3,2,1,0:T(8,128)}, f32[2,2,256,256]{3,2,1,0:T(8,128)S(1)}, u32[]{:S(2)}, u32[]{:S(2)}) collective-permute-start(f32[2,2,256,256]{3,2,1,0:T(8,128)} %own_probe_ref.1), channel_id=1, source_target_pairs={{0,1},{1,0},{2,3},{3,2},{4,5},{5,4},{6,7},{7,6},{8,9},{9,8},{10,11... | collective-permute-start | bytes 3145736 | tf_op jit(solution)/shard_map/ppermute | solution.py:479
  1.4 10.2 %collective-permute-start.5 = (f32[1,256,256]{2,1,0:T(8,128)}, f32[1,256,256]{2,1,0:T(8,128)S(1)}, u32[]{:S(2)}, u32[]{:S(2)}) collective-permute-start(f32[1,256,256]{2,1,0:T(8,128)} %own_ref.1), channel_id=1, source_target_pairs={{2,6},{6,10},{10,14},{14,18},{18,22},{22,26},{26,30}} | collective-permute-start | bytes 786440 | tf_op jit(solution)/shard_map/ppermute | solution.py:479
  2.0 5.5 %collective-permute-start = (s32[1,1]{1,0:T(1,128)}, s32[1,1]{1,0:T(1,128)}, u32[]{:S(2)}, u32[]{:S(2)}) collective-permute-start(s32[1,1]{1,0:T(1,128)} %bitcast), channel_id=1, source_target_pairs={{0,2},{2,4},{4,6},{6,8},{8,10},{10,12},{12,14},{14,16},{16,18},{18... | collective-permute-start | bytes 20 | tf_op jit(solution)/shard_map/ppermute | solution.py:479
  5.9 15.0 %copy-start.2 = (f32[1,256,256]{2,1,0:T(8,128)S(1)}, f32[1,256,256]{2,1,0:T(8,128)}, u32[]{:S(2)}) copy-start(f32[1,256,256]{2,1,0:T(8,128)} %own_ref.1) | copy-start | bytes 786436
  7.5 14.7 %copy-start = (bf16[8,256,256]{2,1,0:T(8,128)(2,1)S(1)}, bf16[8,256,256]{2,1,0:T(8,128)(2,1)}, u32[]{:S(2)}) copy-start(bf16[8,256,256]{2,1,0:T(8,128)(2,1)} %constant.2.clone.matrix_ref) | copy-start | bytes 3145732
  7.5 14.7 %copy-start.1 = (f32[2,2,256,256]{3,2,1,0:T(8,128)S(1)}, f32[2,2,256,256]{3,2,1,0:T(8,128)}, u32[]{:S(2)}) copy-start(f32[2,2,256,256]{3,2,1,0:T(8,128)} %own_probe_ref.1) | copy-start | bytes 3145732
  8.5 7.1 %collective-permute-start.3 = (f32[2,128,256]{2,1,0:T(8,128)S(1)}, f32[2,128,256]{2,1,0:T(8,128)S(1)}, u32[]{:S(2)}, u32[]{:S(2)}) collective-permute-start(f32[2,128,256]{2,1,0:T(8,128)S(1)} %shard_map.79), channel_id=1, source_target_pairs={{0,2},{2,0},{4,6},{6,4},{8,10},{10,8},{12,14},{14,12},{16,18},{18,... | collective-permute-start | bytes 786440 | tf_op jit(solution)/shard_map/ppermute | solution.py:479
  11.6 9.3 %collective-permute-start.6 = (f32[1,256,256]{2,1,0:T(8,128)S(1)}, f32[1,256,256]{2,1,0:T(8,128)S(1)}, u32[]{:S(2)}, u32[]{:S(2)}) collective-permute-start(f32[1,256,256]{2,1,0:T(8,128)S(1)} %collective-permute-done.5.received_ref), channel_id=1, source_target_pairs={{0,1},{1,0},{2,3},{3,2},{4,5},{5,4},{6,7},{7,6},{8,9},{9,8},{10,11... | collective-permute-start | bytes 786440 | tf_op jit(solution)/shard_map/ppermute | solution.py:479
  15.6 11.6 %collective-permute-start.4 = (f32[2,128,256]{2,1,0:T(8,128)S(1)}, f32[2,128,256]{2,1,0:T(8,128)S(1)}, u32[]{:S(2)}, u32[]{:S(2)}) collective-permute-start(f32[2,128,256]{2,1,0:T(8,128)S(1)} %collective-permute-done.3.received_ref), channel_id=1, source_target_pairs={{0,1},{1,0},{2,3},{3,2},{4,5},{5,4},{6,7},{7,6},{8,9},{9,8},{10,11... | collective-permute-start | bytes 786440 | tf_op jit(solution)/shard_map/ppermute | solution.py:479
  20.9 1.4 %collective-permute-start.1 = (s32[1,1]{1,0:T(1,128)}, s32[1,1]{1,0:T(1,128)}, u32[]{:S(2)}, u32[]{:S(2)}) collective-permute-start(s32[1,1]{1,0:T(1,128)} %collective-permute-done.received_ref.scan_ref), channel_id=1, source_target_pairs={{0,1},{1,0},{2,3},{3,2},{4,5},{5,4},{6,7},{7,6},{8,9},{9,8},{10,11... | collective-permute-start | bytes 20 | tf_op jit(solution)/shard_map/ppermute | solution.py:479
  31.2 8.1 %collective-permute-start.7 = (f32[264,256]{1,0:T(8,128)S(1)}, f32[264,256]{1,0:T(8,128)S(1)}, u32[]{:S(2)}, u32[]{:S(2)}) collective-permute-start(f32[264,256]{1,0:T(8,128)S(1)} %get-tuple-element.37), channel_id=1, source_target_pairs={{2,0},{0,2},{6,4},{4,6},{10,8},{8,10},{14,12},{12,14},{18,16},{16,... | collective-permute-start | bytes 811016 | tf_op jit(solution)/shard_map/ppermute | solution.py:479
  39.3 5.5 %collective-permute-start.8 = (f32[264,256]{1,0:T(8,128)S(1)}, f32[264,256]{1,0:T(8,128)S(1)}, u32[]{:S(2)}, u32[]{:S(2)}) collective-permute-start(f32[264,256]{1,0:T(8,128)S(1)} %collective-permute-done.7.received_ref), channel_id=1, source_target_pairs={{0,1},{1,0},{2,3},{3,2},{4,5},{5,4},{6,7},{7,6},{8,9},{9,8},{10,11... | collective-permute-start | bytes 811016 | tf_op jit(solution)/shard_map/ppermute | solution.py:479

commit v6 on v4

--- a/solution.py
+++ b/solution.py
@@ -145,8 +145,8 @@
 
 
 def prepare_kernel(
-    scan_ref, received_ref, swapped_ref, table_ref, object_ref, own_probe_ref, other_probe_ref, matrix_ref,
-    gradient_ref, probe_ref, window_ref, light_ref, total_ref, strip_ref, place_ref,
+    scan_ref, received_ref, swapped_ref, table_ref, object_ref, own_probe_ref, other_probe_ref,
+    gradient_ref, probe_ref, window_ref, light_ref, total_ref, place_ref,
     zero_ref, tall_ref, own_ref, got_ref, other_ref, sems,
 ):
     pairs = [(scan_ref, own_ref), (received_ref, got_ref), (swapped_ref, other_ref)]
@@ -180,7 +180,6 @@
     window_ref[:, :, LANES:] = high
     live = jnp.where(odd == 1, (tile >= 2).astype(jnp.int32), 1)
     keep_scalars(place_ref, (jnp.where(odd == 1, 0, row), jnp.where(odd == 1, row, height), live))
-    transform_rows(probe_ref, 0, window_ref, matrix_ref, strip_ref)
     for copy in copies:
         copy.wait()
 
@@ -228,9 +227,10 @@
         out_ref[mode, 1] = jnp.concatenate([even[at, half:], odd[at, half:]], axis=1)
 
 
-def strip_kernel(received_ref, probe_ref, matrix_ref, out_ref):
+def strip_kernel(own_ref, received_ref, probe_ref, matrix_ref, own_out_ref, out_ref):
     height = received_ref.shape[1]
     start = pl.multiple_of((1 - lax.axis_index("mode")) * height, height)
+    transform_rows(probe_ref, 0, own_ref, matrix_ref, own_out_ref)
     transform_rows(probe_ref, start, received_ref, matrix_ref, out_ref)
 
 
@@ -510,7 +510,7 @@
         scalar = pltpu.SMEM((1,), jnp.int32)
         strip = shape(2 * modes, 2, height, frame)
         whole = shape(2, height, breadth)
-        gradient, probe, own_window, light, plain, own_strip, place = call(
+        gradient, probe, own_window, light, plain, place = call(
             prepare_kernel,
             (
                 whole,
@@ -518,11 +518,10 @@
                 shape(2, height, frame),
                 shape(frame, frame),
                 shape(frame, frame),
-                strip,
                 shape(8, LANES),
             ),
-            [space(pl.ANY)] * 3 + [space(VMEM)] * 5,
-            [space(pl.ANY)] + [space(VMEM)] * 6,
+            [space(pl.ANY)] * 3 + [space(VMEM)] * 4,
+            [space(pl.ANY)] + [space(VMEM)] * 5,
             [
                 pltpu.VMEM((height // 8, breadth), jnp.float32),
                 pltpu.VMEM((2 * modes, 2, frame // LANES, frame + height, LANES), jnp.float32),
@@ -531,7 +530,7 @@
                 scalar,
                 pltpu.SemaphoreType.DMA((19,)),
             ],
-        )(slot_scan, received_scan, swapped_scan, table, staged, probe_modes, other_probe, matrix)
+        )(slot_scan, received_scan, swapped_scan, table, staged, probe_modes, other_probe)
         swapped = move(received, swap)
         amplitude = call(
             reorder_kernel,
@@ -540,7 +539,9 @@
             space(VMEM),
             [pltpu.VMEM((frame // LANES, frame, LANES), jnp.float32)],
         )(amplitudes, received_amplitude, swapped_amplitude)
-        first_strip = call(strip_kernel, strip, [space(VMEM)] * 3, space(VMEM))(received, probe, matrix)
+        own_strip, first_strip = call(strip_kernel, (strip, strip), [space(VMEM)] * 4, [space(VMEM)] * 2)(
+            own_window, received, probe, matrix
+        )
         send, keep = call(
             wave_kernel,
             (shape(2 * height + 8, frame), shape(2, height, frame)),

time: 45.6 us -> 45.1 us (0.989)
    pallas_call x1, Pallas kernels: 3.61 us -> 3 us  [step(): call(prepare_kernel, (whole, shape(2 * modes, 2, frame, frame), shape(2,...]
where the time goes in v6:
time: 45.1 us; the launch traced here: 44.6 us
  starting transfers between devices  18.7 us (41%)
  Pallas kernels  16.6 us (37%)
  waiting for transfers between devices  7.87 us (17%)
  between operations  1.45 us (3%)
    ppermute x9, starting transfers between devices, move(): return lax.ppermute(value, AXES, pairs)  18.7 us
    ppermute x9, waiting for transfers between devices, move(): return lax.ppermute(value, AXES, pairs)  7.87 us
    pallas_call x1, Pallas kernels, step(): call(wave_kernel, (shape(2 * height + 8, frame), shape(2, height, frame))...  3.84 us
    pallas_call x1, Pallas kernels, step(): call(base_kernel, (whole, whole, whole, shape(height, breadth), shape(hei...  3.5 us
    pallas_call x1, Pallas kernels, step(): call(prepare_kernel, (whole, shape(2 * modes, 2, frame, frame), shape(2,...  3 us
    pallas_call x1, Pallas kernels, step(): call(stage_kernel, (shape(*object_tiles.shape), shape(*table.shape, dtype...  1.65 us
    pallas_call x1, Pallas kernels, step(): call(second_kernel, (whole, whole), [space(VMEM)] * 8 + [space(pl.ANY)] *...  1.25 us
    pallas_call x1, Pallas kernels, step(): call(first_kernel, (whole, whole), [space(VMEM)] * 6 + [space(pl.ANY)] *...  1.13 us
  transfers between devices with their start and end apart: 9, of which 3 were waited for; matrix products, arithmetic and copies ran while one was open for 0% of the time, Pallas kernels for 26%

profile of v6, /device:TPU:9, one launch (start us, length us, event | category | flops | bytes accessed | tf_op | source)
XLA Modules:
  0.0 44.6 jit_solution(2360184445969557767)
XLA Ops:
  0.6 0.7 %collective-permute-start.2 = (f32[2,2,256,256]{3,2,1,0:T(8,128)}, f32[2,2,256,256]{3,2,1,0:T(8,128)S(1)}, u32[]{:S(2)}, u32[]{:S(2)}) collective-permute-start(f32[2,2,256,256]{3,2,1,0:T(8,128)} %own_probe_ref.1), channel_id=1, source_target_pairs={{0,1},{1,0},{2,3},{3,2},{4,5},{5,4},{6,7},{7,6},{8,9},{9,8},{10,11... | collective-permute-start | bytes 3145736 | tf_op jit(solution)/shard_map/ppermute | solution.py:484
  1.4 0.7 %collective-permute-start.5 = (f32[1,256,256]{2,1,0:T(8,128)}, f32[1,256,256]{2,1,0:T(8,128)S(1)}, u32[]{:S(2)}, u32[]{:S(2)}) collective-permute-start(f32[1,256,256]{2,1,0:T(8,128)} %own_ref.1), channel_id=1, source_target_pairs={{2,6},{6,10},{10,14},{14,18},{18,22},{22,26},{26,30}} | collective-permute-start | bytes 786440 | tf_op jit(solution)/shard_map/ppermute | solution.py:484
  2.0 3.1 %collective-permute-start = (s32[1]{0:T(128)}, s32[1]{0:T(128)}, u32[]{:S(2)}, u32[]{:S(2)}) collective-permute-start(s32[1]{0:T(128)} %param.11), channel_id=1, source_target_pairs={{0,2},{2,4},{4,6},{6,8},{8,10},{10,12},{12,14},{14,16},{16,18},{18... | collective-permute-start | bytes 20 | tf_op jit(solution)/shard_map/ppermute | solution.py:484
  5.9 0.0 copy-start.2
  5.9 1.7 %shard_map.77 = (f32[2,128,2048]{2,1,0:T(8,128)S(1)}, s32[2,8192]{1,0:T(2,128)S(1)}) custom-call(f32[2,128,2048]{2,1,0:T(8,128)} %object_ref.1, s32[2,8192]{1,0:T(2,128)} %bitcast.1), custom_call_target="tpu_custom_call" | custom-call | flops 5000000 | bytes 5000000 | tf_op jit(solution)/shard_map/pallas_call | solution.py:496
  7.5 0.0 copy-start.1
  7.5 0.0 collective-permute-done.received_ref.scan_ref
  7.6 0.8 %shard_map.79 = f32[2,128,256]{2,1,0:T(8,128)S(1)} custom-call(s32[1]{0:T(128)S(6)} %copy.18.scan_ref.own_scan_ref, s32[1]{0:T(128)} %collective-permute-done.received_ref.scan_ref, s32[2,8192]{1,0:T(2,128)S(1)} %get-tuple-element.23.table_ref, f32[2,128,2048]{2,1,0:T(8,128)S(1)} %get-tuple-element.24.object_ref), custom_call_target="tpu_custom_call" | custom-call | flops 5000000 | bytes 5000000 | tf_op jit(solution)/shard_map/pallas_call | solution.py:504
  8.4 3.0 %collective-permute-start.3 = (f32[2,128,256]{2,1,0:T(8,128)S(1)}, f32[2,128,256]{2,1,0:T(8,128)S(1)}, u32[]{:S(2)}, u32[]{:S(2)}) collective-permute-start(f32[2,128,256]{2,1,0:T(8,128)S(1)} %shard_map.79), channel_id=1, source_target_pairs={{0,2},{2,0},{4,6},{6,4},{8,10},{10,8},{12,14},{14,12},{16,18},{18,... | collective-permute-start | bytes 786440 | tf_op jit(solution)/shard_map/ppermute | solution.py:484
  11.4 0.0 collective-permute-done.5.received_ref
  11.5 3.3 %collective-permute-start.6 = (f32[1,256,256]{2,1,0:T(8,128)S(1)}, f32[1,256,256]{2,1,0:T(8,128)S(1)}, u32[]{:S(2)}, u32[]{:S(2)}) collective-permute-start(f32[1,256,256]{2,1,0:T(8,128)S(1)} %collective-permute-done.5.received_ref), channel_id=1, source_target_pairs={{0,1},{1,0},{2,3},{3,2},{4,5},{5,4},{6,7},{7,6},{8,9},{9,8},{10,11... | collective-permute-start | bytes 786440 | tf_op jit(solution)/shard_map/ppermute | solution.py:484
  14.8 0.8 %collective-permute-done.3.received_ref = f32[2,128,256]{2,1,0:T(8,128)S(1)} collective-permute-done((f32[2,128,256]{2,1,0:T(8,128)S(1)}, f32[2,128,256]{2,1,0:T(8,128)S(1)}, u32[]{:S(2)}, u32[]{:S(2)}) %collective-permute-start.3) | collective-permute-done | bytes 262176 | tf_op jit(solution)/shard_map/ppermute | solution.py:484
  15.5 5.3 %collective-permute-start.4 = (f32[2,128,256]{2,1,0:T(8,128)S(1)}, f32[2,128,256]{2,1,0:T(8,128)S(1)}, u32[]{:S(2)}, u32[]{:S(2)}) collective-permute-start(f32[2,128,256]{2,1,0:T(8,128)S(1)} %collective-permute-done.3.received_ref), channel_id=1, source_target_pairs={{0,1},{1,0},{2,3},{3,2},{4,5},{5,4},{6,7},{7,6},{8,9},{9,8},{10,11... | collective-permute-start | bytes 786440 | tf_op jit(solution)/shard_map/ppermute | solution.py:484
  20.8 0.0 collective-permute-start.1
  20.8 0.0 collective-permute-done.6.swapped_ref
  20.8 0.0 copy-done.2
  20.8 0.3 shard_map.81.amplitude_ref
  21.1 0.0 copy-start
  21.2 1.0 %collective-permute-done.1.swapped_ref = s32[1]{0:T(128)} collective-permute-done((s32[1]{0:T(128)}, s32[1]{0:T(128)}, u32[]{:S(2)}, u32[]{:S(2)}) %collective-permute-start.1) | collective-permute-done | bytes 36 | tf_op jit(solution)/shard_map/ppermute | solution.py:484
  22.2 0.0 collective-permute-done.2.other_probe_ref
  22.2 0.0 copy-done.1
  22.2 3.0 %shard_map.78 = (f32[2,128,2048]{2,1,0:T(8,128)}, f32[4,2,256,256]{3,2,1,0:T(8,128)S(1)}, f32[2,128,256]{2,1,0:T(8,128)S(1)}, f32[256,256]{1,0:T(8,128)S(1)}, f3...) custom-call(s32[1]{0:T(128)S(6)} %copy.18.scan_ref.own_scan_ref, s32[1]{0:T(128)} %collective-permute-done.received_ref.scan_ref, ...), custom_call_target="tpu_custom_call" | custom-call | flops 5000000 | bytes 5000000 | tf_op jit(solution)/shard_map/pallas_call | solution.py:513
  25.2 1.1 %shard_map.80 = (f32[4,2,128,256]{3,2,1,0:T(8,128)S(1)}, f32[4,2,128,256]{3,2,1,0:T(8,128)S(1)}) custom-call(f32[2,128,256]{2,1,0:T(8,128)S(1)} %get-tuple-element.26.own_ref.window_ref, f32[2,128,256]{2,1,0:T(8,128)S(1)} %collective-permute-done.3.received_ref, f32[4,2,256,256]{3,2,1,0:T(8,128)S(1)} %get-tuple-element.27.probe_ref, ...), custom_call_target="tpu_custom_call" | custom-call | flops 5000000 | bytes 5000000 | tf_op jit(solution)/shard_map/pallas_call | solution.py:542
  26.3 0.0 collective-permute-done.4.swapped_ref
  26.3 3.8 %shard_map.82 = (f32[264,256]{1,0:T(8,128)S(1)}, f32[2,128,256]{2,1,0:T(8,128)S(1)}) custom-call(f32[8,128]{1,0:T(8,128)S(1)} %get-tuple-element.25.place_ref, f32[2,128,256]{2,1,0:T(8,128)S(1)} %get-tuple-element.26.own_ref.window_ref, f32[2,128,256]{2,1,0:T(8,128)S(1)} %collective-permute-done.3.received_ref, ...), custom_call_target="tpu_custom_call" | custom-call | flops 5000000 | bytes 5000000 | tf_op jit(solution)/shard_map/pallas_call | solution.py:545
  30.2 2.0 %collective-permute-start.7 = (f32[264,256]{1,0:T(8,128)S(1)}, f32[264,256]{1,0:T(8,128)S(1)}, u32[]{:S(2)}, u32[]{:S(2)}) collective-permute-start(f32[264,256]{1,0:T(8,128)S(1)} %get-tuple-element.39), channel_id=1, source_target_pairs={{2,0},{0,2},{6,4},{4,6},{10,8},{8,10},{14,12},{12,14},{18,16},{16,... | collective-permute-start | bytes 811016 | tf_op jit(solution)/shard_map/ppermute | solution.py:484
  32.2 6.1 %collective-permute-done.7.received_ref = f32[264,256]{1,0:T(8,128)S(1)} collective-permute-done((f32[264,256]{1,0:T(8,128)S(1)}, f32[264,256]{1,0:T(8,128)S(1)}, u32[]{:S(2)}, u32[]{:S(2)}) %collective-permute-start.7) | collective-permute-done | bytes 270368 | tf_op jit(solution)/shard_map/ppermute | solution.py:484
  38.3 0.4 collective-permute-start.8
  38.7 3.5 %shard_map.83 = (f32[2,128,2048]{2,1,0:T(8,128)}, f32[2,128,2048]{2,1,0:T(8,128)}, f32[2,128,2048]{2,1,0:T(8,128)S(1)}, f32[128,2048]{1,0:T(8,128)S(1)}, f32[128...) custom-call(f32[8,128]{1,0:T(8,128)S(1)} %get-tuple-element.25.place_ref, ...), custom_call_target="tpu_custom_call", output_to_operand_aliasing={{1}: (9, {})} | custom-call | flops 5000000 | bytes 5000000 | tf_op jit(solution)/shard_map/pallas_call | solution.py:560
  42.2 1.1 %shard_map.84 = (f32[2,128,2048]{2,1,0:T(8,128)}, f32[2,128,2048]{2,1,0:T(8,128)}) custom-call(f32[8,128]{1,0:T(8,128)S(1)} %get-tuple-element.34.others_ref, f32[2,128,2048]{2,1,0:T(8,128)S(1)} %get-tuple-element.24.object_ref, f32[2,128,2048]{2,1,0:T(8,128)S(1)} %get-tuple-element.35.total_ref, ...), custom_call_target="tpu_custom_call", output_to_operand_aliasing={{0}: (6, {}), {1}: (7, {})} | custom-call | flops 5000000 | bytes 5000000 | tf_op jit(solution)/shard_map/pallas_call | solution.py:586
  43.3 0.0 collective-permute-done.8.swapped_ref
  43.4 1.2 %shard_map.85 = (f32[2,128,2048]{2,1,0:T(8,128)}, f32[2,128,2048]{2,1,0:T(8,128)}) custom-call(f32[8,128]{1,0:T(8,128)S(1)} %get-tuple-element.34.others_ref, f32[2,128,2048]{2,1,0:T(8,128)S(1)} %get-tuple-element.24.object_ref, f32[2,128,2048]{2,1,0:T(8,128)S(1)} %get-tuple-element.35.total_ref, ...), custom_call_target="tpu_custom_call", output_to_operand_aliasing={{0}: (8, {}), {1}: (9, {})} | custom-call | flops 5000000 | bytes 5000000 | tf_op jit(solution)/shard_map/pallas_call | solution.py:594
  (1 shorter events, 0.0 us)
Async XLA Ops:
  0.6 21.6 %collective-permute-start.2 = (f32[2,2,256,256]{3,2,1,0:T(8,128)}, f32[2,2,256,256]{3,2,1,0:T(8,128)S(1)}, u32[]{:S(2)}, u32[]{:S(2)}) collective-permute-start(f32[2,2,256,256]{3,2,1,0:T(8,128)} %own_probe_ref.1), channel_id=1, source_target_pairs={{0,1},{1,0},{2,3},{3,2},{4,5},{5,4},{6,7},{7,6},{8,9},{9,8},{10,11... | collective-permute-start | bytes 3145736 | tf_op jit(solution)/shard_map/ppermute | solution.py:484
  1.4 10.1 %collective-permute-start.5 = (f32[1,256,256]{2,1,0:T(8,128)}, f32[1,256,256]{2,1,0:T(8,128)S(1)}, u32[]{:S(2)}, u32[]{:S(2)}) collective-permute-start(f32[1,256,256]{2,1,0:T(8,128)} %own_ref.1), channel_id=1, source_target_pairs={{2,6},{6,10},{10,14},{14,18},{18,22},{22,26},{26,30}} | collective-permute-start | bytes 786440 | tf_op jit(solution)/shard_map/ppermute | solution.py:484
  2.0 5.5 %collective-permute-start = (s32[1]{0:T(128)}, s32[1]{0:T(128)}, u32[]{:S(2)}, u32[]{:S(2)}) collective-permute-start(s32[1]{0:T(128)} %param.11), channel_id=1, source_target_pairs={{0,2},{2,4},{4,6},{6,8},{8,10},{10,12},{12,14},{14,16},{16,18},{18... | collective-permute-start | bytes 20 | tf_op jit(solution)/shard_map/ppermute | solution.py:484
  5.9 15.0 %copy-start.2 = (f32[1,256,256]{2,1,0:T(8,128)S(1)}, f32[1,256,256]{2,1,0:T(8,128)}, u32[]{:S(2)}) copy-start(f32[1,256,256]{2,1,0:T(8,128)} %own_ref.1) | copy-start | bytes 786436
  7.5 14.7 %copy-start.1 = (f32[2,2,256,256]{3,2,1,0:T(8,128)S(1)}, f32[2,2,256,256]{3,2,1,0:T(8,128)}, u32[]{:S(2)}) copy-start(f32[2,2,256,256]{3,2,1,0:T(8,128)} %own_probe_ref.1) | copy-start | bytes 3145732
  8.4 7.1 %collective-permute-start.3 = (f32[2,128,256]{2,1,0:T(8,128)S(1)}, f32[2,128,256]{2,1,0:T(8,128)S(1)}, u32[]{:S(2)}, u32[]{:S(2)}) collective-permute-start(f32[2,128,256]{2,1,0:T(8,128)S(1)} %shard_map.79), channel_id=1, source_target_pairs={{0,2},{2,0},{4,6},{6,4},{8,10},{10,8},{12,14},{14,12},{16,18},{18,... | collective-permute-start | bytes 786440 | tf_op jit(solution)/shard_map/ppermute | solution.py:484
  11.5 9.4 %collective-permute-start.6 = (f32[1,256,256]{2,1,0:T(8,128)S(1)}, f32[1,256,256]{2,1,0:T(8,128)S(1)}, u32[]{:S(2)}, u32[]{:S(2)}) collective-permute-start(f32[1,256,256]{2,1,0:T(8,128)S(1)} %collective-permute-done.5.received_ref), channel_id=1, source_target_pairs={{0,1},{1,0},{2,3},{3,2},{4,5},{5,4},{6,7},{7,6},{8,9},{9,8},{10,11... | collective-permute-start | bytes 786440 | tf_op jit(solution)/shard_map/ppermute | solution.py:484
  15.5 10.8 %collective-permute-start.4 = (f32[2,128,256]{2,1,0:T(8,128)S(1)}, f32[2,128,256]{2,1,0:T(8,128)S(1)}, u32[]{:S(2)}, u32[]{:S(2)}) collective-permute-start(f32[2,128,256]{2,1,0:T(8,128)S(1)} %collective-permute-done.3.received_ref), channel_id=1, source_target_pairs={{0,1},{1,0},{2,3},{3,2},{4,5},{5,4},{6,7},{7,6},{8,9},{9,8},{10,11... | collective-permute-start | bytes 786440 | tf_op jit(solution)/shard_map/ppermute | solution.py:484
  20.8 1.4 %collective-permute-start.1 = (s32[1]{0:T(128)}, s32[1]{0:T(128)}, u32[]{:S(2)}, u32[]{:S(2)}) collective-permute-start(s32[1]{0:T(128)} %collective-permute-done.received_ref.scan_ref), channel_id=1, source_target_pairs={{0,1},{1,0},{2,3},{3,2},{4,5},{5,4},{6,7},{7,6},{8,9},{9,8},{10,11... | collective-permute-start | bytes 20 | tf_op jit(solution)/shard_map/ppermute | solution.py:484
  21.1 4.1 %copy-start = (bf16[8,256,256]{2,1,0:T(8,128)(2,1)S(1)}, bf16[8,256,256]{2,1,0:T(8,128)(2,1)}, u32[]{:S(2)}) copy-start(bf16[8,256,256]{2,1,0:T(8,128)(2,1)} %constant.2.clone.matrix_ref) | copy-start | bytes 3145732
  30.2 8.1 %collective-permute-start.7 = (f32[264,256]{1,0:T(8,128)S(1)}, f32[264,256]{1,0:T(8,128)S(1)}, u32[]{:S(2)}, u32[]{:S(2)}) collective-permute-start(f32[264,256]{1,0:T(8,128)S(1)} %get-tuple-element.39), channel_id=1, source_target_pairs={{2,0},{0,2},{6,4},{4,6},{10,8},{8,10},{14,12},{12,14},{18,16},{16,... | collective-permute-start | bytes 811016 | tf_op jit(solution)/shard_map/ppermute | solution.py:484
  38.3 5.1 %collective-permute-start.8 = (f32[264,256]{1,0:T(8,128)S(1)}, f32[264,256]{1,0:T(8,128)S(1)}, u32[]{:S(2)}, u32[]{:S(2)}) collective-permute-start(f32[264,256]{1,0:T(8,128)S(1)} %collective-permute-done.7.received_ref), channel_id=1, source_target_pairs={{0,1},{1,0},{2,3},{3,2},{4,5},{5,4},{6,7},{7,6},{8,9},{9,8},{10,11... | collective-permute-start | bytes 811016 | tf_op jit(solution)/shard_map/ppermute | solution.py:484

commit v7 on v6

--- a/solution.py
+++ b/solution.py
@@ -58,15 +58,6 @@
     third = object_ref[:, :, pl.ds(pl.multiple_of(last * LANES, LANES), LANES)]
     lane = lax.broadcasted_iota(jnp.int32, first.shape, 2)
     return jnp.where(lane < shift, third, first), second
-
-
-def stage_kernel(object_ref, table_ref, staged_ref, held_ref, sems):
-    first = pltpu.make_async_copy(object_ref, staged_ref, sems.at[0])
-    second = pltpu.make_async_copy(table_ref, held_ref, sems.at[1])
-    first.start()
-    second.start()
-    first.wait()
-    second.wait()
 
 
 def fetch(pairs, sems, first=0):
@@ -490,17 +481,11 @@
         table = scan_offsets.T
         matrix = jnp.asarray(matrices(frame))
         received_scan = move(slot_scan, up)
+        staged = move(object_tiles, swap)
+        table = move(table, swap)
         other_probe = move(probe_modes, swap)
         received_amplitude = move(amplitudes, onward)
         scalar = pltpu.SMEM((1,), jnp.int32)
-        staged, table = call(
-            stage_kernel,
-            (shape(*object_tiles.shape), shape(*table.shape, dtype=jnp.int32)),
-            [space(pltpu.HBM)] * 2,
-            [space(VMEM)] * 2,
-            [pltpu.SemaphoreType.DMA((2,))],
-            mebibytes=8,
-        )(pltpu.with_memory_space_constraint(object_tiles, pltpu.HBM), pltpu.with_memory_space_constraint(table, pltpu.HBM))
         window = call(
             select_kernel, shape(2, height, frame), [space(SMEM)] * 2 + [space(VMEM)] * 2, space(VMEM)
         )(slot_scan, received_scan, table, staged)

time: 45.1 us -> 45.7 us (1.013)
  waiting for transfers between devices: 7.87 us -> 9.4 us
  Pallas kernels: 16.6 us -> 15.3 us
  starting transfers between devices: 18.7 us -> 19.3 us
    pallas_call x1 -> x0, Pallas kernels: 1.65 us -> none  [step(): call(stage_kernel, (shape(*object_tiles.shape), shape(*table.shape, dtype...]
    ppermute x9 -> x11, waiting for transfers between devices: 7.87 us -> 9.4 us  [move(): return lax.ppermute(value, AXES, pairs)]
    ppermute x9 -> x11, starting transfers between devices: 18.7 us -> 19.3 us  [move(): return lax.ppermute(value, AXES, pairs)]
  transfers between devices with their start and end apart: 9 -> 11, of which waited for: 3 -> 4; matrix products, arithmetic and copies ran while one was open for 0% -> 0% of each run, Pallas kernels for 26% -> 22%
where the time goes in v7:
time: 45.7 us; the launch traced here: 45.5 us
  starting transfers between devices  19.3 us (42%)
  Pallas kernels  15.3 us (33%)
  waiting for transfers between devices  9.4 us (21%)
  between operations  1.44 us (3%)
    ppermute x11, starting transfers between devices, move(): return lax.ppermute(value, AXES, pairs)  19.3 us
    ppermute x11, waiting for transfers between devices, move(): return lax.ppermute(value, AXES, pairs)  9.4 us
    pallas_call x1, Pallas kernels, step(): call(wave_kernel, (shape(2 * height + 8, frame), shape(2, height, frame))...  3.84 us
    pallas_call x1, Pallas kernels, step(): call(base_kernel, (whole, whole, whole, shape(height, breadth), shape(hei...  3.65 us
    pallas_call x1, Pallas kernels, step(): call(prepare_kernel, (whole, shape(2 * modes, 2, frame, frame), shape(2,...  3.15 us
    pallas_call x1, Pallas kernels, step(): call(second_kernel, (whole, whole), [space(VMEM)] * 8 + [space(pl.ANY)] *...  1.25 us
    pallas_call x1, Pallas kernels, step(): call(first_kernel, (whole, whole), [space(VMEM)] * 6 + [space(pl.ANY)] *...  1.13 us
    pallas_call x1, Pallas kernels, step(): call(strip_kernel, (strip, strip), [space(VMEM)] * 4, [space(VMEM)] * 2)  1.08 us
  transfers between devices with their start and end apart: 11, of which 4 were waited for; matrix products, arithmetic and copies ran while one was open for 0% of the time, Pallas kernels for 22%

profile of v7, /device:TPU:9, one launch (start us, length us, event | category | flops | bytes accessed | tf_op | source)
XLA Modules:
  0.0 45.5 jit_solution(9416722381532605)
XLA Ops:
  0.6 0.0 copy-start.1
  0.7 0.7 %collective-permute-start.3 = (f32[2,128,2048]{2,1,0:T(8,128)}, f32[2,128,2048]{2,1,0:T(8,128)S(1)}, u32[]{:S(2)}, u32[]{:S(2)}) collective-permute-start(f32[2,128,2048]{2,1,0:T(8,128)} %param.7), channel_id=1, source_target_pairs={{0,1},{1,0},{2,3},{3,2},{4,5},{5,4},{6,7},{7,6},{8,9},{9,8},{10,11... | collective-permute-start | bytes 6291464 | tf_op jit(solution)/shard_map/ppermute | solution.py:475
  1.4 0.1 collective-permute-start.4
  1.5 0.4 collective-permute-start.2
  1.9 0.7 %collective-permute-start.7 = (f32[1,256,256]{2,1,0:T(8,128)}, f32[1,256,256]{2,1,0:T(8,128)S(1)}, u32[]{:S(2)}, u32[]{:S(2)}) collective-permute-start(f32[1,256,256]{2,1,0:T(8,128)} %own_ref.1), channel_id=1, source_target_pairs={{2,6},{6,10},{10,14},{14,18},{18,22},{22,26},{26,30}} | collective-permute-start | bytes 786440 | tf_op jit(solution)/shard_map/ppermute | solution.py:475
  2.6 3.1 %collective-permute-start = (s32[1]{0:T(128)}, s32[1]{0:T(128)}, u32[]{:S(2)}, u32[]{:S(2)}) collective-permute-start(s32[1]{0:T(128)} %param.11), channel_id=1, source_target_pairs={{0,2},{2,4},{4,6},{6,8},{8,10},{10,12},{12,14},{14,16},{16,18},{18... | collective-permute-start | bytes 20 | tf_op jit(solution)/shard_map/ppermute | solution.py:475
  6.4 1.6 %collective-permute-done.received_ref.scan_ref = s32[1]{0:T(128)} collective-permute-done((s32[1]{0:T(128)}, s32[1]{0:T(128)}, u32[]{:S(2)}, u32[]{:S(2)}) %collective-permute-start) | collective-permute-done | bytes 36 | tf_op jit(solution)/shard_map/ppermute | solution.py:475
  8.0 0.0 collective-permute-done.2.table_ref
  8.0 0.0 collective-permute-done.3.object_ref
  8.0 0.9 %shard_map.78 = f32[2,128,256]{2,1,0:T(8,128)S(1)} custom-call(s32[1]{0:T(128)S(6)} %copy.18.scan_ref.own_scan_ref, s32[1]{0:T(128)} %collective-permute-done.received_ref.scan_ref, s32[2,8192]{1,0:T(2,128)S(1)} %collective-permute-done.2.table_ref, f32[2,128,2048]{2,1,0:T(8,128)S(1)} %collective-permute-done.3.object_ref), custom_call_target="tpu_custom_call" | custom-call | flops 5000000 | bytes 5000000 | tf_op jit(solution)/shard_map/pallas_call | solution.py:489
  8.9 2.1 %collective-permute-start.5 = (f32[2,128,256]{2,1,0:T(8,128)S(1)}, f32[2,128,256]{2,1,0:T(8,128)S(1)}, u32[]{:S(2)}, u32[]{:S(2)}) collective-permute-start(f32[2,128,256]{2,1,0:T(8,128)S(1)} %shard_map.78), channel_id=1, source_target_pairs={{0,2},{2,0},{4,6},{6,4},{8,10},{10,8},{12,14},{14,12},{16,18},{18,... | collective-permute-start | bytes 786440 | tf_op jit(solution)/shard_map/ppermute | solution.py:475
  11.1 0.0 collective-permute-done.7.received_ref
  11.1 4.3 %collective-permute-start.8 = (f32[1,256,256]{2,1,0:T(8,128)S(1)}, f32[1,256,256]{2,1,0:T(8,128)S(1)}, u32[]{:S(2)}, u32[]{:S(2)}) collective-permute-start(f32[1,256,256]{2,1,0:T(8,128)S(1)} %collective-permute-done.7.received_ref), channel_id=1, source_target_pairs={{0,1},{1,0},{2,3},{3,2},{4,5},{5,4},{6,7},{7,6},{8,9},{9,8},{10,11... | collective-permute-start | bytes 786440 | tf_op jit(solution)/shard_map/ppermute | solution.py:475
  15.3 0.7 %collective-permute-done.5.received_ref = f32[2,128,256]{2,1,0:T(8,128)S(1)} collective-permute-done((f32[2,128,256]{2,1,0:T(8,128)S(1)}, f32[2,128,256]{2,1,0:T(8,128)S(1)}, u32[]{:S(2)}, u32[]{:S(2)}) %collective-permute-start.5) | collective-permute-done | bytes 262176 | tf_op jit(solution)/shard_map/ppermute | solution.py:475
  16.1 5.4 %collective-permute-start.6 = (f32[2,128,256]{2,1,0:T(8,128)S(1)}, f32[2,128,256]{2,1,0:T(8,128)S(1)}, u32[]{:S(2)}, u32[]{:S(2)}) collective-permute-start(f32[2,128,256]{2,1,0:T(8,128)S(1)} %collective-permute-done.5.received_ref), channel_id=1, source_target_pairs={{0,1},{1,0},{2,3},{3,2},{4,5},{5,4},{6,7},{7,6},{8,9},{9,8},{10,11... | collective-permute-start | bytes 786440 | tf_op jit(solution)/shard_map/ppermute | solution.py:475
  21.4 0.0 collective-permute-start.1
  21.4 0.0 collective-permute-done.8.swapped_ref
  21.4 0.3 shard_map.80.amplitude_ref
  21.7 0.0 copy-start
  21.7 0.9 %collective-permute-done.1.swapped_ref = s32[1]{0:T(128)} collective-permute-done((s32[1]{0:T(128)}, s32[1]{0:T(128)}, u32[]{:S(2)}, u32[]{:S(2)}) %collective-permute-start.1) | collective-permute-done | bytes 36 | tf_op jit(solution)/shard_map/ppermute | solution.py:475
  22.6 0.0 collective-permute-done.4.other_probe_ref
  22.6 3.1 %shard_map.77 = (f32[2,128,2048]{2,1,0:T(8,128)}, f32[4,2,256,256]{3,2,1,0:T(8,128)S(1)}, f32[2,128,256]{2,1,0:T(8,128)S(1)}, f32[256,256]{1,0:T(8,128)S(1)}, f3...) custom-call(s32[1]{0:T(128)S(6)} %copy.18.scan_ref.own_scan_ref, s32[1]{0:T(128)} %collective-permute-done.received_ref.scan_ref, ...), custom_call_target="tpu_custom_call" | custom-call | flops 5000000 | bytes 5000000 | tf_op jit(solution)/shard_map/pallas_call | solution.py:498
  25.8 1.1 %shard_map.79 = (f32[4,2,128,256]{3,2,1,0:T(8,128)S(1)}, f32[4,2,128,256]{3,2,1,0:T(8,128)S(1)}) custom-call(f32[2,128,256]{2,1,0:T(8,128)S(1)} %get-tuple-element.22.own_ref.window_ref, f32[2,128,256]{2,1,0:T(8,128)S(1)} %collective-permute-done.5.received_ref, f32[4,2,256,256]{3,2,1,0:T(8,128)S(1)} %get-tuple-element.23.probe_ref, ...), custom_call_target="tpu_custom_call" | custom-call | flops 5000000 | bytes 5000000 | tf_op jit(solution)/shard_map/pallas_call | solution.py:527
  26.9 0.0 collective-permute-done.6.swapped_ref
  26.9 3.8 %shard_map.81 = (f32[264,256]{1,0:T(8,128)S(1)}, f32[2,128,256]{2,1,0:T(8,128)S(1)}) custom-call(f32[8,128]{1,0:T(8,128)S(1)} %get-tuple-element.21.place_ref, f32[2,128,256]{2,1,0:T(8,128)S(1)} %get-tuple-element.22.own_ref.window_ref, f32[2,128,256]{2,1,0:T(8,128)S(1)} %collective-permute-done.5.received_ref, ...), custom_call_target="tpu_custom_call" | custom-call | flops 5000000 | bytes 5000000 | tf_op jit(solution)/shard_map/pallas_call | solution.py:530
  30.7 1.9 %collective-permute-start.9 = (f32[264,256]{1,0:T(8,128)S(1)}, f32[264,256]{1,0:T(8,128)S(1)}, u32[]{:S(2)}, u32[]{:S(2)}) collective-permute-start(f32[264,256]{1,0:T(8,128)S(1)} %get-tuple-element.35), channel_id=1, source_target_pairs={{2,0},{0,2},{6,4},{4,6},{10,8},{8,10},{14,12},{12,14},{18,16},{16,... | collective-permute-start | bytes 811016 | tf_op jit(solution)/shard_map/ppermute | solution.py:475
  32.7 6.2 %collective-permute-done.9.received_ref = f32[264,256]{1,0:T(8,128)S(1)} collective-permute-done((f32[264,256]{1,0:T(8,128)S(1)}, f32[264,256]{1,0:T(8,128)S(1)}, u32[]{:S(2)}, u32[]{:S(2)}) %collective-permute-start.9) | collective-permute-done | bytes 270368 | tf_op jit(solution)/shard_map/ppermute | solution.py:475
  38.8 0.6 %collective-permute-start.10 = (f32[264,256]{1,0:T(8,128)S(1)}, f32[264,256]{1,0:T(8,128)S(1)}, u32[]{:S(2)}, u32[]{:S(2)}) collective-permute-start(f32[264,256]{1,0:T(8,128)S(1)} %collective-permute-done.9.received_ref), channel_id=1, source_target_pairs={{0,1},{1,0},{2,3},{3,2},{4,5},{5,4},{6,7},{7,6},{8,9},{9,8},{10,11... | collective-permute-start | bytes 811016 | tf_op jit(solution)/shard_map/ppermute | solution.py:475
  39.4 3.6 %shard_map.82 = (f32[2,128,2048]{2,1,0:T(8,128)}, f32[2,128,2048]{2,1,0:T(8,128)}, f32[2,128,2048]{2,1,0:T(8,128)S(1)}, f32[128,2048]{1,0:T(8,128)S(1)}, f32[128...) custom-call(f32[8,128]{1,0:T(8,128)S(1)} %get-tuple-element.21.place_ref, ...), custom_call_target="tpu_custom_call", output_to_operand_aliasing={{1}: (9, {})} | custom-call | flops 5000000 | bytes 5000000 | tf_op jit(solution)/shard_map/pallas_call | solution.py:545
  43.1 1.1 %shard_map.83 = (f32[2,128,2048]{2,1,0:T(8,128)}, f32[2,128,2048]{2,1,0:T(8,128)}) custom-call(f32[8,128]{1,0:T(8,128)S(1)} %get-tuple-element.30.others_ref, f32[2,128,2048]{2,1,0:T(8,128)S(1)} %collective-permute-done.3.object_ref, f32[2,128,2048]{2,1,0:T(8,128)S(1)} %get-tuple-element.31.total_ref, ...), custom_call_target="tpu_custom_call", output_to_operand_aliasing={{0}: (6, {}), {1}: (7, {})} | custom-call | flops 5000000 | bytes 5000000 | tf_op jit(solution)/shard_map/pallas_call | solution.py:571
  44.2 0.0 collective-permute-done.10.swapped_ref
  44.2 1.2 %shard_map.84 = (f32[2,128,2048]{2,1,0:T(8,128)}, f32[2,128,2048]{2,1,0:T(8,128)}) custom-call(f32[8,128]{1,0:T(8,128)S(1)} %get-tuple-element.30.others_ref, f32[2,128,2048]{2,1,0:T(8,128)S(1)} %collective-permute-done.3.object_ref, f32[2,128,2048]{2,1,0:T(8,128)S(1)} %get-tuple-element.31.total_ref, ...), custom_call_target="tpu_custom_call", output_to_operand_aliasing={{0}: (8, {}), {1}: (9, {})} | custom-call | flops 5000000 | bytes 5000000 | tf_op jit(solution)/shard_map/pallas_call | solution.py:579
  (4 shorter events, 0.0 us)
Async XLA Ops:
  0.6 22.0 %copy-start.1 = (f32[2,2,256,256]{3,2,1,0:T(8,128)S(1)}, f32[2,2,256,256]{3,2,1,0:T(8,128)}, u32[]{:S(2)}) copy-start(f32[2,2,256,256]{3,2,1,0:T(8,128)} %own_probe_ref.1) | copy-start | bytes 3145732
  0.6 20.8 %copy-start.2 = (f32[1,256,256]{2,1,0:T(8,128)S(1)}, f32[1,256,256]{2,1,0:T(8,128)}, u32[]{:S(2)}) copy-start(f32[1,256,256]{2,1,0:T(8,128)} %own_ref.1) | copy-start | bytes 786436
  0.7 7.4 %collective-permute-start.3 = (f32[2,128,2048]{2,1,0:T(8,128)}, f32[2,128,2048]{2,1,0:T(8,128)S(1)}, u32[]{:S(2)}, u32[]{:S(2)}) collective-permute-start(f32[2,128,2048]{2,1,0:T(8,128)} %param.7), channel_id=1, source_target_pairs={{0,1},{1,0},{2,3},{3,2},{4,5},{5,4},{6,7},{7,6},{8,9},{9,8},{10,11... | collective-permute-start | bytes 6291464 | tf_op jit(solution)/shard_map/ppermute | solution.py:475
  1.4 21.2 %collective-permute-start.4 = (f32[2,2,256,256]{3,2,1,0:T(8,128)}, f32[2,2,256,256]{3,2,1,0:T(8,128)S(1)}, u32[]{:S(2)}, u32[]{:S(2)}) collective-permute-start(f32[2,2,256,256]{3,2,1,0:T(8,128)} %own_probe_ref.1), channel_id=1, source_target_pairs={{0,1},{1,0},{2,3},{3,2},{4,5},{5,4},{6,7},{7,6},{8,9},{9,8},{10,11... | collective-permute-start | bytes 3145736 | tf_op jit(solution)/shard_map/ppermute | solution.py:475
  1.5 6.6 %collective-permute-start.2 = (s32[2,8192]{1,0:T(2,128)}, s32[2,8192]{1,0:T(2,128)S(1)}, u32[]{:S(2)}, u32[]{:S(2)}) collective-permute-start(s32[2,8192]{1,0:T(2,128)} %bitcast.1), channel_id=1, source_target_pairs={{0,1},{1,0},{2,3},{3,2},{4,5},{5,4},{6,7},{7,6},{8,9},{9,8},{10,11... | collective-permute-start | bytes 196616 | tf_op jit(solution)/shard_map/ppermute | solution.py:475
  1.9 9.2 %collective-permute-start.7 = (f32[1,256,256]{2,1,0:T(8,128)}, f32[1,256,256]{2,1,0:T(8,128)S(1)}, u32[]{:S(2)}, u32[]{:S(2)}) collective-permute-start(f32[1,256,256]{2,1,0:T(8,128)} %own_ref.1), channel_id=1, source_target_pairs={{2,6},{6,10},{10,14},{14,18},{18,22},{22,26},{26,30}} | collective-permute-start | bytes 786440 | tf_op jit(solution)/shard_map/ppermute | solution.py:475
  2.6 5.5 %collective-permute-start = (s32[1]{0:T(128)}, s32[1]{0:T(128)}, u32[]{:S(2)}, u32[]{:S(2)}) collective-permute-start(s32[1]{0:T(128)} %param.11), channel_id=1, source_target_pairs={{0,2},{2,4},{4,6},{6,8},{8,10},{10,12},{12,14},{14,16},{16,18},{18... | collective-permute-start | bytes 20 | tf_op jit(solution)/shard_map/ppermute | solution.py:475
  8.9 7.1 %collective-permute-start.5 = (f32[2,128,256]{2,1,0:T(8,128)S(1)}, f32[2,128,256]{2,1,0:T(8,128)S(1)}, u32[]{:S(2)}, u32[]{:S(2)}) collective-permute-start(f32[2,128,256]{2,1,0:T(8,128)S(1)} %shard_map.78), channel_id=1, source_target_pairs={{0,2},{2,0},{4,6},{6,4},{8,10},{10,8},{12,14},{14,12},{16,18},{18,... | collective-permute-start | bytes 786440 | tf_op jit(solution)/shard_map/ppermute | solution.py:475
  11.1 10.3 %collective-permute-start.8 = (f32[1,256,256]{2,1,0:T(8,128)S(1)}, f32[1,256,256]{2,1,0:T(8,128)S(1)}, u32[]{:S(2)}, u32[]{:S(2)}) collective-permute-start(f32[1,256,256]{2,1,0:T(8,128)S(1)} %collective-permute-done.7.received_ref), channel_id=1, source_target_pairs={{0,1},{1,0},{2,3},{3,2},{4,5},{5,4},{6,7},{7,6},{8,9},{9,8},{10,11... | collective-permute-start | bytes 786440 | tf_op jit(solution)/shard_map/ppermute | solution.py:475
  16.1 10.8 %collective-permute-start.6 = (f32[2,128,256]{2,1,0:T(8,128)S(1)}, f32[2,128,256]{2,1,0:T(8,128)S(1)}, u32[]{:S(2)}, u32[]{:S(2)}) collective-permute-start(f32[2,128,256]{2,1,0:T(8,128)S(1)} %collective-permute-done.5.received_ref), channel_id=1, source_target_pairs={{0,1},{1,0},{2,3},{3,2},{4,5},{5,4},{6,7},{7,6},{8,9},{9,8},{10,11... | collective-permute-start | bytes 786440 | tf_op jit(solution)/shard_map/ppermute | solution.py:475
  21.4 1.2 %collective-permute-start.1 = (s32[1]{0:T(128)}, s32[1]{0:T(128)}, u32[]{:S(2)}, u32[]{:S(2)}) collective-permute-start(s32[1]{0:T(128)} %collective-permute-done.received_ref.scan_ref), channel_id=1, source_target_pairs={{0,1},{1,0},{2,3},{3,2},{4,5},{5,4},{6,7},{7,6},{8,9},{9,8},{10,11... | collective-permute-start | bytes 20 | tf_op jit(solution)/shard_map/ppermute | solution.py:475
  21.7 4.0 %copy-start = (bf16[8,256,256]{2,1,0:T(8,128)(2,1)S(1)}, bf16[8,256,256]{2,1,0:T(8,128)(2,1)}, u32[]{:S(2)}) copy-start(bf16[8,256,256]{2,1,0:T(8,128)(2,1)} %constant.2.clone.matrix_ref) | copy-start | bytes 3145732
  30.7 8.1 %collective-permute-start.9 = (f32[264,256]{1,0:T(8,128)S(1)}, f32[264,256]{1,0:T(8,128)S(1)}, u32[]{:S(2)}, u32[]{:S(2)}) collective-permute-start(f32[264,256]{1,0:T(8,128)S(1)} %get-tuple-element.35), channel_id=1, source_target_pairs={{2,0},{0,2},{6,4},{4,6},{10,8},{8,10},{14,12},{12,14},{18,16},{16,... | collective-permute-start | bytes 811016 | tf_op jit(solution)/shard_map/ppermute | solution.py:475
  38.8 5.4 %collective-permute-start.10 = (f32[264,256]{1,0:T(8,128)S(1)}, f32[264,256]{1,0:T(8,128)S(1)}, u32[]{:S(2)}, u32[]{:S(2)}) collective-permute-start(f32[264,256]{1,0:T(8,128)S(1)} %collective-permute-done.9.received_ref), channel_id=1, source_target_pairs={{0,1},{1,0},{2,3},{3,2},{4,5},{5,4},{6,7},{7,6},{8,9},{9,8},{10,11... | collective-permute-start | bytes 811016 | tf_op jit(solution)/shard_map/ppermute | solution.py:475

commit v8 on v7

--- a/solution.py
+++ b/solution.py
@@ -135,27 +135,33 @@
         factor_ref[half:, at] = rows_ref[index, pl.ds(1, half, stride=2), :]
 
 
-def prepare_kernel(
-    scan_ref, received_ref, swapped_ref, table_ref, object_ref, own_probe_ref, other_probe_ref,
-    gradient_ref, probe_ref, window_ref, light_ref, total_ref, place_ref,
-    zero_ref, tall_ref, own_ref, got_ref, other_ref, sems,
-):
-    pairs = [(scan_ref, own_ref), (received_ref, got_ref), (swapped_ref, other_ref)]
-    scalars = fetch(pairs, sems)
+def probe_parts(own_probe_ref, other_probe_ref):
+    modes = own_probe_ref.shape[0]
+    return [ref.at[mode, part] for ref in (own_probe_ref, other_probe_ref) for mode in range(modes) for part in range(2)]
+
+
+def fill_kernel(own_probe_ref, other_probe_ref, gradient_ref, total_ref, zero_ref, sems):
     zero_ref[...] = jnp.zeros_like(zero_ref)
     step = zero_ref.shape[0]
     copies = []
     for part in range(2):
-        for at in range(0, object_ref.shape[1], step):
-            copies += fetch([(zero_ref, gradient_ref.at[part, at : at + step])], sems, len(pairs) + len(copies))
-    modes = own_probe_ref.shape[0]
-    sources = [ref.at[mode, part] for ref in (own_probe_ref, other_probe_ref) for mode in range(modes) for part in range(2)]
-    total = sources[0][...] * sources[0][...]
-    for source in sources[1:]:
+        for at in range(0, gradient_ref.shape[1], step):
+            copies += fetch([(zero_ref, gradient_ref.at[part, at : at + step])], sems, len(copies))
+    total = jnp.zeros(total_ref.shape, jnp.float32)
+    for source in probe_parts(own_probe_ref, other_probe_ref):
         total = total + source[...] * source[...]
     total_ref[...] = total
-    for copy in scalars:
+    for copy in copies:
         copy.wait()
+
+
+def prepare_kernel(
+    scan_ref, received_ref, swapped_ref, table_ref, object_ref, own_probe_ref, other_probe_ref, total_ref,
+    probe_ref, window_ref, light_ref, place_ref, tall_ref, own_ref, got_ref, other_ref, sems,
+):
+    for copy in fetch([(scan_ref, own_ref), (received_ref, got_ref), (swapped_ref, other_ref)], sems):
+        copy.wait()
+    sources = probe_parts(own_probe_ref, other_probe_ref)
     height = object_ref.shape[1]
     tile = lax.axis_index("tile")
     odd = tile % 2
@@ -163,16 +169,13 @@
     row, col = within(table_ref, scan, tile - 2 * odd, height)
     shift = col % LANES
     for index, source in enumerate(sources):
-        mode, part = divmod(index, 2)
-        roll_into(probe_ref.at[mode, part], source[...], row, shift, tall_ref.at[mode, part])
-    roll_into(light_ref, total_ref[...], row, shift, tall_ref.at[0, 0])
+        roll_into(probe_ref.at[index // 2, index % 2], source[...], row, shift, tall_ref.at[index])
+    roll_into(light_ref, total_ref[...], row, shift, tall_ref.at[len(sources)])
     low, high = strip_window(object_ref, col)
     window_ref[:, :, :LANES] = low
     window_ref[:, :, LANES:] = high
     live = jnp.where(odd == 1, (tile >= 2).astype(jnp.int32), 1)
     keep_scalars(place_ref, (jnp.where(odd == 1, 0, row), jnp.where(odd == 1, row, height), live))
-    for copy in copies:
-        copy.wait()
 
 
 def right(value, high, low):
@@ -495,27 +498,31 @@
         scalar = pltpu.SMEM((1,), jnp.int32)
         strip = shape(2 * modes, 2, height, frame)
         whole = shape(2, height, breadth)
-        gradient, probe, own_window, light, plain, place = call(
+        gradient, plain = call(
+            fill_kernel,
+            (whole, shape(frame, frame)),
+            [space(VMEM)] * 2,
+            [space(pl.ANY), space(VMEM)],
+            [pltpu.VMEM((height // 8, breadth), jnp.float32), pltpu.SemaphoreType.DMA((16,))],
+        )(probe_modes, other_probe)
+        probe, own_window, light, place = call(
             prepare_kernel,
             (
-                whole,
                 shape(2 * modes, 2, frame, frame),
                 shape(2, height, frame),
                 shape(frame, frame),
-                shape(frame, frame),
                 shape(8, LANES),
             ),
-            [space(pl.ANY)] * 3 + [space(VMEM)] * 4,
-            [space(pl.ANY)] + [space(VMEM)] * 5,
+            [space(pl.ANY)] * 3 + [space(VMEM)] * 5,
+            [space(VMEM)] * 4,
             [
-                pltpu.VMEM((height // 8, breadth), jnp.float32),
-                pltpu.VMEM((2 * modes, 2, frame // LANES, frame + height, LANES), jnp.float32),
+                pltpu.VMEM((4 * modes + 1, frame // LANES, frame + height, LANES), jnp.float32),
                 scalar,
                 scalar,
                 scalar,
-                pltpu.SemaphoreType.DMA((19,)),
+                pltpu.SemaphoreType.DMA((3,)),
             ],
-        )(slot_scan, received_scan, swapped_scan, table, staged, probe_modes, other_probe)
+        )(slot_scan, received_scan, swapped_scan, table, staged, probe_modes, other_probe, plain)
         swapped = move(received, swap)
         amplitude = call(
             reorder_kernel,

time: 45.7 us -> 46.2 us (1.011)
  Pallas kernels: 15.3 us -> 16.4 us
  waiting for transfers between devices: 9.4 us -> 8.53 us
    pallas_call x1 -> x2, Pallas kernels: 3.15 us -> 4.39 us  [the longest x1 2.94 us: step(): call(prepare_kernel, (shape(2 * modes, 2, frame, frame), shape(2, height,...]
    ppermute x11, waiting for transfers between devices: 9.4 us -> 8.53 us  [move(): return lax.ppermute(value, AXES, pairs)]
  transfers between devices with their start and end apart: 11 -> 11, of which waited for: 4 -> 3; matrix products, arithmetic and copies ran while one was open for 0% -> 0% of each run, Pallas kernels for 22% -> 25%
where the time goes in v8:
time: 46.2 us; the launch traced here: 45.9 us
  starting transfers between devices  19.5 us (42%)
  Pallas kernels  16.4 us (35%)
  waiting for transfers between devices  8.53 us (18%)
  between operations  1.47 us (3%)
    ppermute x11, starting transfers between devices, move(): return lax.ppermute(value, AXES, pairs)  19.5 us
    ppermute x11, waiting for transfers between devices, move(): return lax.ppermute(value, AXES, pairs)  8.53 us
    pallas_call x1, Pallas kernels, step(): call(wave_kernel, (shape(2 * height + 8, frame), shape(2, height, frame))...  3.83 us
    pallas_call x1, Pallas kernels, step(): call(base_kernel, (whole, whole, whole, shape(height, breadth), shape(hei...  3.52 us
    pallas_call x1, Pallas kernels, step(): call(prepare_kernel, (shape(2 * modes, 2, frame, frame), shape(2, height,...  2.94 us
    pallas_call x1, Pallas kernels, step(): call(fill_kernel, (whole, shape(frame, frame)), [space(VMEM)] * 2, [space...  1.45 us
    pallas_call x1, Pallas kernels, step(): call(second_kernel, (whole, whole), [space(VMEM)] * 8 + [space(pl.ANY)] *...  1.25 us
    pallas_call x1, Pallas kernels, step(): call(first_kernel, (whole, whole), [space(VMEM)] * 6 + [space(pl.ANY)] *...  1.13 us
  transfers between devices with their start and end apart: 11, of which 3 were waited for; matrix products, arithmetic and copies ran while one was open for 0% of the time, Pallas kernels for 25%

profile of v8, /device:TPU:9, one launch (start us, length us, event | category | flops | bytes accessed | tf_op | source)
XLA Modules:
  0.0 45.9 jit_solution(15651803784015477480)
XLA Ops:
  0.7 0.7 %collective-permute-start.3 = (f32[2,128,2048]{2,1,0:T(8,128)}, f32[2,128,2048]{2,1,0:T(8,128)S(1)}, u32[]{:S(2)}, u32[]{:S(2)}) collective-permute-start(f32[2,128,2048]{2,1,0:T(8,128)} %param.7), channel_id=1, source_target_pairs={{0,1},{1,0},{2,3},{3,2},{4,5},{5,4},{6,7},{7,6},{8,9},{9,8},{10,11... | collective-permute-start | bytes 6291464 | tf_op jit(solution)/shard_map/ppermute | solution.py:478
  1.4 0.1 collective-permute-start.4
  1.5 0.4 collective-permute-start.2
  1.9 0.7 %collective-permute-start.7 = (f32[1,256,256]{2,1,0:T(8,128)}, f32[1,256,256]{2,1,0:T(8,128)S(1)}, u32[]{:S(2)}, u32[]{:S(2)}) collective-permute-start(f32[1,256,256]{2,1,0:T(8,128)} %own_ref.1), channel_id=1, source_target_pairs={{2,6},{6,10},{10,14},{14,18},{18,22},{22,26},{26,30}} | collective-permute-start | bytes 786440 | tf_op jit(solution)/shard_map/ppermute | solution.py:478
  2.6 3.1 %collective-permute-start = (s32[1]{0:T(128)}, s32[1]{0:T(128)}, u32[]{:S(2)}, u32[]{:S(2)}) collective-permute-start(s32[1]{0:T(128)} %param.11), channel_id=1, source_target_pairs={{0,2},{2,4},{4,6},{6,8},{8,10},{10,12},{12,14},{14,16},{16,18},{18... | collective-permute-start | bytes 20 | tf_op jit(solution)/shard_map/ppermute | solution.py:478
  6.4 1.6 %collective-permute-done.received_ref.scan_ref = s32[1]{0:T(128)} collective-permute-done((s32[1]{0:T(128)}, s32[1]{0:T(128)}, u32[]{:S(2)}, u32[]{:S(2)}) %collective-permute-start) | collective-permute-done | bytes 36 | tf_op jit(solution)/shard_map/ppermute | solution.py:478
  8.0 0.0 collective-permute-done.2.table_ref
  8.0 0.0 collective-permute-done.3.object_ref
  8.0 0.9 %shard_map.79 = f32[2,128,256]{2,1,0:T(8,128)S(1)} custom-call(s32[1]{0:T(128)S(6)} %copy.18.scan_ref.own_scan_ref, s32[1]{0:T(128)} %collective-permute-done.received_ref.scan_ref, s32[2,8192]{1,0:T(2,128)S(1)} %collective-permute-done.2.table_ref, f32[2,128,2048]{2,1,0:T(8,128)S(1)} %collective-permute-done.3.object_ref), custom_call_target="tpu_custom_call" | custom-call | flops 5000000 | bytes 5000000 | tf_op jit(solution)/shard_map/pallas_call | solution.py:492
  8.9 2.1 %collective-permute-start.5 = (f32[2,128,256]{2,1,0:T(8,128)S(1)}, f32[2,128,256]{2,1,0:T(8,128)S(1)}, u32[]{:S(2)}, u32[]{:S(2)}) collective-permute-start(f32[2,128,256]{2,1,0:T(8,128)S(1)} %shard_map.79), channel_id=1, source_target_pairs={{0,2},{2,0},{4,6},{6,4},{8,10},{10,8},{12,14},{14,12},{16,18},{18,... | collective-permute-start | bytes 786440 | tf_op jit(solution)/shard_map/ppermute | solution.py:478
  11.1 0.0 collective-permute-done.7.received_ref
  11.1 4.3 %collective-permute-start.8 = (f32[1,256,256]{2,1,0:T(8,128)S(1)}, f32[1,256,256]{2,1,0:T(8,128)S(1)}, u32[]{:S(2)}, u32[]{:S(2)}) collective-permute-start(f32[1,256,256]{2,1,0:T(8,128)S(1)} %collective-permute-done.7.received_ref), channel_id=1, source_target_pairs={{0,1},{1,0},{2,3},{3,2},{4,5},{5,4},{6,7},{7,6},{8,9},{9,8},{10,11... | collective-permute-start | bytes 786440 | tf_op jit(solution)/shard_map/ppermute | solution.py:478
  15.3 0.7 %collective-permute-done.5.received_ref = f32[2,128,256]{2,1,0:T(8,128)S(1)} collective-permute-done((f32[2,128,256]{2,1,0:T(8,128)S(1)}, f32[2,128,256]{2,1,0:T(8,128)S(1)}, u32[]{:S(2)}, u32[]{:S(2)}) %collective-permute-start.5) | collective-permute-done | bytes 262176 | tf_op jit(solution)/shard_map/ppermute | solution.py:478
  16.1 5.4 %collective-permute-start.6 = (f32[2,128,256]{2,1,0:T(8,128)S(1)}, f32[2,128,256]{2,1,0:T(8,128)S(1)}, u32[]{:S(2)}, u32[]{:S(2)}) collective-permute-start(f32[2,128,256]{2,1,0:T(8,128)S(1)} %collective-permute-done.5.received_ref), channel_id=1, source_target_pairs={{0,1},{1,0},{2,3},{3,2},{4,5},{5,4},{6,7},{7,6},{8,9},{9,8},{10,11... | collective-permute-start | bytes 786440 | tf_op jit(solution)/shard_map/ppermute | solution.py:478
  21.4 0.0 collective-permute-start.1
  21.4 0.0 collective-permute-done.8.swapped_ref
  21.4 0.3 shard_map.81.amplitude_ref
  21.7 0.0 collective-permute-done.4.other_probe_ref
  21.7 1.4 %shard_map.77 = (f32[2,128,2048]{2,1,0:T(8,128)}, f32[256,256]{1,0:T(8,128)S(1)}) custom-call(f32[2,2,256,256]{3,2,1,0:T(8,128)S(1)} %copy-done.1, f32[2,2,256,256]{3,2,1,0:T(8,128)S(1)} %collective-permute-done.4.other_probe_ref), custom_call_target="tpu_custom_call" | custom-call | flops 5000000 | bytes 5000000 | tf_op jit(solution)/shard_map/pallas_call | solution.py:501
  23.2 0.0 collective-permute-done.1.swapped_ref
  23.2 0.0 copy-start
  23.2 2.9 %shard_map.78 = (f32[4,2,256,256]{3,2,1,0:T(8,128)S(1)}, f32[2,128,256]{2,1,0:T(8,128)S(1)}, f32[256,256]{1,0:T(8,128)S(1)}, f32[8,128]{1,0:T(8,128)S(1)}) custom-call(s32[1]{0:T(128)S(6)} %copy.18.scan_ref.own_scan_ref, s32[1]{0:T(128)} %collective-permute-done.received_ref.scan_ref, s32[1]{0:T(128)} %collective-permute-done.1.swapped_ref, ...), custom_call_target="tpu_custom_call" | custom-call | flops 5000000 | bytes 5000000 | tf_op jit(solution)/shard_map/pallas_call | solution.py:508
  26.2 1.1 %shard_map.80 = (f32[4,2,128,256]{3,2,1,0:T(8,128)S(1)}, f32[4,2,128,256]{3,2,1,0:T(8,128)S(1)}) custom-call(f32[2,128,256]{2,1,0:T(8,128)S(1)} %get-tuple-element.23.own_ref.window_ref, f32[2,128,256]{2,1,0:T(8,128)S(1)} %collective-permute-done.5.received_ref, f32[4,2,256,256]{3,2,1,0:T(8,128)S(1)} %get-tuple-element.24.probe_ref, ...), custom_call_target="tpu_custom_call" | custom-call | flops 5000000 | bytes 5000000 | tf_op jit(solution)/shard_map/pallas_call | solution.py:534
  27.3 0.0 collective-permute-done.6.swapped_ref
  27.3 3.8 %shard_map.82 = (f32[264,256]{1,0:T(8,128)S(1)}, f32[2,128,256]{2,1,0:T(8,128)S(1)}) custom-call(f32[8,128]{1,0:T(8,128)S(1)} %get-tuple-element.22.place_ref, f32[2,128,256]{2,1,0:T(8,128)S(1)} %get-tuple-element.23.own_ref.window_ref, f32[2,128,256]{2,1,0:T(8,128)S(1)} %collective-permute-done.5.received_ref, ...), custom_call_target="tpu_custom_call" | custom-call | flops 5000000 | bytes 5000000 | tf_op jit(solution)/shard_map/pallas_call | solution.py:537
  31.1 1.9 %collective-permute-start.9 = (f32[264,256]{1,0:T(8,128)S(1)}, f32[264,256]{1,0:T(8,128)S(1)}, u32[]{:S(2)}, u32[]{:S(2)}) collective-permute-start(f32[264,256]{1,0:T(8,128)S(1)} %get-tuple-element.35), channel_id=1, source_target_pairs={{2,0},{0,2},{6,4},{4,6},{10,8},{8,10},{14,12},{12,14},{18,16},{16,... | collective-permute-start | bytes 811016 | tf_op jit(solution)/shard_map/ppermute | solution.py:478
  33.0 6.2 %collective-permute-done.9.received_ref = f32[264,256]{1,0:T(8,128)S(1)} collective-permute-done((f32[264,256]{1,0:T(8,128)S(1)}, f32[264,256]{1,0:T(8,128)S(1)}, u32[]{:S(2)}, u32[]{:S(2)}) %collective-permute-start.9) | collective-permute-done | bytes 270368 | tf_op jit(solution)/shard_map/ppermute | solution.py:478
  39.2 0.8 %collective-permute-start.10 = (f32[264,256]{1,0:T(8,128)S(1)}, f32[264,256]{1,0:T(8,128)S(1)}, u32[]{:S(2)}, u32[]{:S(2)}) collective-permute-start(f32[264,256]{1,0:T(8,128)S(1)} %collective-permute-done.9.received_ref), channel_id=1, source_target_pairs={{0,1},{1,0},{2,3},{3,2},{4,5},{5,4},{6,7},{7,6},{8,9},{9,8},{10,11... | collective-permute-start | bytes 811016 | tf_op jit(solution)/shard_map/ppermute | solution.py:478
  40.0 3.5 %shard_map.83 = (f32[2,128,2048]{2,1,0:T(8,128)}, f32[2,128,2048]{2,1,0:T(8,128)}, f32[2,128,2048]{2,1,0:T(8,128)S(1)}, f32[128,2048]{1,0:T(8,128)S(1)}, f32[128...) custom-call(f32[8,128]{1,0:T(8,128)S(1)} %get-tuple-element.22.place_ref, ...), custom_call_target="tpu_custom_call", output_to_operand_aliasing={{1}: (9, {})} | custom-call | flops 5000000 | bytes 5000000 | tf_op jit(solution)/shard_map/pallas_call | solution.py:552
  43.5 1.1 %shard_map.84 = (f32[2,128,2048]{2,1,0:T(8,128)}, f32[2,128,2048]{2,1,0:T(8,128)}) custom-call(f32[8,128]{1,0:T(8,128)S(1)} %get-tuple-element.30.others_ref, f32[2,128,2048]{2,1,0:T(8,128)S(1)} %collective-permute-done.3.object_ref, f32[2,128,2048]{2,1,0:T(8,128)S(1)} %get-tuple-element.31.total_ref, ...), custom_call_target="tpu_custom_call", output_to_operand_aliasing={{0}: (6, {}), {1}: (7, {})} | custom-call | flops 5000000 | bytes 5000000 | tf_op jit(solution)/shard_map/pallas_call | solution.py:578
  44.7 0.0 collective-permute-done.10.swapped_ref
  44.7 1.2 %shard_map.85 = (f32[2,128,2048]{2,1,0:T(8,128)}, f32[2,128,2048]{2,1,0:T(8,128)}) custom-call(f32[8,128]{1,0:T(8,128)S(1)} %get-tuple-element.30.others_ref, f32[2,128,2048]{2,1,0:T(8,128)S(1)} %collective-permute-done.3.object_ref, f32[2,128,2048]{2,1,0:T(8,128)S(1)} %get-tuple-element.31.total_ref, ...), custom_call_target="tpu_custom_call", output_to_operand_aliasing={{0}: (8, {}), {1}: (9, {})} | custom-call | flops 5000000 | bytes 5000000 | tf_op jit(solution)/shard_map/pallas_call | solution.py:586
  (5 shorter events, 0.0 us)
Async XLA Ops:
  0.6 21.1 %copy-start.1 = (f32[2,2,256,256]{3,2,1,0:T(8,128)S(1)}, f32[2,2,256,256]{3,2,1,0:T(8,128)}, u32[]{:S(2)}) copy-start(f32[2,2,256,256]{3,2,1,0:T(8,128)} %own_probe_ref.3) | copy-start | bytes 3145732
  0.6 20.8 %copy-start.2 = (f32[1,256,256]{2,1,0:T(8,128)S(1)}, f32[1,256,256]{2,1,0:T(8,128)}, u32[]{:S(2)}) copy-start(f32[1,256,256]{2,1,0:T(8,128)} %own_ref.1) | copy-start | bytes 786436
  0.7 7.4 %collective-permute-start.3 = (f32[2,128,2048]{2,1,0:T(8,128)}, f32[2,128,2048]{2,1,0:T(8,128)S(1)}, u32[]{:S(2)}, u32[]{:S(2)}) collective-permute-start(f32[2,128,2048]{2,1,0:T(8,128)} %param.7), channel_id=1, source_target_pairs={{0,1},{1,0},{2,3},{3,2},{4,5},{5,4},{6,7},{7,6},{8,9},{9,8},{10,11... | collective-permute-start | bytes 6291464 | tf_op jit(solution)/shard_map/ppermute | solution.py:478
  1.4 20.3 %collective-permute-start.4 = (f32[2,2,256,256]{3,2,1,0:T(8,128)}, f32[2,2,256,256]{3,2,1,0:T(8,128)S(1)}, u32[]{:S(2)}, u32[]{:S(2)}) collective-permute-start(f32[2,2,256,256]{3,2,1,0:T(8,128)} %own_probe_ref.3), channel_id=1, source_target_pairs={{0,1},{1,0},{2,3},{3,2},{4,5},{5,4},{6,7},{7,6},{8,9},{9,8},{10,11... | collective-permute-start | bytes 3145736 | tf_op jit(solution)/shard_map/ppermute | solution.py:478
  1.5 6.6 %collective-permute-start.2 = (s32[2,8192]{1,0:T(2,128)}, s32[2,8192]{1,0:T(2,128)S(1)}, u32[]{:S(2)}, u32[]{:S(2)}) collective-permute-start(s32[2,8192]{1,0:T(2,128)} %bitcast.1), channel_id=1, source_target_pairs={{0,1},{1,0},{2,3},{3,2},{4,5},{5,4},{6,7},{7,6},{8,9},{9,8},{10,11... | collective-permute-start | bytes 196616 | tf_op jit(solution)/shard_map/ppermute | solution.py:478
  1.9 9.2 %collective-permute-start.7 = (f32[1,256,256]{2,1,0:T(8,128)}, f32[1,256,256]{2,1,0:T(8,128)S(1)}, u32[]{:S(2)}, u32[]{:S(2)}) collective-permute-start(f32[1,256,256]{2,1,0:T(8,128)} %own_ref.1), channel_id=1, source_target_pairs={{2,6},{6,10},{10,14},{14,18},{18,22},{22,26},{26,30}} | collective-permute-start | bytes 786440 | tf_op jit(solution)/shard_map/ppermute | solution.py:478
  2.6 5.5 %collective-permute-start = (s32[1]{0:T(128)}, s32[1]{0:T(128)}, u32[]{:S(2)}, u32[]{:S(2)}) collective-permute-start(s32[1]{0:T(128)} %param.11), channel_id=1, source_target_pairs={{0,2},{2,4},{4,6},{6,8},{8,10},{10,12},{12,14},{14,16},{16,18},{18... | collective-permute-start | bytes 20 | tf_op jit(solution)/shard_map/ppermute | solution.py:478
  8.9 7.1 %collective-permute-start.5 = (f32[2,128,256]{2,1,0:T(8,128)S(1)}, f32[2,128,256]{2,1,0:T(8,128)S(1)}, u32[]{:S(2)}, u32[]{:S(2)}) collective-permute-start(f32[2,128,256]{2,1,0:T(8,128)S(1)} %shard_map.79), channel_id=1, source_target_pairs={{0,2},{2,0},{4,6},{6,4},{8,10},{10,8},{12,14},{14,12},{16,18},{18,... | collective-permute-start | bytes 786440 | tf_op jit(solution)/shard_map/ppermute | solution.py:478
  11.1 10.3 %collective-permute-start.8 = (f32[1,256,256]{2,1,0:T(8,128)S(1)}, f32[1,256,256]{2,1,0:T(8,128)S(1)}, u32[]{:S(2)}, u32[]{:S(2)}) collective-permute-start(f32[1,256,256]{2,1,0:T(8,128)S(1)} %collective-permute-done.7.received_ref), channel_id=1, source_target_pairs={{0,1},{1,0},{2,3},{3,2},{4,5},{5,4},{6,7},{7,6},{8,9},{9,8},{10,11... | collective-permute-start | bytes 786440 | tf_op jit(solution)/shard_map/ppermute | solution.py:478
  16.1 11.2 %collective-permute-start.6 = (f32[2,128,256]{2,1,0:T(8,128)S(1)}, f32[2,128,256]{2,1,0:T(8,128)S(1)}, u32[]{:S(2)}, u32[]{:S(2)}) collective-permute-start(f32[2,128,256]{2,1,0:T(8,128)S(1)} %collective-permute-done.5.received_ref), channel_id=1, source_target_pairs={{0,1},{1,0},{2,3},{3,2},{4,5},{5,4},{6,7},{7,6},{8,9},{9,8},{10,11... | collective-permute-start | bytes 786440 | tf_op jit(solution)/shard_map/ppermute | solution.py:478
  21.4 1.8 %collective-permute-start.1 = (s32[1]{0:T(128)}, s32[1]{0:T(128)}, u32[]{:S(2)}, u32[]{:S(2)}) collective-permute-start(s32[1]{0:T(128)} %collective-permute-done.received_ref.scan_ref), channel_id=1, source_target_pairs={{0,1},{1,0},{2,3},{3,2},{4,5},{5,4},{6,7},{7,6},{8,9},{9,8},{10,11... | collective-permute-start | bytes 20 | tf_op jit(solution)/shard_map/ppermute | solution.py:478
  23.2 3.0 %copy-start = (bf16[8,256,256]{2,1,0:T(8,128)(2,1)S(1)}, bf16[8,256,256]{2,1,0:T(8,128)(2,1)}, u32[]{:S(2)}) copy-start(bf16[8,256,256]{2,1,0:T(8,128)(2,1)} %constant.2.clone.matrix_ref) | copy-start | bytes 3145732
  31.1 8.1 %collective-permute-start.9 = (f32[264,256]{1,0:T(8,128)S(1)}, f32[264,256]{1,0:T(8,128)S(1)}, u32[]{:S(2)}, u32[]{:S(2)}) collective-permute-start(f32[264,256]{1,0:T(8,128)S(1)} %get-tuple-element.35), channel_id=1, source_target_pairs={{2,0},{0,2},{6,4},{4,6},{10,8},{8,10},{14,12},{12,14},{18,16},{16,... | collective-permute-start | bytes 811016 | tf_op jit(solution)/shard_map/ppermute | solution.py:478
  39.2 5.4 %collective-permute-start.10 = (f32[264,256]{1,0:T(8,128)S(1)}, f32[264,256]{1,0:T(8,128)S(1)}, u32[]{:S(2)}, u32[]{:S(2)}) collective-permute-start(f32[264,256]{1,0:T(8,128)S(1)} %collective-permute-done.9.received_ref), channel_id=1, source_target_pairs={{0,1},{1,0},{2,3},{3,2},{4,5},{5,4},{6,7},{7,6},{8,9},{9,8},{10,11... | collective-permute-start | bytes 811016 | tf_op jit(solution)/shard_map/ppermute | solution.py:478
